TPU v7x, 32 devices: a whole 2x2x4 slice. The times are simulated.
32 devices in a mesh: ctx: 8 (over y, x, core), batch: 4 (over z).
Axes of the slice: x: 2, y: 2, z: 4, core: 2. Of those that a mesh axis runs over, the one named last changes fastest.
Arguments:
- tokens: bfloat16 [4, 2048, 768], P('batch', 'ctx'), may hold values from -6 to 6
- seg_ids: int32 [4, 2048], P('batch', 'ctx'), may hold values from 0 to 7, never falling along the last dimension, each value on 1 to 1024 neighbouring positions
- routes: int32 [8, 4, 256, 1], P('ctx', 'batch'), may hold values from 0 to 3; in each aligned block of 256 rows (0 to 255, 256 to 511, ..., all dimensions but the last counted through in order) at most 128 rows name the same one
- attn_gain: bfloat16 [768], replicated, may hold values from 0.25 to 1.75
- query_key_value_weight: bfloat16 [768, 2304], P(('ctx', 'batch')), may hold values from -0.21875 to 0.21875
- attention_output_weight: bfloat16 [768, 768], P(('ctx', 'batch')), may hold values from -1.5 to 1.5
- bias_table: bfloat16 [32, 12], replicated, may hold values from -4 to 4
- ffn_gain: bfloat16 [768], replicated, may hold values from 0.25 to 1.75
- router_weight: bfloat16 [768, 4], P(('ctx', 'batch')), may hold values from -0.15625 to 0.15625
- expert_in: bfloat16 [4, 768, 3072], P('batch'), may hold values from -0.21875 to 0.21875
- expert_out: bfloat16 [4, 3072, 768], P('batch'), may hold values from -3 to 3
- out_grad: bfloat16 [4, 2048, 768], P('batch', 'ctx'), may hold values from -6 to 6
Outputs:
- layer_out: bfloat16 [4, 2048, 768], P('batch', 'ctx')
- tokens_grad: bfloat16 [4, 2048, 768], P('batch', 'ctx')
- attn_gain_grad: float32 [768], replicated
- qkv_weight_grad: float32 [768, 2304], P(('ctx', 'batch'))
- attn_out_weight_grad: float32 [768, 768], P(('ctx', 'batch'))
- bias_table_grad: float32 [32, 12], replicated
- ffn_gain_grad: float32 [768], replicated
- router_weight_grad: float32 [768, 4], P(('ctx', 'batch'))
- expert_in_grad: float32 [4, 768, 3072], P('batch', 'ctx')
- expert_out_grad: float32 [4, 3072, 768], P('batch', 'ctx')
Inputs may be any that keep to these rules, and one draw needn't show every extreme that they name: In each aligned block of 256 rows of routes, taken in the array's order (the rows of one device), no expert is named by more than 128 rows, and some block names some expert exactly 128 times. `seg_ids`: segment numbers never fall along a sequence; a segment holds at most 1024 tokens, and some segment holds exactly that many.
All inputs are finite; a program needn't handle non-finite values.
Results may differ from a plain program's by a relative error of at most 0.019.
Values may be sent and summed in bfloat16 or wider, within the bound.
No kernel may reach another device: no remote copies, remote signals or barrier semaphores. Data moves between devices by JAX's collectives and lax.ppermute only.
A program may use at most 192 MiB of HBM per device.

v0:
```python
import functools
import math

import jax
import jax.numpy as jnp
import numpy as np
from jax import lax
from jax.experimental import pallas as pl
from jax.experimental.pallas import tpu as pltpu
from jax.sharding import PartitionSpec as P

BUCKETS = 32
MAX_DIST = 128
EPSILON = 1e-06
MASKED = -1e30
F32 = jnp.float32
BF16 = jnp.bfloat16


def bucket_limits():
    half_span = BUCKETS // 2
    exact_span = half_span // 2
    log_levels = half_span - exact_span
    limits = []
    for level_at in range(1, log_levels):
        bound_row = exact_span
        while (
            bound_row**log_levels * exact_span**level_at
            < MAX_DIST**level_at * exact_span**log_levels
        ):
            bound_row = bound_row + 1
        limits.append(bound_row)
    return limits


def relative_bucket(offsets):
    half_span = BUCKETS // 2
    exact_span = half_span // 2
    distance = np.abs(offsets)
    far = np.full(distance.shape, exact_span, np.int32)
    for bound_row in bucket_limits():
        far = far + (distance >= bound_row).astype(np.int32)
    near = np.where(distance < exact_span, distance, far)
    return near + np.where(offsets > 0, half_span, 0)


def band_onehot(block):
    column = np.arange(2 * block)
    rows = []
    for d in range(5):
        if d in (0, 4):
            offsets = np.full((2 * block,), (d - 2) * max(block, MAX_DIST), np.int64)
        else:
            offsets = (d - 2) * block + block - column
        rows.append(relative_bucket(offsets)[None, :] == np.arange(BUCKETS)[:, None])
    return np.stack(rows)


def dot(a, b, dims, precision=None):
    return lax.dot_general(a, b, (dims, ((), ())), preferred_element_type=F32, precision=precision)


NN = ((1,), (0,))
NT = ((1,), (1,))
TN = ((0,), (0,))


def xor_order(parts, index):
    parts = list(parts)
    step = 1
    while step < len(parts):
        odd = (index // step) % 2 == 1
        parts = [jnp.where(odd, parts[i ^ step], parts[i]) for i in range(len(parts))]
        step = step * 2
    return parts


def vmem(count):
    return [pl.BlockSpec(memory_space=pltpu.VMEM)] * count


def smem(count):
    return [pl.BlockSpec(memory_space=pltpu.SMEM)] * count


def kernel_call(kernel, name, scalars, arrays, out_shape, scratch=()):
    return pl.pallas_call(
        kernel,
        out_shape=tuple(jax.ShapeDtypeStruct(shape, kind) for shape, kind in out_shape),
        in_specs=smem(len(scalars)) + vmem(len(arrays)),
        out_specs=vmem(len(out_shape)),
        scratch_shapes=[pltpu.VMEM(shape, kind) for shape, kind in scratch],
        compiler_params=pltpu.CompilerParams(vmem_limit_bytes=56 << 20),
        cost_estimate=pl.CostEstimate(flops=1, transcendentals=1, bytes_accessed=1),
        name=name,
    )(*scalars, *arrays)


def swap(value, axis, size, mask):
    return lax.ppermute(value, axis, [(i, i ^ mask) for i in range(size)])


def column(row, size):
    return jnp.broadcast_to(row, (size, row.shape[1])).T


def first_kernel(info_ref, tokens_ref, seg_ref, gain_ref, row_ref, message_ref, *cut_refs, part):
    tokens = tokens_ref[...].astype(F32)
    per, width = tokens.shape
    scale = lax.rsqrt(jnp.mean(tokens * tokens, axis=1, keepdims=True) + EPSILON)
    message_ref[:per, :] = (tokens * scale * gain_ref[...].astype(F32)).astype(BF16)
    message_ref[per:, :] = jnp.zeros((message_ref.shape[0] - per, width), BF16)
    message_ref[per:, :per] = jnp.broadcast_to(
        seg_ref[...].astype(F32), (message_ref.shape[0] - per, per)
    ).astype(BF16)
    rows = row_ref[...].astype(F32)
    groups = len(cut_refs)
    cuts = [
        jnp.concatenate(
            [rows[:, k * width + g * part : k * width + (g + 1) * part] for k in range(3)], axis=1
        )
        for g in range(groups)
    ]
    for ref, cut in zip(cut_refs, xor_order(cuts, info_ref[0])):
        ref[...] = cut.astype(BF16)


def row_place(info_ref, g, r, z, ring, batch):
    return ((g ^ info_ref[0]) * ring + (r ^ info_ref[1])) * batch + (z ^ info_ref[2])


def assemble(info_ref, piece_refs, dest_ref, groups, batch, tall):
    ring = len(piece_refs)
    for r in range(ring):
        for z in range(batch):
            for g in range(groups):
                place = row_place(info_ref, g, r, z, ring, batch)
                at = (z * groups + g) * tall
                dest_ref[pl.ds(pl.multiple_of(place * tall, 8), tall), :] = piece_refs[r][
                    at : at + tall, :
                ].astype(F32)


def project_kernel(info_ref, *refs, groups, ring, batch, tall, part, per, pieces):
    x_refs, refs = refs[:groups], refs[groups:]
    w_refs, refs = refs[:pieces], refs[pieces:]
    q_ref, kv_ref, w_out, x_out, w_s = refs
    wide = 256
    if tall % 8 == 0:
        assemble(info_ref, w_refs, w_s, groups, batch, tall)
    else:
        w_s[...] = w_refs[0][...].astype(F32)
    gap = jnp.zeros((w_s.shape[0], wide - part), BF16)
    w = jnp.concatenate(
        [x for k in range(3) for x in (w_s[:, k * part : (k + 1) * part].astype(BF16), gap)],
        axis=1,
    )
    w_out[...] = w
    kv_ref[groups * per :, :] = jnp.zeros((kv_ref.shape[0] - groups * per, 2 * wide), BF16)
    seg = jnp.concatenate([x_ref[per : per + 1, :wide].astype(F32) for x_ref in x_refs], axis=0)
    seg = jnp.concatenate(
        [seg, jnp.zeros((kv_ref.shape[0] - groups * per - groups, wide), F32)], axis=0
    )
    kv_ref[groups * per :, :wide] = seg.astype(BF16)
    for m in range(groups):
        x = x_refs[m][:per, :]
        x_out[m * per : (m + 1) * per, :] = x
        packed = dot(x, w_out[...], NN).astype(BF16)
        q_ref[m * per : (m + 1) * per, :] = packed[:, :wide]
        kv_ref[m * per : (m + 1) * per, :] = packed[:, wide:]


def slot_row(route, capacity):
    per = route.shape[1]
    earlier = lax.broadcasted_iota(jnp.int32, (per, per), 0) < lax.broadcasted_iota(
        jnp.int32, (per, per), 1
    )
    same = jnp.where((column(route, per) == route) & earlier, 1.0, 0.0)
    return route * capacity + jnp.sum(same, axis=0, keepdims=True)


def dispatch_kernel(route_ref, dz_ref, pick_ref, pick_t_ref, sent_ref, *, capacity):
    target = slot_row(route_ref[...].astype(F32), capacity).astype(jnp.int32)
    slots, per = pick_ref.shape
    slot = lax.broadcasted_iota(jnp.int32, (slots, per), 0)
    pick = jnp.where(slot == target, 1.0, 0.0)
    pick_ref[...] = pick.astype(BF16)
    pick_t_ref[...] = pick.T.astype(BF16)
    sent_ref[...] = dot(pick.astype(BF16), dz_ref[...], NN).astype(BF16)


def middle_kernel(info_ref, *refs, groups, ring, batch, tall, part, pieces, lanes):
    mixed_refs, refs = refs[:groups], refs[groups:]
    w_refs, refs = refs[:pieces], refs[pieces:]
    tokens_ref, gain_ref, pick_ref, route_ref = refs[:4]
    w_out, router_out, middle_ref, gate_ref, sent_ref, w_s = refs[4:]
    if tall % 8 == 0:
        assemble(info_ref, w_refs, w_s, groups, batch, tall)
    else:
        w_s[...] = w_refs[0][...].astype(F32)
    width = tokens_ref.shape[1]
    w_out[...] = w_s[:, :width].astype(BF16)
    router = w_s[:, width:]
    router_out[...] = router.T.astype(BF16)
    middle = tokens_ref[...].astype(F32)
    for m in range(groups):
        start = pl.multiple_of((info_ref[0] ^ m) * part, 16)
        middle += dot(mixed_refs[m][...], w_out[pl.ds(start, part), :], NN)
    middle_ref[...] = middle
    scale = lax.rsqrt(jnp.mean(middle * middle, axis=1, keepdims=True) + EPSILON)
    normed = (middle * scale * gain_ref[...].astype(F32)).astype(BF16)
    logits = dot(normed, router.astype(BF16), NN)
    lane = lax.broadcasted_iota(jnp.int32, logits.shape, 1)
    logits = jnp.where(lane < batch, logits, MASKED)
    expo = jnp.exp(logits - jnp.max(logits, axis=1, keepdims=True))
    probs = expo / jnp.sum(expo, axis=1, keepdims=True)
    route = column(route_ref[...].astype(F32), lanes).astype(jnp.int32)
    gate_ref[...] = jnp.sum(jnp.where(lane == route, probs, 0.0), axis=1, keepdims=True)
    sent_ref[...] = dot(pick_ref[...], normed, NN).astype(BF16)


def scatter_rows(info_ref, value, g, own_ref, other_refs, ring, batch, tall):
    for r in range(ring):
        for z in range(batch):
            rows = value[(r * batch + z) * tall : (r * batch + z + 1) * tall, :]
            place = z ^ info_ref[2]
            for m in range(ring):

                @pl.when((info_ref[1] ^ m) == r)
                def _():
                    if m == 0:
                        own_ref[place, g] = rows
                    else:
                        other_refs[m - 1][place, g] = rows.astype(BF16)


def branch_kernel(info_ref, back_ref, *refs, groups, ring, batch, tall, part, lanes):
    mixed_refs, refs = refs[:groups], refs[groups:]
    pick_t_ref, middle_ref, dz_ref, gain_ref, w_ref, rpart_ref = refs[:6]
    d_middle_ref, gain_part_ref = refs[6:8]
    d_mixed_refs, grad_refs = refs[8 : 8 + groups], refs[8 + groups :]
    d_normed = dot(pick_t_ref[...], back_ref[...], NN)
    middle = middle_ref[...]
    scale = lax.rsqrt(jnp.mean(middle * middle, axis=1, keepdims=True) + EPSILON)
    gain_part_ref[...] = jnp.sum(d_normed * middle * scale, axis=0, keepdims=True)
    scaled = gain_ref[...].astype(F32) * d_normed
    d_middle = (
        dz_ref[...].astype(F32)
        + scale * scaled
        - middle
        * (scale * scale * scale)
        * jnp.mean(scaled * middle, axis=1, keepdims=True)
    )
    d_middle_ref[...] = d_middle
    d_branch = d_middle.astype(BF16)
    for m in range(groups):
        start = pl.multiple_of((info_ref[0] ^ m) * part, 16)
        d_mixed_refs[m][...] = dot(d_branch, w_ref[pl.ds(start, part), :], NT).astype(BF16)
    for m in range(groups):
        start = pl.multiple_of((info_ref[0] ^ m) * part, 16)
        grad = dot(mixed_refs[m][...], d_branch, TN)
        grad = jnp.concatenate([grad, rpart_ref[pl.ds(start, part), :]], axis=1)
        if tall % 8 == 0:
            scatter_rows(info_ref, grad, m, grad_refs[0], grad_refs[1:], ring, batch, tall)
        else:
            grad_refs[0][pl.ds(start, part), :] = grad


def weight_kernel(info_ref, dq_ref, *refs, groups, ring, batch, tall, part, per):
    got_refs, refs = refs[:ring], refs[ring:]
    x_ref, dp_ref, grad_refs = refs[0], refs[1], refs[2:]
    wide = 256
    for m in range(groups):
        rows = slice(m * per, (m + 1) * per)
        dkv = got_refs[0][rows, :]
        for ref in got_refs[1:]:
            dkv += ref[rows, :].astype(F32)
        dp_ref[rows, :wide] = dq_ref[rows, :]
        dp_ref[rows, wide:] = dkv.astype(BF16)
    share = ring * batch * tall
    for g in range(groups):
        grad = dot(x_ref[:, g * share : (g + 1) * share], dp_ref[...], TN)
        grad = jnp.concatenate([grad[:, k * wide : k * wide + part] for k in range(3)], axis=1)
        if tall % 8 == 0:
            scatter_rows(
                info_ref, grad, g ^ info_ref[0], grad_refs[0], grad_refs[1:], ring, batch, tall
            )
        else:
            grad_refs[0][g * share : (g + 1) * share, :] = grad


def unproject_kernel(dp_ref, x_ref, w_ref, gain_ref, *refs, per):
    d_refs, gain_part_ref = refs[:-1], refs[-1]
    total = jnp.zeros(gain_part_ref.shape, F32)
    for m, ref in enumerate(d_refs):
        rows = slice(m * per, (m + 1) * per)
        d_normed = dot(dp_ref[rows, :], w_ref[...], NT)
        ref[...] = d_normed.astype(ref.dtype)
        total += jnp.sum(d_normed * x_ref[rows, :].astype(F32), axis=0, keepdims=True)
    gain_part_ref[...] = total / gain_ref[...].astype(F32)


def combine_kernel(got_ref, pick_t_ref, middle_ref, gate_ref, out_ref):
    returned = dot(pick_t_ref[...], got_ref[...], NN)
    out_ref[...] = (middle_ref[...] + gate_ref[...] * returned).astype(BF16)


def head_mask(value, half):
    lane = lax.broadcasted_iota(jnp.int32, value.shape, 1)
    return jnp.where((lane // 64) == half, value, jnp.zeros_like(value))


def set_bias(band_ref, bias_s, heads, block):
    for h in range(heads):
        for d in range(5):
            row = jnp.broadcast_to(band_ref[h, d : d + 1, :], (block, 2 * block))
            bias_s[h, d] = pltpu.roll(row, block, 1, stride=1, stride_axis=0)[:, :block]


def key_at(kb, info_ref, ring, groups):
    return ((kb % ring) ^ info_ref[1]) * groups + ((kb // ring) ^ info_ref[0])


def set_keys(info_ref, kv_refs, seg_s, groups, ring, block):
    rows = [ref[groups * block : groups * block + groups, :block].astype(F32) for ref in kv_refs]
    seg = jnp.concatenate(rows, axis=0)
    blocks = groups * ring
    for at in range(blocks):
        seg_s[at * block : (at + 1) * block, :] = column(seg[at : at + 1, :], 128)
    low, high = seg[:, 0:1], seg[:, block - 1 : block]
    place = lax.broadcasted_iota(jnp.int32, (blocks, 1), 0)
    natural = ((place % groups) ^ info_ref[0]) * ring + ((place // groups) ^ info_ref[1])
    natural = natural.astype(F32)
    spans = []
    for i in range(groups):
        meets = (low <= high[i : i + 1, :]) & (high >= low[i : i + 1, :])
        first = jnp.min(jnp.where(meets, natural, float(blocks)))
        last = jnp.max(jnp.where(meets, natural, -1.0))
        spans.append((first.astype(jnp.int32), last.astype(jnp.int32) + 1))
    return seg, spans


def set_mask(mask_s, seg_s, segq, start, block):
    segk = seg_s[pl.ds(start, block), :]
    for cut in range(block // 128):
        lanes = slice(cut * 128, (cut + 1) * 128)
        mask_s[:, lanes] = jnp.where(segk == segq[:, lanes], 0.0, MASKED).astype(F32)


def attend_kernel(info_ref, q_ref, *refs, heads, groups, ring, block):
    kv_refs, refs = refs[:ring], refs[ring:]
    band_ref, ot_ref, lse_ref = refs[:3]
    mixed_refs, refs = refs[3 : 3 + groups], refs[3 + groups :]
    bias_s, key_s, vt_s, seg_s, mask_s, stat_s, acc_s = refs
    wide = 256
    set_bias(band_ref, bias_s, heads, block)
    seg, spans = set_keys(info_ref, kv_refs, seg_s, groups, ring, block)
    for r in range(ring):
        for g in range(groups):
            at, rows = r * groups + g, slice(g * block, (g + 1) * block)
            key_s[at] = kv_refs[r][rows, :wide]
            vt_s[at] = kv_refs[r][rows, wide:].astype(F32).T.astype(BF16)
    for i in range(groups):
        qb = (i ^ info_ref[0]) * ring + info_ref[1]
        rows = slice(i * block, (i + 1) * block)
        segq = seg[i : i + 1, :]
        stat_s[0:heads] = jnp.full((heads, 1, block), MASKED, F32)
        stat_s[heads : 2 * heads] = jnp.zeros((heads, 1, block), F32)
        acc_s[...] = jnp.zeros_like(acc_s)

        @pl.loop(spans[i][0], spans[i][1])
        def _(kb):
            at = key_at(kb, info_ref, ring, groups)
            set_mask(mask_s, seg_s, segq, pl.multiple_of(at * block, block), block)
            d = jnp.clip(kb - qb, -2, 2) + 2
            for h in range(heads):
                lane = (h // 2) * 128
                query = head_mask(q_ref[rows, lane : lane + 128], h % 2) * 0.125
                key = key_s[at, :, lane : lane + 128]
                scores = dot(key, query.astype(BF16), NT) + bias_s[h, d] + mask_s[...]
                top = stat_s[h]
                top_next = jnp.maximum(top, jnp.max(scores, axis=0, keepdims=True))
                expo = jnp.exp(scores - top_next)
                decay = jnp.exp(top - top_next)
                stat_s[h] = top_next
                stat_s[heads + h] = stat_s[heads + h] * decay + jnp.sum(
                    expo, axis=0, keepdims=True
                )
                value_t = vt_s[at, h * 64 : (h + 1) * 64, :]
                acc_s[h] = acc_s[h] * decay + dot(value_t, expo.astype(BF16), NN)

        for h in range(heads):
            total = stat_s[heads + h]
            ot_ref[i, h * 64 : (h + 1) * 64, :] = acc_s[h] / total
            lse_ref[i, h : h + 1, :] = stat_s[h] + jnp.log(total)
        mixed_refs[i][...] = ot_ref[i].T.astype(BF16)


def attend(info, q, kv_all, band, heads, groups, ring, block):
    width = heads * 64
    return kernel_call(
        functools.partial(attend_kernel, heads=heads, groups=groups, ring=ring, block=block),
        "attend",
        [info],
        [q, *kv_all, band],
        [((groups, width, block), F32), ((groups, 8, block), F32)]
        + [((block, width), BF16)] * groups,
        [
            ((heads, 5, block, block), F32),
            ((groups * ring, block, 256), BF16),
            ((groups * ring, 256, block), BF16),
            ((groups * ring * block, 128), F32),
            ((block, block), F32),
            ((2 * heads, 1, block), F32),
            ((heads, 64, block), F32),
        ],
    )


def attend_back_kernel(info_ref, q_ref, *refs, heads, groups, ring, block):
    kv_refs, refs = refs[:ring], refs[ring:]
    band_ref, refs = refs[0], refs[1:]
    dmix_refs, refs = refs[:groups], refs[groups:]
    ot_ref, lse_ref, dq_ref, own_ref = refs[:4]
    other_refs, refs = refs[4 : 3 + ring], refs[3 + ring :]
    dband_ref, bias_s, key_s, value_s, kt_s, seg_s, mask_s, delta_s, dqt_s, dkv_s, dbias_s, dmix_s = refs
    wide = 256
    set_bias(band_ref, bias_s, heads, block)
    seg, spans = set_keys(info_ref, kv_refs, seg_s, groups, ring, block)
    for r in range(ring):
        for g in range(groups):
            at, rows = r * groups + g, slice(g * block, (g + 1) * block)
            key_s[at] = kv_refs[r][rows, :wide]
            value_s[at] = kv_refs[r][rows, wide:]
            kt_s[at] = kv_refs[r][rows, :wide].astype(F32).T.astype(BF16)
    dkv_s[...] = jnp.zeros_like(dkv_s)
    dbias_s[...] = jnp.zeros_like(dbias_s)
    spare = jnp.zeros((block, wide - heads * 64), BF16)
    for i in range(groups):
        qb = (i ^ info_ref[0]) * ring + info_ref[1]
        rows = slice(i * block, (i + 1) * block)
        segq = seg[i : i + 1, :]
        dmix_s[...] = jnp.concatenate([dmix_refs[i][...], spare], axis=1)
        dmix_t = dmix_s[...].astype(F32).T
        for h in range(heads):
            cut = slice(h * 64, (h + 1) * 64)
            delta_s[h] = jnp.sum(dmix_t[cut, :] * ot_ref[i, cut, :], axis=0, keepdims=True)
        dqt_s[...] = jnp.zeros_like(dqt_s)

        @pl.loop(spans[i][0], spans[i][1])
        def _(kb):
            at = key_at(kb, info_ref, ring, groups)
            set_mask(mask_s, seg_s, segq, pl.multiple_of(at * block, block), block)
            d = jnp.clip(kb - qb, -2, 2) + 2
            for h in range(heads):
                lane = (h // 2) * 128
                query = (head_mask(q_ref[rows, lane : lane + 128], h % 2) * 0.125).astype(BF16)
                d_out = head_mask(dmix_s[:, lane : lane + 128], h % 2)
                key = key_s[at, :, lane : lane + 128]
                value = value_s[at, :, lane : lane + 128]
                scores = dot(key, query, NT) + bias_s[h, d] + mask_s[...]
                soft = jnp.exp(scores - lse_ref[i, h : h + 1, :])
                d_soft = dot(value, d_out, NT)
                d_scores = (soft * (d_soft - delta_s[h])).astype(BF16)
                dkv_s[at, :, wide + lane : wide + lane + 128] += dot(soft.astype(BF16), d_out, NN)
                dkv_s[at, :, lane : lane + 128] += dot(d_scores, query, NN)
                dqt_s[h * 64 : (h + 1) * 64, :] += dot(
                    kt_s[at, h * 64 : (h + 1) * 64, :], d_scores, NN
                )
                dbias_s[h, d] += d_scores.astype(F32)

        pad = jnp.zeros((wide - heads * 64, block), F32)
        dq_ref[rows, :] = (jnp.concatenate([dqt_s[...], pad], axis=0) * 0.125).T.astype(BF16)
    for r in range(ring):
        for g in range(groups):
            at, rows = r * groups + g, slice(g * block, (g + 1) * block)
            if r == 0:
                own_ref[rows, :] = dkv_s[at]
            else:
                other_refs[r - 1][rows, :] = dkv_s[at].astype(BF16)
    zero = jnp.zeros((block, block), F32)
    for h in range(heads):
        for d in range(5):
            if d in (0, 4):
                tile = jnp.sum(dbias_s[h, d], axis=0, keepdims=True)
                tile = jnp.concatenate([tile, zero[:1]], axis=1)
            else:
                tile = jnp.concatenate([zero, dbias_s[h, d]], axis=1)
                tall = block
                while tall > 1:
                    tall = tall // 2
                    tile = tile[:tall] + pltpu.roll(tile[tall:], 2 * block - tall, 1)
            dband_ref[h, d : d + 1, :] = tile


def attend_back(info, q, kv_all, band, d_mix, out_t, lse, heads, groups, ring, block):
    own = groups * block
    return kernel_call(
        functools.partial(attend_back_kernel, heads=heads, groups=groups, ring=ring, block=block),
        "attend_back",
        [info],
        [q, *kv_all, band, *d_mix, out_t, lse],
        [((own, 256), BF16), ((own, 512), F32)]
        + [((own, 512), BF16)] * (ring - 1)
        + [((heads, 8, 2 * block), F32)],
        [
            ((heads, 5, block, block), F32),
            ((groups * ring, block, 256), BF16),
            ((groups * ring, block, 256), BF16),
            ((groups * ring, 256, block), BF16),
            ((groups * ring * block, 128), F32),
            ((block, block), F32),
            ((heads, 1, block), F32),
            ((heads * 64, block), F32),
            ((groups * ring, block, 512), F32),
            ((heads, 5, block, block), F32),
            ((block, 256), BF16),
        ],
    )


def expert_kernel(info_ref, *refs, experts, groups, ring):
    rows_ref, dz_ref, router_ref, w1_ref, w2_ref, prod_ref, back_ref, rpart_ref = refs[:8]
    g1_refs, g2_refs = refs[8 : 8 + ring], refs[8 + ring : 8 + 2 * ring]
    rows_t, dret_s, prob_s, prod_s, back_s = refs[8 + 2 * ring :]
    step = pl.program_id(0)
    me = info_ref[2]
    lane = lax.broadcasted_iota(jnp.int32, prob_s.shape, 1)

    @pl.when(step == 0)
    def _():
        rows = rows_ref[...]
        rows_t[...] = rows.astype(F32).T.astype(BF16)
        logits = dot(rows, router_ref[...], NT)
        logits = jnp.where(lane < experts, logits, MASKED)
        expo = jnp.exp(logits - jnp.max(logits, axis=1, keepdims=True))
        probs = expo / jnp.sum(expo, axis=1, keepdims=True)
        prob_s[...] = probs
        gate = jnp.sum(jnp.where(lane == me, probs, 0.0), axis=1, keepdims=True)
        dret_s[...] = (gate * dz_ref[...].astype(F32)).astype(BF16)
        prod_s[...] = jnp.zeros_like(prod_s)
        back_s[...] = jnp.zeros_like(back_s)

    w1 = w1_ref[...]
    w2 = w2_ref[...]
    d_ret = dret_s[...]
    pre = dot(rows_ref[...], w1, NN)
    cumulative = 0.5 * (1.0 + lax.erf(pre * (1.0 / math.sqrt(2.0))))
    density = jnp.exp(-0.5 * pre * pre) * (1.0 / math.sqrt(2.0 * math.pi))
    hidden = (pre * cumulative).astype(BF16)
    d_hidden = dot(d_ret, w2, NT)
    d_pre = (d_hidden * (cumulative + pre * density)).astype(BF16)
    prod_s[...] += dot(hidden, w2, NN)
    back_s[...] += dot(d_pre, w1, NT)
    g2 = dot(hidden, d_ret, TN).astype(BF16)
    share = g2_refs[0].shape[0]
    joint = g2.shape[0] // share
    for c in range(joint):
        where = ((step * joint + c) % ring) ^ info_ref[1]
        for m in range(ring):

            @pl.when(where == m)
            def _():
                g2_refs[m][...] = g2[c * share : (c + 1) * share, :]

    g1 = dot(rows_t[...], d_pre, NN).astype(BF16)
    tall = g1.shape[0] // (groups * ring)
    for c in range(groups * ring):
        for m in range(ring):

            @pl.when(((c % ring) ^ info_ref[1]) == m)
            def _():
                g1_refs[m][(c // ring) ^ info_ref[0]] = g1[c * tall : (c + 1) * tall, :]

    @pl.when(step == pl.num_programs(0) - 1)
    def _():
        probs = prob_s[...]
        gate = jnp.sum(jnp.where(lane == me, probs, 0.0), axis=1, keepdims=True)
        chosen = jnp.where(lane == me, 1.0, 0.0)
        produced = prod_s[...].astype(BF16)
        prod_ref[...] = produced
        d_gate = jnp.sum(
            dz_ref[...].astype(F32) * produced.astype(F32), axis=1, keepdims=True
        )
        d_logits = (d_gate * probs * (chosen - gate)).astype(BF16)
        back = back_s[...].astype(BF16).astype(F32) + dot(d_logits, router_ref[...], NN)
        back_ref[...] = back.astype(BF16)
        rpart_ref[...] = dot(rows_t[...], d_logits, NN)


def expert_layer(info, rows, dz, router_t, w1, w2, experts, groups, ring):
    slots, width = rows.shape
    lanes = router_t.shape[0]
    hidden = w1.shape[1]
    devices = groups * ring
    share = hidden // devices
    joint = 1
    while (share * joint) % 128:
        joint = joint * 2
    cut = share * joint
    grid = (hidden // cut,)
    fixed = lambda j, info_ref: (0, 0)
    piece = pl.BlockSpec((slots, width), fixed)
    return pl.pallas_call(
        functools.partial(expert_kernel, experts=experts, groups=groups, ring=ring),
        grid_spec=pltpu.PrefetchScalarGridSpec(
            num_scalar_prefetch=1,
            grid=grid,
            in_specs=[piece] * 2
            + [
                pl.BlockSpec((lanes, width), fixed),
                pl.BlockSpec((width, cut), lambda j, info_ref: (0, j)),
                pl.BlockSpec((cut, width), lambda j, info_ref: (j, 0)),
            ],
            out_specs=[piece] * 2
            + [pl.BlockSpec((width, lanes), fixed)]
            + [pl.BlockSpec((groups, width // devices, cut), lambda j, info_ref: (0, 0, j))] * ring
            + [
                pl.BlockSpec(
                    (None, share, width),
                    lambda j, info_ref: ((j * joint // ring) ^ info_ref[0], 0, 0),
                )
            ]
            * ring,
            scratch_shapes=[
                pltpu.VMEM((width, slots), BF16),
                pltpu.VMEM((slots, width), BF16),
                pltpu.VMEM((slots, lanes), F32),
                pltpu.VMEM((slots, width), F32),
                pltpu.VMEM((slots, width), F32),
            ],
        ),
        out_shape=(
            jax.ShapeDtypeStruct((slots, width), BF16),
            jax.ShapeDtypeStruct((slots, width), BF16),
            jax.ShapeDtypeStruct((width, lanes), F32),
        )
        + (jax.ShapeDtypeStruct((groups, width // devices, hidden), BF16),) * ring
        + (jax.ShapeDtypeStruct((groups, share, width), BF16),) * ring,
        compiler_params=pltpu.CompilerParams(
            dimension_semantics=("arbitrary",), vmem_limit_bytes=56 << 20
        ),
        cost_estimate=pl.CostEstimate(flops=1, transcendentals=1, bytes_accessed=1),
        name="experts",
    )(info, rows, dz, router_t, w1, w2)


def body(
    tokens,
    seg_ids,
    routes,
    attn_gain,
    query_key_value_weight,
    attention_output_weight,
    bias_table,
    ffn_gain,
    router_weight,
    expert_in,
    expert_out,
    out_grad,
):
    n_ctx = lax.axis_size("ctx")
    n_batch = lax.axis_size("batch")
    per, width = tokens.shape[1:]
    head_count = bias_table.shape[1]
    groups = math.gcd(head_count, n_ctx)
    ring = n_ctx // groups
    heads = head_count // groups
    part = heads * 64
    tall = query_key_value_weight.shape[0]
    lanes = 128
    wide = 256
    rows_own = groups * per
    capacity = max(2, 2 * per // n_batch)
    fine = tall % 8 == 0
    ctx = lax.axis_index("ctx").astype(jnp.int32)
    zed = lax.axis_index("batch").astype(jnp.int32)
    group, own = ctx // ring, ctx % ring
    info = jnp.stack([group, own, zed])

    def over_groups(parts):
        return [
            parts[m] if m == 0 else swap(parts[m], "ctx", n_ctx, ring * m) for m in range(groups)
        ]

    def over_ring(parts):
        return [parts[m] if m == 0 else swap(parts[m], "ctx", n_ctx, m) for m in range(ring)]

    def over_batch(parts):
        return [
            parts[m] if m == 0 else swap(parts[m], "batch", n_batch, m) for m in range(n_batch)
        ]

    def gather_batch(rows):
        step = 1
        while step < n_batch:
            rows = jnp.concatenate([rows, swap(rows, "batch", n_batch, step)], axis=0)
            step = step * 2
        return rows

    def turn_batch(rows):
        rows = rows.reshape(n_batch, capacity, width)
        rows = lax.all_to_all(rows, "batch", split_axis=0, concat_axis=0, tiled=True)
        return rows.reshape(n_batch * capacity, width)

    def natural(pieces, columns):
        pieces = [p.reshape(n_batch, groups, tall, columns) for p in pieces]
        pieces = xor_order(pieces, own)
        pieces = [xor_order([c[z] for z in range(n_batch)], zed) for c in pieces]
        pieces = [[xor_order([b[g] for g in range(groups)], group) for b in c] for c in pieces]
        order = [(g, r, z) for g in range(groups) for r in range(ring) for z in range(n_batch)]
        return [jnp.concatenate([pieces[r][z][g] for g, r, z in order], axis=0)]

    first = kernel_call(
        functools.partial(first_kernel, part=part),
        "first",
        [info],
        [tokens[0], seg_ids, attn_gain[None, :], query_key_value_weight],
        [((per + 16, width), BF16)] + [((tall, 3 * part), BF16)] * groups,
    )
    message, cuts = first[0], list(first[1:])
    cuts = jnp.concatenate(over_groups(cuts), axis=0)
    arrived = over_groups([message] * groups)
    cuts = gather_batch(cuts)

    route_row = routes.reshape(1, per)
    d_result = out_grad[0]
    slots = n_batch * capacity
    pick, pick_t, dz_sent = kernel_call(
        functools.partial(dispatch_kernel, capacity=capacity),
        "dispatch",
        [],
        [route_row, d_result],
        [((slots, per), BF16), ((per, slots), BF16), ((slots, width), BF16)],
    )

    both = jnp.concatenate(
        [attention_output_weight, jnp.pad(router_weight, ((0, 0), (0, lanes - n_batch)))], axis=1
    )
    both = gather_batch(both)
    arrived, cuts = lax.optimization_barrier((arrived, cuts))
    cuts = over_ring([cuts] * ring)
    cuts, dz_sent, both = lax.optimization_barrier((cuts, dz_sent, both))
    dz_there = turn_batch(dz_sent)
    both = [both] + [swap(both, "ctx", n_ctx, ring * m) for m in range(1, groups)]
    if not fine:
        cuts = natural(cuts, 3 * part)
    kv_rows = rows_own + 16
    q, kv_own, w_head, x_all = kernel_call(
        functools.partial(
            project_kernel,
            groups=groups,
            ring=ring,
            batch=n_batch,
            tall=tall,
            part=part,
            per=per,
            pieces=len(cuts),
        ),
        "project",
        [info],
        [*arrived, *cuts],
        [
            ((rows_own, wide), BF16),
            ((kv_rows, 2 * wide), BF16),
            ((width, 3 * wide), BF16),
            ((rows_own, width), BF16),
        ],
        [((width, 3 * part), F32)],
    )
    kv_all = over_ring([kv_own] * ring)

    table = sum(
        jnp.where(group == g, bias_table[:, g * heads : (g + 1) * heads], 0) for g in range(groups)
    )
    onehot = band_onehot(per)
    band = jnp.einsum("dbc,bh->hdc", jnp.asarray(onehot, BF16), table, preferred_element_type=F32)
    band = jnp.pad(band, ((0, 0), (0, 3), (0, 0)))
    out_t, lse, *mixed = attend(info, q, kv_all, band, heads, groups, ring, per)

    mixed, both, dz_there = lax.optimization_barrier((mixed, both, dz_there))
    both = jnp.stack([b.reshape(n_batch, tall, -1) for b in both], axis=1)
    both = over_ring([both.reshape(n_batch * groups * tall, -1)] * ring)
    if not fine:
        both = natural(both, width + lanes)
    mixed = over_groups(mixed)
    shapes = dict(groups=groups, ring=ring, batch=n_batch, tall=tall, part=part, lanes=lanes)
    w_out, router_t, middle, gate, rows_sent = kernel_call(
        functools.partial(middle_kernel, pieces=len(both), **shapes),
        "middle",
        [info],
        [*mixed, *both, tokens[0], ffn_gain[None, :], pick, route_row],
        [
            ((width, width), BF16),
            ((lanes, width), BF16),
            ((per, width), F32),
            ((per, 1), F32),
            ((slots, width), BF16),
        ],
        [((width, width + lanes), F32)],
    )
    rows_there = turn_batch(rows_sent)
    outs = expert_layer(
        info, rows_there, dz_there, router_t, expert_in[0], expert_out[0], n_batch, groups, ring
    )
    produced, back, router_part = outs[:3]
    g1, g2 = list(outs[3 : 3 + ring]), list(outs[3 + ring :])
    back = turn_batch(back)

    def ring_sum(grads):
        return sum(g.astype(F32) for g in over_ring(grads)).astype(BF16)

    def group_sum(got):
        return sum(g.astype(F32) for g in got)[None]

    g1, g2 = ring_sum(g1), ring_sum(g2)
    g1 = over_groups([g1[m] for m in range(groups)])
    back, g2 = lax.optimization_barrier((back, g2))
    grads_shape = (
        [((n_batch, groups, tall, width + lanes), F32)]
        + [((n_batch, groups, tall, width + lanes), BF16)] * (ring - 1)
        if fine
        else [((width, width + lanes), F32)]
    )
    d_middle, ffn_gain_part, *rest = kernel_call(
        functools.partial(branch_kernel, **shapes),
        "branch",
        [info],
        [back, *mixed, pick_t, middle, d_result, ffn_gain[None, :], w_out, router_part],
        [((per, width), F32), ((1, width), F32)] + [((per, part), BF16)] * groups + grads_shape,
    )
    d_mix, out_parts = rest[:groups], rest[groups:]
    d_mix, g1 = lax.optimization_barrier((d_mix, g1))
    d_mix = over_groups(d_mix)
    expert_in_grad = group_sum(g1)
    d_mix, g2, produced = lax.optimization_barrier((d_mix, g2, produced))
    g2 = over_groups([g2[m] for m in range(groups)])
    returned = turn_batch(produced)

    dq, dkv_own, *rest = attend_back(
        info, q, kv_all, band, d_mix, out_t, lse, heads, groups, ring, per
    )
    dkv_other, dband = rest[: ring - 1], rest[ring - 1]
    dkv_other, g2, returned = lax.optimization_barrier((dkv_other, g2, returned))
    dkv_got = over_ring([dkv_own] + dkv_other)[1:]
    expert_out_grad = group_sum(g2)

    grads_shape = (
        [((n_batch, groups, tall, 3 * part), F32)]
        + [((n_batch, groups, tall, 3 * part), BF16)] * (ring - 1)
        if fine
        else [((width, 3 * part), F32)]
    )
    d_packed, *packed_parts = kernel_call(
        functools.partial(
            weight_kernel,
            groups=groups,
            ring=ring,
            batch=n_batch,
            tall=tall,
            part=part,
            per=per,
        ),
        "weight",
        [info],
        [dq, dkv_own, *dkv_got, x_all],
        [((rows_own, 3 * wide), BF16)] + grads_shape,
    )
    *d_normed, attn_gain_part = kernel_call(
        functools.partial(unproject_kernel, per=per),
        "unproject",
        [],
        [d_packed, x_all, w_head, attn_gain[None, :]],
        [((per, width), F32)] + [((per, width), BF16)] * (groups - 1) + [((1, width), F32)],
    )
    got = over_groups(d_normed)
    d_normed = sum(g.astype(F32) for g in got)
    flat = tokens[0].astype(F32)
    gain1 = attn_gain.astype(F32)[None, :]
    r1 = lax.rsqrt(jnp.mean(flat * flat, axis=1, keepdims=True) + EPSILON)
    scaled1 = gain1 * d_normed
    tokens_grad = (
        d_middle
        + r1 * scaled1
        - flat * (r1 * r1 * r1) * jnp.mean(scaled1 * flat, axis=1, keepdims=True)
    ).astype(BF16)[None]

    def weight_sum(parts):
        if not fine:
            grad = parts[0].reshape(groups, ring, n_batch, tall, parts[0].shape[1])
            parts = xor_order([grad[:, r] for r in range(ring)], own)
            parts = [xor_order([p[:, z] for z in range(n_batch)], zed) for p in parts]
            parts = [[xor_order([z[g] for g in range(groups)], group) for z in p] for p in parts]
            parts = [jnp.stack([jnp.stack(z) for z in p]) for p in parts]
            parts = [parts[0]] + [p.astype(BF16) for p in parts[1:]]
        got = over_ring(parts)
        half = sum(g.astype(F32) for g in got)
        got = over_batch([half[0]] + [half[m].astype(BF16) for m in range(1, n_batch)])
        return sum(g.astype(F32) for g in got)

    parts = weight_sum(packed_parts)
    parts = over_groups([parts[m].astype(BF16) for m in range(groups)])
    parts = xor_order(parts, group)
    qkv_grad = jnp.concatenate(
        [p[:, k * part : (k + 1) * part] for k in range(3) for p in parts], axis=1
    ).astype(F32)
    parts = weight_sum(out_parts)
    got = over_groups([parts[0]] + [parts[m].astype(BF16) for m in range(1, groups)])
    out_grad_sum = sum(g.astype(F32) for g in got)
    out_weight_grad = out_grad_sum[:, :width]
    router_grad = out_grad_sum[:, width : width + n_batch]

    d_table = jnp.einsum(
        "dbc,hdc->bh",
        jnp.asarray(onehot, F32),
        dband[:, :5],
        precision=lax.Precision.HIGHEST,
        preferred_element_type=F32,
    )
    d_table = jnp.concatenate(
        [jnp.where(group == g, d_table, 0.0) for g in range(groups)], axis=1
    )
    late = jnp.concatenate([attn_gain_part[0], ffn_gain_part[0], d_table.reshape(-1)])
    late = jnp.pad(late, (0, -late.shape[0] % lanes)).reshape(-1, lanes)
    late = jnp.broadcast_to(late[None], (n_ctx * n_batch, *late.shape))
    late = lax.all_to_all(late, ("ctx", "batch"), split_axis=0, concat_axis=0, tiled=True)
    late = jnp.sum(late, axis=0).reshape(-1)
    attn_gain_grad = late[:width]
    ffn_gain_grad = late[width : 2 * width]
    bias_grad = late[2 * width : 2 * width + bias_table.size].reshape(bias_table.shape)
    layer_out = kernel_call(
        combine_kernel,
        "combine",
        [],
        [returned, pick_t, middle, gate],
        [((per, width), BF16)],
    )[0][None]
    return (
        layer_out,
        tokens_grad,
        attn_gain_grad,
        qkv_grad,
        out_weight_grad,
        bias_grad,
        ffn_gain_grad,
        router_grad,
        expert_in_grad,
        expert_out_grad,
    )


def solution(mesh):
    return jax.shard_map(
        body,
        mesh=mesh,
        in_specs=(
            P("batch", "ctx", None),
            P("batch", "ctx"),
            P("ctx", "batch", None, None),
            P(),
            P(("ctx", "batch"), None),
            P(("ctx", "batch"), None),
            P(),
            P(),
            P(("ctx", "batch"), None),
            P("batch", None, None),
            P("batch", None, None),
            P("batch", "ctx", None),
        ),
        out_specs=(
            P("batch", "ctx", None),
            P("batch", "ctx", None),
            P(),
            P(("ctx", "batch"), None),
            P(("ctx", "batch"), None),
            P(),
            P(),
            P(("ctx", "batch"), None),
            P("batch", "ctx", None),
            P("batch", "ctx", None),
        ),
        check_vma=False,
    )
```

profile of v0, /device:TPU:0, one launch (start us, length us, event | category | flops | bytes accessed | tf_op | source)
XLA Modules:
  0.0 325.6 jit_solution(7194930017860688665)
XLA Ops:
  4.6 2.9 collective-permute-start
  9.7 2.9 collective-permute-start.5
  13.3 5.1 %collective-permute-done.3 = bf16[24,576]{1,0:T(8,128)(2,1)S(1)} collective-permute-done((bf16[24,576]{1,0:T(8,128)(2,1)}, bf16[24,576]{1,0:T(8,128)(2,1)S(1)}, u32[]{:S(2)}, u32[]{:S(2)}) %collective-permute-start.3) | collective-permute-done | bytes 27680 | tf_op jit(solution)/shard_map/ppermute | solution.py:100
  18.4 2.7 collective-permute-start.2
  23.6 3.3 collective-permute-done.6
  26.9 2.7 collective-permute-start.7
  29.6 8.8 %collective-permute-done.7 = bf16[192,576]{1,0:T(8,128)(2,1)S(1)} collective-permute-done((bf16[192,576]{1,0:T(8,128)(2,1)S(1)}, bf16[192,576]{1,0:T(8,128)(2,1)S(1)}, u32[]{:S(2)}, u32[]{:S(2)}) %collective-permute-start.7) | collective-permute-done | bytes 221216 | tf_op jit(solution)/shard_map/ppermute | solution.py:100
  39.4 3.4 %collective-permute-done.9 = bf16[24,896]{1,0:T(8,128)(2,1)S(1)} collective-permute-done((bf16[24,896]{1,0:T(8,128)(2,1)S(1)}, bf16[24,896]{1,0:T(8,128)(2,1)S(1)}, u32[]{:S(2)}, u32[]{:S(2)}) %collective-permute-start.9) | collective-permute-done | bytes 43040 | tf_op jit(solution)/shard_map/ppermute | solution.py:100
  49.5 4.6 %all-to-all-start = ((bf16[4,128,768]{2,1,0:T(8,128)(2,1)}), bf16[4,128,768]{2,1,0:T(8,128)(2,1)S(1)}, u32[]{:S(2)}, u32[]{:S(2)}) async-start(bf16[4,128,768]{2,1,0:T(8,128)(2,1)} %bitcast.157), calls=%async_computation | async-start | bytes 1572864 | tf_op jit(solution)/shard_map/all_to_all | solution.py:703
  54.1 5.0 %project.1 = (bf16[1024,256]{1,0:T(8,128)(2,1)}, bf16[1040,512]{1,0:T(8,128)(2,1)}, bf16[768,768]{1,0:T(8,128)(2,1)}, bf16[1024,768]{1,0:T(8,128)(2,1)}) custom-call(s32[3]{0:T(128)} %pad_add_fusion.info_ref, bf16[272,768]{1,0:T(8,128)(2,1)} %get-tuple-element.105.refs_0_, bf16[272,768]{1,0:T(8,128)(2,1)} %copy-done.18, bf16[272,768]{1,0:T(8,128)(2,1)} %copy-done.19, ...), custom_call_target="tpu_custom_call" | custom-call | flops 1 | bytes 1 | tf_op jit(solution)/shard_map/project/pallas_call | solution.py:87
  60.0 2.6 collective-permute-start.14
  65.3 23.5 %attend.1 = (f32[4,192,256]{2,1,0:T(8,128)}, f32[4,8,256]{2,1,0:T(8,128)}, bf16[256,192]{1,0:T(8,128)(2,1)}, bf16[256,192]{1,0:T(8,128)(2,1)}, bf16[256,192]{1,0:T(8,128)(2,1)}, /*index=5*/bf16[256,192]{1,0:T(8,128)(2,1)}) custom-call(s32[3]{0:T(128)} %pad_add_fusion.info_ref, bf16[1024,256]{1,0:T(8,128)(2,1)} %get-tuple-element.113.q_ref, ...), custom_call_target="tpu_custom_call" | custom-call | flops 1 | bytes 1 | tf_op jit(solution)/shard_map/attend/pallas_call | solution.py:87
  89.9 2.6 collective-permute-start.17
  99.0 4.4 %middle.1 = (bf16[768,768]{1,0:T(8,128)(2,1)}, bf16[128,768]{1,0:T(8,128)(2,1)}, f32[256,768]{1,0:T(8,128)}, f32[256,1]{1,0:T(8,128)}, bf16[512,768]{1,0:T(8,128)(2,1)}) custom-call(s32[3]{0:T(128)} %pad_add_fusion.info_ref, bf16[256,192]{1,0:T(8,128)(2,1)} %get-tuple-element.121.refs_0_, bf16[256,192]{1,0:T(8,128)(2,1)} %copy-done.13, ...), custom_call_target="tpu_custom_call" | custom-call | flops 1 | bytes 1 | tf_op jit(solution)/shard_map/middle/pallas_call | solution.py:87
  103.3 25.4 %all_to_all.25 = bf16[4,128,768]{2,1,0:T(8,128)(2,1)} all-to-all(bf16[4,128,768]{2,1,0:T(8,128)(2,1)} %bitcast.159), channel_id=1, replica_groups=mesh['ctx'=8,'batch'=4] {'batch'}, dimensions={0} | all-to-all | bytes 1572864 | tf_op jit(solution)/shard_map/all_to_all | solution.py:703
  128.8 30.1 %experts.1 = (bf16[512,768]{1,0:T(8,128)(2,1)}, bf16[512,768]{1,0:T(8,128)(2,1)}, f32[768,128]{1,0:T(8,128)}, bf16[4,96,3072]{2,1,0:T(8,128)(2,1)}, bf16[4,96,30...) custom-call(s32[3]{0:T(128)} %pad_add_fusion.info_ref, bf16[512,768]{1,0:T(8,128)(2,1)} %bitcast.150, ...), custom_call_target="tpu_custom_call" | custom-call | flops 1 | bytes 1 | tf_op jit(solution)/shard_map/experts/pallas_call | solution.py:604
  159.4 3.5 %all-to-all-start.2 = ((bf16[4,128,768]{2,1,0:T(8,128)(2,1)}), bf16[4,128,768]{2,1,0:T(8,128)(2,1)S(1)}, u32[]{:S(2)}, u32[]{:S(2)}) async-start(bf16[4,128,768]{2,1,0:T(8,128)(2,1)} %bitcast.158), calls=%async_computation.2 | async-start | bytes 1572864 | tf_op jit(solution)/shard_map/all_to_all | solution.py:703
  162.9 3.4 %collective-permute-done.20 = bf16[4,96,3072]{2,1,0:T(8,128)(2,1)S(1)} collective-permute-done((bf16[4,96,3072]{2,1,0:T(8,128)(2,1)}, bf16[4,96,3072]{2,1,0:T(8,128)(2,1)S(1)}, u32[]{:S(2)}, u32[]{:S(2)}) %collective-permute-start.20) | collective-permute-done | bytes 2359328 | tf_op jit(solution)/shard_map/ppermute | solution.py:100
  175.9 7.5 %all-to-all-done.2 = bf16[4,128,768]{2,1,0:T(8,128)(2,1)S(1)} async-done(((bf16[4,128,768]{2,1,0:T(8,128)(2,1)}), bf16[4,128,768]{2,1,0:T(8,128)(2,1)S(1)}, u32[]{:S(2)}, u32[]{:S(2)}) %all-to-all-start.2) | async-done | bytes 786464 | tf_op jit(solution)/shard_map/all_to_all | solution.py:703
  184.4 6.7 %branch.1 = (f32[256,768]{1,0:T(8,128)}, f32[1,768]{1,0:T(1,128)}, bf16[256,192]{1,0:T(8,128)(2,1)}, bf16[256,192]{1,0:T(8,128)(2,1)}, bf16[256,192]{1,0:T(8,128...) custom-call(s32[3]{0:T(128)} %pad_add_fusion.info_ref, ...), custom_call_target="tpu_custom_call" | custom-call | flops 1 | bytes 1 | tf_op jit(solution)/shard_map/branch/pallas_call | solution.py:87
  191.1 9.0 %collective-permute-done.22 = bf16[96,3072]{1,0:T(8,128)(2,1)} collective-permute-done((bf16[96,3072]{1,0:T(8,128)(2,1)}, bf16[96,3072]{1,0:T(8,128)(2,1)}, u32[]{:S(2)}, u32[]{:S(2)}) %collective-permute-start.22) | collective-permute-done | bytes 589856 | tf_op jit(solution)/shard_map/ppermute | solution.py:100
  214.4 3.7 %all-to-all-start.3 = ((bf16[4,128,768]{2,1,0:T(8,128)(2,1)}), bf16[4,128,768]{2,1,0:T(8,128)(2,1)S(1)}, u32[]{:S(2)}, u32[]{:S(2)}) async-start(bf16[4,128,768]{2,1,0:T(8,128)(2,1)} %bitcast.156), calls=%async_computation.3 | async-start | bytes 1572864 | tf_op jit(solution)/shard_map/all_to_all | solution.py:703
  218.2 2.8 add_bitcast_fusion.1
  227.2 25.9 %attend_back.1 = (bf16[1024,256]{1,0:T(8,128)(2,1)}, f32[1024,512]{1,0:T(8,128)}, bf16[1024,512]{1,0:T(8,128)(2,1)}, f32[3,8,512]{2,1,0:T(8,128)}) custom-call(s32[3]{0:T(128)} %pad_add_fusion.info_ref, bf16[1024,256]{1,0:T(8,128)(2,1)} %get-tuple-element.113.q_ref, bf16[1040,512]{1,0:T(8,128)(2,1)} %get-tuple-element.114.refs_0_, ...), custom_call_target="tpu_custom_call" | custom-call | flops 1 | bytes 1 | tf_op jit(solution)/shard_map/attend_back/pallas_call | solution.py:87
  254.9 5.8 %collective-permute-done.44 = bf16[4,24,896]{2,1,0:T(8,128)(2,1)} collective-permute-done((bf16[4,24,896]{2,1,0:T(8,128)(2,1)}, bf16[4,24,896]{2,1,0:T(8,128)(2,1)}, u32[]{:S(2)}, u32[]{:S(2)}) %collective-permute-start.44) | collective-permute-done | bytes 172064 | tf_op jit(solution)/shard_map/ppermute | solution.py:100
  272.8 7.9 %weight.1 = (bf16[1024,768]{1,0:T(8,128)(2,1)}, f32[4,4,24,576]{3,2,1,0:T(8,128)}, bf16[4,4,24,576]{3,2,1,0:T(8,128)(2,1)}) custom-call(s32[3]{0:T(128)} %pad_add_fusion.info_ref, bf16[1024,256]{1,0:T(8,128)(2,1)} %get-tuple-element.165.dq_ref, f32[1024,512]{1,0:T(8,128)} %get-tuple-element.166.refs_0_, bf16[1024,512]{1,0:T(8,128)(2,1)} %collective-permute-done.30.refs_1_, ...), custom_call_target="tpu_custom_call" | custom-call | flops 1 | bytes 1 | tf_op jit(solution)/shard_map/weight/pallas_call | solution.py:87
  280.8 4.4 %unproject.1 = (f32[256,768]{1,0:T(8,128)}, bf16[256,768]{1,0:T(8,128)(2,1)}, bf16[256,768]{1,0:T(8,128)(2,1)}, bf16[256,768]{1,0:T(8,128)(2,1)}, f32[1,768]{1,0:T(1,128)}) custom-call(bf16[1024,768]{1,0:T(8,128)(2,1)} %get-tuple-element.169.dp_ref, bf16[1024,768]{1,0:T(8,128)(2,1)} %get-tuple-element.168.refs_2_.x_ref, ...), custom_call_target="tpu_custom_call" | custom-call | flops 1 | bytes 1 | tf_op jit(solution)/shard_map/unproject/pallas_call | solution.py:87
  288.7 2.7 add_bitcast_fusion
  292.2 3.3 %all-to-all-start.4 = ((f32[32,15,128]{2,1,0:T(8,128)}), f32[32,15,128]{2,1,0:T(8,128)}, u32[]{:S(2)}, u32[]{:S(2)}) async-start(f32[32,15,128]{2,1,0:T(8,128)} %broadcast_in_dim.51), calls=%async_computation.4 | async-start | bytes 524288 | tf_op jit(solution)/shard_map/all_to_all | solution.py:926
  295.5 3.9 %collective-permute-done.32 = bf16[256,768]{1,0:T(8,128)(2,1)S(1)} collective-permute-done((bf16[256,768]{1,0:T(8,128)(2,1)}, bf16[256,768]{1,0:T(8,128)(2,1)S(1)}, u32[]{:S(2)}, u32[]{:S(2)}) %collective-permute-start.32) | collective-permute-done | bytes 393248 | tf_op jit(solution)/shard_map/ppermute | solution.py:100
  303.1 6.3 %collective-permute-start.36 = (bf16[4,24,576]{2,1,0:T(8,128)(2,1)}, bf16[4,24,576]{2,1,0:T(8,128)(2,1)}, u32[]{:S(2)}, u32[]{:S(2)}) collective-permute-start(bf16[4,24,576]{2,1,0:T(8,128)(2,1)} %get-tuple-element.251), channel_id=1, source_target_pairs={{0,2},{1,3},{2,0},{3,1},{4,6},{5,7},{6,4},{7,5},{8,10},{9,11},{10,... | collective-permute-start | bytes 331784 | tf_op jit(solution)/shard_map/ppermute | solution.py:100
  312.6 3.9 %collective-permute-done.37 = bf16[4,24,576]{2,1,0:T(8,128)(2,1)} collective-permute-done((bf16[4,24,576]{2,1,0:T(8,128)(2,1)}, bf16[4,24,576]{2,1,0:T(8,128)(2,1)}, u32[]{:S(2)}, u32[]{:S(2)}) %collective-permute-start.37) | collective-permute-done | bytes 110624 | tf_op jit(solution)/shard_map/ppermute | solution.py:100
  (206 shorter events, 93.6 us)
Async XLA Ops:
  4.6 33.9 %collective-permute-start = (bf16[272,768]{1,0:T(8,128)(2,1)}, bf16[272,768]{1,0:T(8,128)(2,1)S(1)}, u32[]{:S(2)}, u32[]{:S(2)}) collective-permute-start(bf16[272,768]{1,0:T(8,128)(2,1)} %get-tuple-element.105.refs_0_), channel_id=1, source_target_pairs={{0,8},{4,12},{8,0},{12,4},{16,24},{20,28},{24,16},{28,20},{1,9},{5... | collective-permute-start | bytes 1253384 | tf_op jit(solution)/shard_map/ppermute | solution.py:100
  7.6 30.9 %collective-permute-start.1 = (bf16[272,768]{1,0:T(8,128)(2,1)}, bf16[272,768]{1,0:T(8,128)(2,1)S(1)}, u32[]{:S(2)}, u32[]{:S(2)}) collective-permute-start(bf16[272,768]{1,0:T(8,128)(2,1)} %get-tuple-element.105.refs_0_), channel_id=1, source_target_pairs={{0,16},{4,20},{8,24},{12,28},{16,0},{20,4},{24,8},{28,12},{1,17},{... | collective-permute-start | bytes 1253384 | tf_op jit(solution)/shard_map/ppermute | solution.py:100
  9.1 9.3 %collective-permute-start.3 = (bf16[24,576]{1,0:T(8,128)(2,1)}, bf16[24,576]{1,0:T(8,128)(2,1)S(1)}, u32[]{:S(2)}, u32[]{:S(2)}) collective-permute-start(bf16[24,576]{1,0:T(8,128)(2,1)} %get-tuple-element.102), channel_id=1, source_target_pairs={{0,8},{4,12},{8,0},{12,4},{16,24},{20,28},{24,16},{28,20},{1,9},{5... | collective-permute-start | bytes 82952 | tf_op jit(solution)/shard_map/ppermute | solution.py:100
  9.6 11.5 %collective-permute-start.4 = (bf16[24,576]{1,0:T(8,128)(2,1)}, bf16[24,576]{1,0:T(8,128)(2,1)S(1)}, u32[]{:S(2)}, u32[]{:S(2)}) collective-permute-start(bf16[24,576]{1,0:T(8,128)(2,1)} %get-tuple-element.103), channel_id=1, source_target_pairs={{0,16},{4,20},{8,24},{12,28},{16,0},{20,4},{24,8},{28,12},{1,17},{... | collective-permute-start | bytes 82952 | tf_op jit(solution)/shard_map/ppermute | solution.py:100
  9.7 11.5 %collective-permute-start.5 = (bf16[24,576]{1,0:T(8,128)(2,1)}, bf16[24,576]{1,0:T(8,128)(2,1)S(1)}, u32[]{:S(2)}, u32[]{:S(2)}) collective-permute-start(bf16[24,576]{1,0:T(8,128)(2,1)} %get-tuple-element.104), channel_id=1, source_target_pairs={{0,24},{4,28},{8,16},{12,20},{16,8},{20,12},{24,0},{28,4},{1,25},{... | collective-permute-start | bytes 82952 | tf_op jit(solution)/shard_map/ppermute | solution.py:100
  18.4 20.1 %collective-permute-start.2 = (bf16[272,768]{1,0:T(8,128)(2,1)}, bf16[272,768]{1,0:T(8,128)(2,1)S(1)}, u32[]{:S(2)}, u32[]{:S(2)}) collective-permute-start(bf16[272,768]{1,0:T(8,128)(2,1)} %get-tuple-element.105.refs_0_), channel_id=1, source_target_pairs={{0,24},{4,28},{8,16},{12,20},{16,8},{20,12},{24,0},{28,4},{1,25},{... | collective-permute-start | bytes 1253384 | tf_op jit(solution)/shard_map/ppermute | solution.py:100
  26.9 11.6 %collective-permute-start.7 = (bf16[192,576]{1,0:T(8,128)(2,1)S(1)}, bf16[192,576]{1,0:T(8,128)(2,1)S(1)}, u32[]{:S(2)}, u32[]{:S(2)}) collective-permute-start(bf16[192,576]{1,0:T(8,128)(2,1)S(1)} %get-tuple-element.262), channel_id=1, source_target_pairs={{0,2},{1,3},{2,0},{3,1},{4,6},{5,7},{6,4},{7,5},{8,10},{9,11},{10,... | collective-permute-start | bytes 663560 | tf_op jit(solution)/shard_map/ppermute | solution.py:100
  38.6 10.9 %collective-permute-start.8 = (bf16[384,576]{1,0:T(8,128)(2,1)S(1)}, bf16[384,576]{1,0:T(8,128)(2,1)S(1)}, u32[]{:S(2)}, u32[]{:S(2)}) collective-permute-start(bf16[384,576]{1,0:T(8,128)(2,1)S(1)} %constant_dynamic-update-slice_fusion.5.refs_4_), channel_id=1, source_target_pairs={{0,4},{4,0},{8,12},{12,8},{16,20},{20,16},{24,28},{28,24},{1,5},{5... | collective-permute-start | bytes 1327112 | tf_op jit(solution)/shard_map/ppermute | solution.py:100
  49.5 39.4 %all-to-all-start = ((bf16[4,128,768]{2,1,0:T(8,128)(2,1)}), bf16[4,128,768]{2,1,0:T(8,128)(2,1)S(1)}, u32[]{:S(2)}, u32[]{:S(2)}) async-start(bf16[4,128,768]{2,1,0:T(8,128)(2,1)} %bitcast.157), calls=%async_computation | async-start | bytes 1572864 | tf_op jit(solution)/shard_map/all_to_all | solution.py:703
  59.1 29.7 %collective-permute-start.12 = (bf16[96,896]{1,0:T(8,128)(2,1)S(1)}, bf16[96,896]{1,0:T(8,128)(2,1)S(1)}, u32[]{:S(2)}, u32[]{:S(2)}) collective-permute-start(bf16[96,896]{1,0:T(8,128)(2,1)S(1)} %pad_maximum_fusion.1), channel_id=1, source_target_pairs={{0,8},{4,12},{8,0},{12,4},{16,24},{20,28},{24,16},{28,20},{1,9},{5... | collective-permute-start | bytes 516104 | tf_op jit(solution)/shard_map/ppermute | solution.py:100
  59.5 29.3 %collective-permute-start.13 = (bf16[96,896]{1,0:T(8,128)(2,1)S(1)}, bf16[96,896]{1,0:T(8,128)(2,1)S(1)}, u32[]{:S(2)}, u32[]{:S(2)}) collective-permute-start(bf16[96,896]{1,0:T(8,128)(2,1)S(1)} %pad_maximum_fusion.1), channel_id=1, source_target_pairs={{0,16},{4,20},{8,24},{12,28},{16,0},{20,4},{24,8},{28,12},{1,17},{... | collective-permute-start | bytes 516104 | tf_op jit(solution)/shard_map/ppermute | solution.py:100
  60.0 28.8 %collective-permute-start.14 = (bf16[96,896]{1,0:T(8,128)(2,1)S(1)}, bf16[96,896]{1,0:T(8,128)(2,1)S(1)}, u32[]{:S(2)}, u32[]{:S(2)}) collective-permute-start(bf16[96,896]{1,0:T(8,128)(2,1)S(1)} %pad_maximum_fusion.1), channel_id=1, source_target_pairs={{0,24},{4,28},{8,16},{12,20},{16,8},{20,12},{24,0},{28,4},{1,25},{... | collective-permute-start | bytes 516104 | tf_op jit(solution)/shard_map/ppermute | solution.py:100
  89.0 9.1 %collective-permute-start.18 = (bf16[384,896]{1,0:T(8,128)(2,1)S(1)}, bf16[384,896]{1,0:T(8,128)(2,1)S(1)}, u32[]{:S(2)}, u32[]{:S(2)}) collective-permute-start(bf16[384,896]{1,0:T(8,128)(2,1)S(1)} %bitcast.152), channel_id=1, source_target_pairs={{0,4},{4,0},{8,12},{12,8},{16,20},{20,16},{24,28},{28,24},{1,5},{5... | collective-permute-start | bytes 2064392 | tf_op jit(solution)/shard_map/ppermute | solution.py:100
  158.9 14.9 %collective-permute-start.19 = (bf16[4,384,768]{2,1,0:T(8,128)(2,1)}, bf16[4,384,768]{2,1,0:T(8,128)(2,1)}, u32[]{:S(2)}, u32[]{:S(2)}) collective-permute-start(bf16[4,384,768]{2,1,0:T(8,128)(2,1)} %get-tuple-element.135), channel_id=1, source_target_pairs={{0,4},{4,0},{8,12},{12,8},{16,20},{20,16},{24,28},{28,24},{1,5},{5... | collective-permute-start | bytes 7077896 | tf_op jit(solution)/shard_map/ppermute | solution.py:100
  159.4 24.1 %all-to-all-start.2 = ((bf16[4,128,768]{2,1,0:T(8,128)(2,1)}), bf16[4,128,768]{2,1,0:T(8,128)(2,1)S(1)}, u32[]{:S(2)}, u32[]{:S(2)}) async-start(bf16[4,128,768]{2,1,0:T(8,128)(2,1)} %bitcast.158), calls=%async_computation.2 | async-start | bytes 1572864 | tf_op jit(solution)/shard_map/all_to_all | solution.py:703
  170.2 20.9 %collective-permute-start.21 = (bf16[96,3072]{1,0:T(8,128)(2,1)}, bf16[96,3072]{1,0:T(8,128)(2,1)}, u32[]{:S(2)}, u32[]{:S(2)}) collective-permute-start(bf16[96,3072]{1,0:T(8,128)(2,1)} %get-tuple-element.244), channel_id=1, source_target_pairs={{0,8},{4,12},{8,0},{12,4},{16,24},{20,28},{24,16},{28,20},{1,9},{5... | collective-permute-start | bytes 1769480 | tf_op jit(solution)/shard_map/ppermute | solution.py:100
  172.1 28.0 %collective-permute-start.22 = (bf16[96,3072]{1,0:T(8,128)(2,1)}, bf16[96,3072]{1,0:T(8,128)(2,1)}, u32[]{:S(2)}, u32[]{:S(2)}) collective-permute-start(bf16[96,3072]{1,0:T(8,128)(2,1)} %get-tuple-element.243), channel_id=1, source_target_pairs={{0,16},{4,20},{8,24},{12,28},{16,0},{20,4},{24,8},{28,12},{1,17},{... | collective-permute-start | bytes 1769480 | tf_op jit(solution)/shard_map/ppermute | solution.py:100
  172.1 28.0 %collective-permute-start.23 = (bf16[96,3072]{1,0:T(8,128)(2,1)}, bf16[96,3072]{1,0:T(8,128)(2,1)}, u32[]{:S(2)}, u32[]{:S(2)}) collective-permute-start(bf16[96,3072]{1,0:T(8,128)(2,1)} %get-tuple-element.242), channel_id=1, source_target_pairs={{0,24},{4,28},{8,16},{12,20},{16,8},{20,12},{24,0},{28,4},{1,25},{... | collective-permute-start | bytes 1769480 | tf_op jit(solution)/shard_map/ppermute | solution.py:100
  203.6 17.4 %collective-permute-start.41 = (bf16[4,4,24,896]{3,2,1,0:T(8,128)(2,1)}, bf16[4,4,24,896]{3,2,1,0:T(8,128)(2,1)}, u32[]{:S(2)}, u32[]{:S(2)}) collective-permute-start(bf16[4,4,24,896]{3,2,1,0:T(8,128)(2,1)} %get-tuple-element.181), channel_id=1, source_target_pairs={{0,4},{4,0},{8,12},{12,8},{16,20},{20,16},{24,28},{28,24},{1,5},{5... | collective-permute-start | bytes 2064392 | tf_op jit(solution)/shard_map/ppermute | solution.py:100
  210.9 42.2 %collective-permute-start.27 = (bf16[384,768]{1,0:T(8,128)(2,1)}, bf16[384,768]{1,0:T(8,128)(2,1)}, u32[]{:S(2)}, u32[]{:S(2)}) collective-permute-start(bf16[384,768]{1,0:T(8,128)(2,1)} %get-tuple-element.240), channel_id=1, source_target_pairs={{0,8},{4,12},{8,0},{12,4},{16,24},{20,28},{24,16},{28,20},{1,9},{5... | collective-permute-start | bytes 1769480 | tf_op jit(solution)/shard_map/ppermute | solution.py:100
  211.9 41.3 %collective-permute-start.28 = (bf16[384,768]{1,0:T(8,128)(2,1)}, bf16[384,768]{1,0:T(8,128)(2,1)}, u32[]{:S(2)}, u32[]{:S(2)}) collective-permute-start(bf16[384,768]{1,0:T(8,128)(2,1)} %get-tuple-element.239), channel_id=1, source_target_pairs={{0,16},{4,20},{8,24},{12,28},{16,0},{20,4},{24,8},{28,12},{1,17},{... | collective-permute-start | bytes 1769480 | tf_op jit(solution)/shard_map/ppermute | solution.py:100
  213.0 40.2 %collective-permute-start.29 = (bf16[384,768]{1,0:T(8,128)(2,1)S(1)}, bf16[384,768]{1,0:T(8,128)(2,1)}, u32[]{:S(2)}, u32[]{:S(2)}) collective-permute-start(bf16[384,768]{1,0:T(8,128)(2,1)S(1)} %get-tuple-element.238), channel_id=1, source_target_pairs={{0,24},{4,28},{8,16},{12,20},{16,8},{20,12},{24,0},{28,4},{1,25},{... | collective-permute-start | bytes 1769480 | tf_op jit(solution)/shard_map/ppermute | solution.py:100
  214.4 38.8 %all-to-all-start.3 = ((bf16[4,128,768]{2,1,0:T(8,128)(2,1)}), bf16[4,128,768]{2,1,0:T(8,128)(2,1)S(1)}, u32[]{:S(2)}, u32[]{:S(2)}) async-start(bf16[4,128,768]{2,1,0:T(8,128)(2,1)} %bitcast.156), calls=%async_computation.3 | async-start | bytes 1572864 | tf_op jit(solution)/shard_map/all_to_all | solution.py:703
  223.1 31.7 %collective-permute-start.42 = (bf16[4,24,896]{2,1,0:T(8,128)(2,1)}, bf16[4,24,896]{2,1,0:T(8,128)(2,1)S(1)}, u32[]{:S(2)}, u32[]{:S(2)}) collective-permute-start(bf16[4,24,896]{2,1,0:T(8,128)(2,1)} %get-tuple-element.246), channel_id=1, source_target_pairs={{0,1},{1,0},{2,3},{3,2},{4,5},{5,4},{6,7},{7,6},{8,9},{9,8},{10,11... | collective-permute-start | bytes 516104 | tf_op jit(solution)/shard_map/ppermute | solution.py:100
  224.9 30.0 %collective-permute-start.43 = (bf16[4,24,896]{2,1,0:T(8,128)(2,1)}, bf16[4,24,896]{2,1,0:T(8,128)(2,1)}, u32[]{:S(2)}, u32[]{:S(2)}) collective-permute-start(bf16[4,24,896]{2,1,0:T(8,128)(2,1)} %get-tuple-element.248), channel_id=1, source_target_pairs={{0,2},{1,3},{2,0},{3,1},{4,6},{5,7},{6,4},{7,5},{8,10},{9,11},{10,... | collective-permute-start | bytes 516104 | tf_op jit(solution)/shard_map/ppermute | solution.py:100
  253.2 19.6 %collective-permute-start.30 = (bf16[1024,512]{1,0:T(8,128)(2,1)}, bf16[1024,512]{1,0:T(8,128)(2,1)}, u32[]{:S(2)}, u32[]{:S(2)}) collective-permute-start(bf16[1024,512]{1,0:T(8,128)(2,1)} %get-tuple-element.167), channel_id=1, source_target_pairs={{0,4},{4,0},{8,12},{12,8},{16,20},{20,16},{24,28},{28,24},{1,5},{5... | collective-permute-start | bytes 3145736 | tf_op jit(solution)/shard_map/ppermute | solution.py:100
  285.2 10.3 %collective-permute-start.31 = (bf16[256,768]{1,0:T(8,128)(2,1)}, bf16[256,768]{1,0:T(8,128)(2,1)S(1)}, u32[]{:S(2)}, u32[]{:S(2)}) collective-permute-start(bf16[256,768]{1,0:T(8,128)(2,1)} %get-tuple-element.172), channel_id=1, source_target_pairs={{0,8},{4,12},{8,0},{12,4},{16,24},{20,28},{24,16},{28,20},{1,9},{5... | collective-permute-start | bytes 1179656 | tf_op jit(solution)/shard_map/ppermute | solution.py:100
  286.2 13.2 %collective-permute-start.32 = (bf16[256,768]{1,0:T(8,128)(2,1)}, bf16[256,768]{1,0:T(8,128)(2,1)S(1)}, u32[]{:S(2)}, u32[]{:S(2)}) collective-permute-start(bf16[256,768]{1,0:T(8,128)(2,1)} %get-tuple-element.173), channel_id=1, source_target_pairs={{0,16},{4,20},{8,24},{12,28},{16,0},{20,4},{24,8},{28,12},{1,17},{... | collective-permute-start | bytes 1179656 | tf_op jit(solution)/shard_map/ppermute | solution.py:100
  287.2 12.2 %collective-permute-start.33 = (bf16[256,768]{1,0:T(8,128)(2,1)}, bf16[256,768]{1,0:T(8,128)(2,1)S(1)}, u32[]{:S(2)}, u32[]{:S(2)}) collective-permute-start(bf16[256,768]{1,0:T(8,128)(2,1)} %get-tuple-element.174), channel_id=1, source_target_pairs={{0,24},{4,28},{8,16},{12,20},{16,8},{20,12},{24,0},{28,4},{1,25},{... | collective-permute-start | bytes 1179656 | tf_op jit(solution)/shard_map/ppermute | solution.py:100
  292.2 19.1 %all-to-all-start.4 = ((f32[32,15,128]{2,1,0:T(8,128)}), f32[32,15,128]{2,1,0:T(8,128)}, u32[]{:S(2)}, u32[]{:S(2)}) async-start(f32[32,15,128]{2,1,0:T(8,128)} %broadcast_in_dim.51), calls=%async_computation.4 | async-start | bytes 524288 | tf_op jit(solution)/shard_map/all_to_all | solution.py:926
  302.9 9.4 %collective-permute-start.35 = (bf16[4,24,576]{2,1,0:T(8,128)(2,1)}, bf16[4,24,576]{2,1,0:T(8,128)(2,1)S(1)}, u32[]{:S(2)}, u32[]{:S(2)}) collective-permute-start(bf16[4,24,576]{2,1,0:T(8,128)(2,1)} %get-tuple-element.249), channel_id=1, source_target_pairs={{0,1},{1,0},{2,3},{3,2},{4,5},{5,4},{6,7},{7,6},{8,9},{9,8},{10,11... | collective-permute-start | bytes 331784 | tf_op jit(solution)/shard_map/ppermute | solution.py:100
  303.1 9.5 %collective-permute-start.36 = (bf16[4,24,576]{2,1,0:T(8,128)(2,1)}, bf16[4,24,576]{2,1,0:T(8,128)(2,1)}, u32[]{:S(2)}, u32[]{:S(2)}) collective-permute-start(bf16[4,24,576]{2,1,0:T(8,128)(2,1)} %get-tuple-element.251), channel_id=1, source_target_pairs={{0,2},{1,3},{2,0},{3,1},{4,6},{5,7},{6,4},{7,5},{8,10},{9,11},{10,... | collective-permute-start | bytes 331784 | tf_op jit(solution)/shard_map/ppermute | solution.py:100
  (51 other events, 420.5 us)
where the time goes:
time: 325 us; the launch traced here: 326 us
  Pallas kernels  115 us (35%)
  starting transfers between devices  73.5 us (23%)
  waiting for transfers between devices  70.5 us (22%)
  blocking collectives  25.4 us (8%)
  other arithmetic  20.9 us (6%)
  local copies, waits for them, and re-layouts  16.6 us (5%)
    pallas_call x10, Pallas kernels, kernel_call(): pl.pallas_call(kernel, out_shape=tuple((jax.ShapeDtypeStruct(shape, kind)...  84.8 us
    ppermute x48, waiting for transfers between devices, swap(): return lax.ppermute(value, axis, [(i, i ^ mask) for i in range(size)])  63 us
    ppermute x48, starting transfers between devices, swap(): return lax.ppermute(value, axis, [(i, i ^ mask) for i in range(size)])  58.3 us
    pallas_call x1, Pallas kernels, expert_layer(): pl.pallas_call(functools.partial(expert_kernel, experts=experts, groups=g...  30.1 us
    all_to_all x1, blocking collectives, turn_batch(): lax.all_to_all(rows, 'batch', split_axis=0, concat_axis=0, tiled=True)  25.4 us
    all_to_all x3, starting transfers between devices, turn_batch(): lax.all_to_all(rows, 'batch', split_axis=0, concat_axis=0, tiled=True)  11.8 us
    all_to_all x3, waiting for transfers between devices, turn_batch(): lax.all_to_all(rows, 'batch', split_axis=0, concat_axis=0, tiled=True)  7.52 us
    unnamed x69, local copies, waits for them, and re-layouts  7.22 us
  transfers between devices with their start and end apart: 52, of which 21 were waited for; matrix products, arithmetic and copies ran while one was open for 10% of the time, Pallas kernels for 20%

commit v1 on v0

v1 whole, which is shorter than its diff:
```python
import functools
import math

import jax
import jax.numpy as jnp
import numpy as np
from jax import lax
from jax.experimental import pallas as pl
from jax.experimental.pallas import tpu as pltpu
from jax.sharding import PartitionSpec as P

BUCKETS = 32
MAX_DIST = 128
EPSILON = 1e-06
MASKED = -1e30
F32 = jnp.float32
BF16 = jnp.bfloat16


def bucket_limits():
    half_span = BUCKETS // 2
    exact_span = half_span // 2
    log_levels = half_span - exact_span
    limits = []
    for level_at in range(1, log_levels):
        bound_row = exact_span
        while (
            bound_row**log_levels * exact_span**level_at
            < MAX_DIST**level_at * exact_span**log_levels
        ):
            bound_row = bound_row + 1
        limits.append(bound_row)
    return limits


def relative_bucket(offsets):
    half_span = BUCKETS // 2
    exact_span = half_span // 2
    distance = np.abs(offsets)
    far = np.full(distance.shape, exact_span, np.int32)
    for bound_row in bucket_limits():
        far = far + (distance >= bound_row).astype(np.int32)
    near = np.where(distance < exact_span, distance, far)
    return near + np.where(offsets > 0, half_span, 0)


def band_buckets(block):
    column = np.arange(2 * block)
    rows = []
    for d in range(5):
        if d in (0, 4):
            offsets = np.full((2 * block,), (d - 2) * max(block, MAX_DIST), np.int64)
        else:
            offsets = (d - 2) * block + block - column
        rows.append(relative_bucket(offsets))
    return np.stack(rows)


def band_onehot(block):
    return band_buckets(block)[:, None, :] == np.arange(BUCKETS)[None, :, None]


def dot(a, b, dims, precision=None):
    return lax.dot_general(a, b, (dims, ((), ())), preferred_element_type=F32, precision=precision)


NN = ((1,), (0,))
NT = ((1,), (1,))
TN = ((0,), (0,))


def xor_order(parts, index):
    parts = list(parts)
    step = 1
    while step < len(parts):
        odd = (index // step) % 2 == 1
        parts = [jnp.where(odd, parts[i ^ step], parts[i]) for i in range(len(parts))]
        step = step * 2
    return parts


def vmem(count):
    return [pl.BlockSpec(memory_space=pltpu.VMEM)] * count


def place(ring):
    ctx = lax.axis_index("ctx").astype(jnp.int32)
    return ctx // ring, ctx % ring, lax.axis_index("batch").astype(jnp.int32)


def kernel_call(kernel, name, arrays, out_shape, scratch=()):
    return pl.pallas_call(
        kernel,
        out_shape=tuple(jax.ShapeDtypeStruct(shape, kind) for shape, kind in out_shape),
        in_specs=vmem(len(arrays)),
        out_specs=vmem(len(out_shape)),
        scratch_shapes=[
            pltpu.SMEM(shape, kind) if kind == jnp.int32 else pltpu.VMEM(shape, kind)
            for shape, kind in scratch
        ],
        compiler_params=pltpu.CompilerParams(vmem_limit_bytes=56 << 20),
        name=name,
    )(*arrays)


def swap(value, axis, size, mask):
    return lax.ppermute(value, axis, [(i, i ^ mask) for i in range(size)])


def column(row, size):
    return jnp.broadcast_to(row, (size, row.shape[1])).T


def first_kernel(tokens_ref, seg_ref, gain_ref, row_ref, message_ref, *cut_refs, part, ring):
    info = place(ring)
    tokens = tokens_ref[...].astype(F32)
    per, width = tokens.shape
    scale = lax.rsqrt(jnp.mean(tokens * tokens, axis=1, keepdims=True) + EPSILON)
    message_ref[:per, :] = (tokens * scale * gain_ref[...].astype(F32)[None, :]).astype(BF16)
    message_ref[per:, :] = jnp.zeros((message_ref.shape[0] - per, width), BF16)
    message_ref[per:, :per] = jnp.broadcast_to(
        seg_ref[...].astype(F32), (message_ref.shape[0] - per, per)
    ).astype(BF16)
    rows = row_ref[...].astype(F32)
    groups = len(cut_refs)
    cuts = [
        jnp.concatenate(
            [rows[:, k * width + g * part : k * width + (g + 1) * part] for k in range(3)], axis=1
        )
        for g in range(groups)
    ]
    for ref, cut in zip(cut_refs, xor_order(cuts, info[0])):
        ref[...] = cut.astype(BF16)


def row_place(info, g, r, z, ring, batch):
    return ((g ^ info[0]) * ring + (r ^ info[1])) * batch + (z ^ info[2])


def assemble(info, piece_refs, dest_ref, groups, batch, tall):
    ring = len(piece_refs)
    for r in range(ring):
        for z in range(batch):
            for g in range(groups):
                block = row_place(info, g, r, z, ring, batch)
                at = (z * groups + g) * tall
                dest_ref[pl.ds(pl.multiple_of(block * tall, 8), tall), :] = piece_refs[r][
                    at : at + tall, :
                ].astype(F32)


def project_kernel(*refs, groups, ring, batch, tall, part, per, pieces):
    x_refs, refs = refs[:groups], refs[groups:]
    w_refs, refs = refs[:pieces], refs[pieces:]
    q_ref, kv_ref, w_out, w_s = refs
    wide = 256
    if tall % 8 == 0:
        assemble(place(ring), w_refs, w_s, groups, batch, tall)
    else:
        w_s[...] = w_refs[0][...].astype(F32)
    gap = jnp.zeros((w_s.shape[0], wide - part), BF16)
    w = jnp.concatenate(
        [x for k in range(3) for x in (w_s[:, k * part : (k + 1) * part].astype(BF16), gap)],
        axis=1,
    )
    w_out[...] = w
    kv_ref[groups * per :, :] = jnp.zeros((kv_ref.shape[0] - groups * per, 2 * wide), BF16)
    seg = jnp.concatenate([x_ref[per : per + 1, :wide].astype(F32) for x_ref in x_refs], axis=0)
    seg = jnp.concatenate(
        [seg, jnp.zeros((kv_ref.shape[0] - groups * per - groups, wide), F32)], axis=0
    )
    kv_ref[groups * per :, :wide] = seg.astype(BF16)
    for m in range(groups):
        packed = dot(x_refs[m][:per, :], w_out[...], NN).astype(BF16)
        q_ref[m * per : (m + 1) * per, :] = packed[:, :wide]
        kv_ref[m * per : (m + 1) * per, :] = packed[:, wide:]


def slot_row(route, capacity):
    per = route.shape[1]
    earlier = lax.broadcasted_iota(jnp.int32, (per, per), 0) < lax.broadcasted_iota(
        jnp.int32, (per, per), 1
    )
    same = jnp.where((column(route, per) == route) & earlier, 1.0, 0.0)
    return route * capacity + jnp.sum(same, axis=0, keepdims=True)


def dispatch_kernel(route_ref, dz_ref, pick_ref, pick_t_ref, sent_ref, *, capacity):
    target = slot_row(route_ref[...].astype(F32), capacity).astype(jnp.int32)
    slots, per = pick_ref.shape
    slot = lax.broadcasted_iota(jnp.int32, (slots, per), 0)
    pick = jnp.where(slot == target, 1.0, 0.0)
    pick_ref[...] = pick.astype(BF16)
    pick_t_ref[...] = pick.T.astype(BF16)
    sent_ref[...] = dot(pick.astype(BF16), dz_ref[...], NN).astype(BF16)


def middle_kernel(*refs, groups, ring, batch, tall, part, capacity, pieces):
    info = place(ring)
    mixed_refs, refs = refs[:groups], refs[groups:]
    w_refs, refs = refs[:pieces], refs[pieces:]
    tokens_ref, gain_ref, pick_ref, route_ref, w_ref, middle_ref, gate_ref = refs[:7]
    sent_refs, w_s = refs[7:-1], refs[-1]
    width = tokens_ref.shape[1]
    if tall % 8 == 0:
        assemble(info, w_refs, w_s, groups, batch, tall)
    else:
        w_s[...] = w_refs[0][...].astype(F32)
    w_ref[...] = w_s[...].astype(BF16)
    middle = tokens_ref[...].astype(F32)
    for m in range(groups):
        start = pl.multiple_of((info[0] ^ m) * part, 16)
        middle += dot(mixed_refs[m][...], w_ref[pl.ds(start, part), :width], NN)
    middle_ref[...] = middle
    scale = lax.rsqrt(jnp.mean(middle * middle, axis=1, keepdims=True) + EPSILON)
    normed = (middle * scale * gain_ref[...].astype(F32)[None, :]).astype(BF16)
    for m, ref in enumerate(sent_refs):
        start = pl.multiple_of((info[2] ^ m) * capacity, capacity)
        ref[...] = dot(pick_ref[pl.ds(start, capacity), :], normed, NN).astype(BF16)
    logits = dot(normed, w_ref[:, width:], NN)
    lane = lax.broadcasted_iota(jnp.int32, logits.shape, 1)
    logits = jnp.where(lane < batch, logits, MASKED)
    expo = jnp.exp(logits - jnp.max(logits, axis=1, keepdims=True))
    probs = expo / jnp.sum(expo, axis=1, keepdims=True)
    route = column(route_ref[...].astype(F32), logits.shape[1]).astype(jnp.int32)
    gate_ref[...] = jnp.sum(jnp.where(lane == route, probs, 0.0), axis=1, keepdims=True)


def branch_kernel(back_ref, *refs, groups, ring, batch, tall, part):
    info = place(ring)
    mixed_refs, refs = refs[:groups], refs[groups:]
    pick_t_ref, middle_ref, dz_ref, gain_ref, w_ref, rpart_ref = refs[:6]
    d_middle_ref, gain_part_ref = refs[6:8]
    d_mixed_refs, grad_refs = refs[8 : 8 + groups], refs[8 + groups :]
    width = middle_ref.shape[1]
    d_normed = dot(pick_t_ref[...], back_ref[...], NN)
    middle = middle_ref[...]
    scale = lax.rsqrt(jnp.mean(middle * middle, axis=1, keepdims=True) + EPSILON)
    gain_part_ref[...] = jnp.sum(d_normed * middle * scale, axis=0, keepdims=True)
    scaled = gain_ref[...].astype(F32)[None, :] * d_normed
    d_middle = (
        dz_ref[...].astype(F32)
        + scale * scaled
        - middle
        * (scale * scale * scale)
        * jnp.mean(scaled * middle, axis=1, keepdims=True)
    )
    d_middle_ref[...] = d_middle
    d_branch = d_middle.astype(BF16)
    for m in range(groups):
        start = pl.multiple_of((info[0] ^ m) * part, 16)
        d_mixed_refs[m][...] = dot(d_branch, w_ref[pl.ds(start, part), :width], NT).astype(BF16)
    for m in range(groups):
        start = pl.multiple_of((info[0] ^ m) * part, 16)
        grad = dot(mixed_refs[m][...], d_branch, TN)
        grad = jnp.concatenate([grad, rpart_ref[pl.ds(start, part), :]], axis=1)
        if tall % 8 == 0:
            scatter_rows(info, grad, m, grad_refs, ring, batch, tall)
        else:
            grad_refs[0][pl.ds(start, part), :] = grad


def scatter_rows(info, grad, g, grad_refs, ring, batch, tall):
    for z in range(batch):
        rows = [
            grad[(r * batch + z) * tall : (r * batch + z + 1) * tall, :] for r in range(ring)
        ]
        for ref, row in zip(grad_refs, xor_order(rows, info[1])):
            ref[z ^ info[2], g] = row.astype(ref.dtype)


def weight_kernel(dq_ref, *refs, groups, ring, batch, tall, part, per):
    info = place(ring)
    got_refs, refs = refs[:ring], refs[ring:]
    x_refs, dp_ref, grad_refs, x_s = refs[:groups], refs[groups], refs[groups + 1 : -1], refs[-1]
    wide = 256
    for m in range(groups):
        rows = slice(m * per, (m + 1) * per)
        dkv = got_refs[0][rows, :]
        for ref in got_refs[1:]:
            dkv += ref[rows, :].astype(F32)
        dp_ref[rows, :wide] = dq_ref[rows, :]
        dp_ref[rows, wide:] = dkv.astype(BF16)
        x_s[rows, :] = x_refs[m][:per, :]
    share = ring * batch * tall
    for g in range(groups):
        grad = dot(x_s[:, g * share : (g + 1) * share], dp_ref[...], TN)
        grad = jnp.concatenate([grad[:, k * wide : k * wide + part] for k in range(3)], axis=1)
        if tall % 8 == 0:
            scatter_rows(info, grad, g ^ info[0], grad_refs, ring, batch, tall)
        else:
            grad_refs[0][g * share : (g + 1) * share, :] = grad


def unproject_kernel(
    dp_ref, w_ref, gain_ref, gain2_ref, table_ref, *refs, per, ring, heads, groups
):
    x_refs, d_refs, late_ref = refs[:groups], refs[groups : 2 * groups], refs[-1]
    width = gain2_ref.shape[1]
    total = jnp.zeros((1, width), F32)
    for m, ref in enumerate(d_refs):
        rows = slice(m * per, (m + 1) * per)
        d_normed = dot(dp_ref[rows, :], w_ref[...], NT)
        ref[...] = d_normed.astype(ref.dtype)
        total += jnp.sum(d_normed * x_refs[m][:per, :].astype(F32), axis=0, keepdims=True)
    total = total / gain_ref[...].astype(F32)[None, :]
    late_ref[0] = jnp.zeros(late_ref.shape[1:], F32)
    count = width // 128
    for k in range(count):
        late_ref[0, k : k + 1, :] = total[:, k * 128 : (k + 1) * 128]
        late_ref[0, count + k : count + k + 1, :] = gain2_ref[:, k * 128 : (k + 1) * 128]
    group = place(ring)[0]
    for h in range(heads):
        late_ref[0, pl.ds(2 * count + group * heads + h, 1), :] = table_ref[h : h + 1, :]
    whole = late_ref[0]

    @pl.loop(1, late_ref.shape[0])
    def _(k):
        late_ref[k] = whole


def late_kernel(got_ref, gain1_ref, gain2_ref, table_ref):
    total = jnp.sum(got_ref[...], axis=0)
    count, heads = gain1_ref.shape[0], table_ref.shape[0]
    gain1_ref[...] = total[:count, :]
    gain2_ref[...] = total[count : 2 * count, :]
    table_ref[...] = total[2 * count : 2 * count + heads, :]


def half_kernel(*refs, ring):
    total = refs[0][...]
    for ref in refs[1:ring]:
        total += ref[...].astype(F32)
    for m, ref in enumerate(refs[ring:]):
        ref[...] = total[m].astype(ref.dtype)


def quarter_kernel(*refs, batch):
    one, two = refs[0][...], refs[batch][...]
    for ref in refs[1:batch]:
        one += ref[...].astype(F32)
    for ref in refs[batch + 1 : 2 * batch]:
        two += ref[...].astype(F32)
    cut = one.shape[2]
    for m, ref in enumerate(refs[2 * batch :]):
        ref[:, :cut] = one[m].astype(BF16)
        ref[:, cut:] = two[m].astype(BF16)


def columns_kernel(*refs, groups, ring, part):
    qkv_ref, out_ref, router_ref = refs[groups:]
    cut, width = 3 * part, out_ref.shape[1]
    parts = xor_order([ref[:, :cut].astype(F32) for ref in refs[:groups]], place(ring)[0])
    qkv_ref[...] = jnp.concatenate(
        [p[:, k * part : (k + 1) * part] for k in range(3) for p in parts], axis=1
    )
    total = sum(ref[:, cut:].astype(F32) for ref in refs[:groups])
    out_ref[...] = total[:, :width]
    router_ref[...] = total[:, width:]


def tokens_kernel(*refs, groups):
    tokens_ref, gain_ref, d_middle_ref, out_ref = refs[groups:]
    d_normed = refs[0][...]
    for ref in refs[1:groups]:
        d_normed += ref[...].astype(F32)
    tokens = tokens_ref[...].astype(F32)
    scale = lax.rsqrt(jnp.mean(tokens * tokens, axis=1, keepdims=True) + EPSILON)
    scaled = gain_ref[...].astype(F32)[None, :] * d_normed
    out_ref[...] = (
        d_middle_ref[...]
        + scale * scaled
        - tokens
        * (scale * scale * scale)
        * jnp.mean(scaled * tokens, axis=1, keepdims=True)
    ).astype(BF16)


def combine_kernel(got_ref, pick_t_ref, middle_ref, gate_ref, out_ref):
    returned = dot(pick_t_ref[...], got_ref[...], NN)
    out_ref[...] = (middle_ref[...] + gate_ref[...] * returned).astype(BF16)


def merge_kernel(*refs, groups, ring):
    g1_refs, g2_refs, one_ref = refs[:ring], refs[ring : 2 * ring], refs[2 * ring]
    g1 = sum(ref[...].astype(F32) for ref in g1_refs)
    g2 = sum(ref[...].astype(F32) for ref in g2_refs)
    rows, more = g1.shape[0], one_ref.shape[0] - g1.shape[0]
    one_ref[:rows, :] = g1.astype(BF16)
    one_ref[rows:, :] = g2[:more, :].astype(BF16)
    for m, ref in enumerate(refs[2 * ring + 1 :]):

        @pl.when((pl.program_id(0) ^ place(ring)[0]) == m)
        def _():
            ref[...] = g2[more:, :].astype(BF16)


def merge(g1, g2, more):
    groups, rows, width = g1[0].shape
    ring = len(g1)
    left = g2[0].shape[1] - more
    outs = pl.pallas_call(
        functools.partial(merge_kernel, groups=groups, ring=ring),
        grid=(groups,),
        out_shape=(jax.ShapeDtypeStruct((groups, rows + more, width), BF16),)
        + (jax.ShapeDtypeStruct((left, width), BF16),) * groups,
        in_specs=[pl.BlockSpec((None, rows, width), lambda g: (g, 0, 0))] * ring
        + [pl.BlockSpec((None, left + more, width), lambda g: (g, 0, 0))] * ring,
        out_specs=[pl.BlockSpec((None, rows + more, width), lambda g: (g, 0, 0))]
        + [pl.BlockSpec((left, width), lambda g: (0, 0))] * groups,
        compiler_params=pltpu.CompilerParams(
            dimension_semantics=("arbitrary",), vmem_limit_bytes=56 << 20
        ),
        name="merge",
    )(*g1, *g2)
    return outs[0], list(outs[1:])


def finish_kernel(one_ref, *refs):
    two_refs, in_ref, out_ref = refs[:-2], *refs[-2:]
    one = jnp.sum(one_ref[...].astype(F32), axis=0)
    tall, width = in_ref.shape[0], out_ref.shape[1]
    tiles = in_ref.shape[1] // width
    for j in range(tiles):
        in_ref[:, j * width : (j + 1) * width] = one[j * tall : (j + 1) * tall, :]
    more = one.shape[0] - tiles * tall
    out_ref[:more, :] = one[tiles * tall :, :]
    out_ref[more:, :] = sum(ref[...].astype(F32) for ref in two_refs)


SEGMENTS = 8


def set_bias(band_ref, bias_s, heads, block):
    @pl.loop(0, heads)
    def _(h):
        @pl.loop(0, 5)
        def _(d):
            row = jnp.broadcast_to(band_ref[h, pl.ds(d, 1), :], (block, 2 * block))
            bias_s[h, d] = pltpu.roll(row, block, 1, stride=1, stride_axis=0)[:, :block]


def key_at(kb, info, ring, groups):
    return ((kb % ring) ^ info[1]) * groups + ((kb // ring) ^ info[0])


def set_spans(info, kv_refs, seg_s, span_s, groups, ring, block):
    rows = [ref[groups * block : groups * block + groups, :block].astype(F32) for ref in kv_refs]
    seg = jnp.concatenate(rows, axis=0)
    seg_s[...] = seg
    blocks = groups * ring
    low, high = seg[:, 0:1], seg[:, block - 1 : block]
    at = lax.broadcasted_iota(jnp.int32, (blocks, 1), 0)
    natural = (((at % groups) ^ info[0]) * ring + ((at // groups) ^ info[1])).astype(F32)
    for i in range(groups):
        meets = (low <= high[i : i + 1, :]) & (high >= low[i : i + 1, :])
        first = jnp.min(jnp.where(meets, natural, float(blocks)))
        last = jnp.max(jnp.where(meets, natural, -1.0))
        span_s[i, 0] = first.astype(jnp.int32)
        span_s[i, 1] = last.astype(jnp.int32) + 1


def with_extras(pair, half, extras):
    lane = lax.broadcasted_iota(jnp.int32, pair.shape, 1)
    kept = jnp.where(lane // 64 == half, pair, 0.0)
    spot = lane - (1 - half) * 64
    for at, extra in extras:
        if at is None:
            kept = jnp.where((spot >= 0) & (spot < SEGMENTS), extra(spot), kept)
        else:
            kept = jnp.where(spot == at, extra, kept)
    return kept


def key_extras(seg_col):
    return (None, lambda spot: jnp.where(spot.astype(F32) == seg_col, 0.0, MASKED))


def query_extras(seg_col):
    return (None, lambda spot: jnp.where(spot.astype(F32) == seg_col, 1.0, 0.0))


def three_parts(value):
    high = value.astype(BF16).astype(F32)
    middle = (value - high).astype(BF16).astype(F32)
    return high, middle, value - high - middle


def set_keys(kv_refs, seg_s, heads, groups, block, ones, key_s, turned_s, turn, value_s=None):
    wide = 256
    for r, ref in enumerate(kv_refs):

        @pl.loop(0, groups)
        def _(g):
            at, rows = r * groups + g, pl.ds(pl.multiple_of(g * block, block), block)
            seg_col = column(seg_s[pl.ds(at, 1), :], 128)
            turned_s[at] = ref[rows, turn : turn + wide].astype(F32).T.astype(BF16)
            for h in range(heads):
                lane = (h // 2) * 128
                extras = [key_extras(seg_col)] + [(SEGMENTS + n, 1.0) for n in range(ones)]
                key = with_extras(ref[rows, lane : lane + 128].astype(F32), h % 2, extras)
                key_s[at, h] = key.astype(BF16)
                if value_s is not None:
                    lane = wide + lane
                    extras = [(n, 1.0) for n in range(ones)]
                    value = with_extras(ref[rows, lane : lane + 128].astype(F32), h % 2, extras)
                    value_s[at, h] = value.astype(BF16)


def attend_kernel(q_ref, *refs, heads, groups, ring, block):
    info = place(ring)
    kv_refs, refs = refs[:ring], refs[ring:]
    band_ref, ot_ref, lse_ref = refs[:3]
    mixed_refs, refs = refs[3 : 3 + groups], refs[3 + groups :]
    bias_s, seg_s, span_s, key_s, vt_s, query_s, stat_s, acc_s = refs
    set_bias(band_ref, bias_s, heads, block)
    set_spans(info, kv_refs, seg_s, span_s, groups, ring, block)
    set_keys(kv_refs, seg_s, heads, groups, block, 0, key_s, vt_s, 256)

    @pl.loop(0, groups)
    def _(i):
        qb = (i ^ info[0]) * ring + info[1]
        rows = pl.ds(pl.multiple_of(i * block, block), block)
        seg_col = column(seg_s[pl.ds(i, 1), :], 128)
        for h in range(heads):
            lane = (h // 2) * 128
            query = q_ref[rows, lane : lane + 128].astype(F32) * 0.125
            query_s[h] = with_extras(query, h % 2, [query_extras(seg_col)]).astype(BF16)
        stat_s[0:heads] = jnp.full((heads, 1, block), MASKED, F32)
        stat_s[heads : 2 * heads] = jnp.zeros((heads, 1, block), F32)
        acc_s[...] = jnp.zeros_like(acc_s)

        @pl.loop(span_s[i, 0], span_s[i, 1])
        def _(kb):
            at = key_at(kb, info, ring, groups)
            d = jnp.clip(kb - qb, -2, 2) + 2
            scores = [dot(key_s[at, h], query_s[h], NT) + bias_s[h, d] for h in range(heads)]
            tops = [
                jnp.maximum(stat_s[h], jnp.max(scores[h], axis=0, keepdims=True))
                for h in range(heads)
            ]
            expos = [jnp.exp(scores[h] - tops[h]) for h in range(heads)]
            for h in range(heads):
                decay = jnp.exp(stat_s[h] - tops[h])
                stat_s[h] = tops[h]
                stat_s[heads + h] = stat_s[heads + h] * decay + jnp.sum(
                    expos[h], axis=0, keepdims=True
                )
                value_t = vt_s[at, h * 64 : (h + 1) * 64, :]
                acc_s[h] = acc_s[h] * decay + dot(value_t, expos[h].astype(BF16), NN)

        for h in range(heads):
            total = stat_s[heads + h]
            ot_ref[i, h * 64 : (h + 1) * 64, :] = acc_s[h] / total
            lse_ref[i, h : h + 1, :] = stat_s[h] + jnp.log(total)

    for i in range(groups):
        mixed_refs[i][...] = ot_ref[i].T.astype(BF16)


def attend(q, kv_all, band, heads, groups, ring, block):
    width = heads * 64
    return kernel_call(
        functools.partial(attend_kernel, heads=heads, groups=groups, ring=ring, block=block),
        "attend",
        [q, *kv_all, band],
        [((groups, width, block), F32), ((groups, 8, block), F32)]
        + [((block, width), BF16)] * groups,
        [
            ((heads, 5, block, block), F32),
            ((groups * ring, block), F32),
            ((groups, 2), jnp.int32),
            ((groups * ring, heads, block, 128), BF16),
            ((groups * ring, 256, block), BF16),
            ((heads, block, 128), BF16),
            ((2 * heads, 1, block), F32),
            ((heads, 64, block), F32),
        ],
    )


def attend_back_kernel(q_ref, *refs, heads, groups, ring, block):
    info = place(ring)
    kv_refs, refs = refs[:ring], refs[ring:]
    band_ref, refs = refs[0], refs[1:]
    dmix_refs, refs = refs[:groups], refs[groups:]
    ot_ref, lse_ref, dq_ref, own_ref = refs[:4]
    other_refs, refs = refs[4 : 3 + ring], refs[3 + ring :]
    dband_ref, bias_s, seg_s, span_s, key_s, value_s, kt_s, query_s, plain_s, dout_s = refs[:10]
    dplain_s, dqt_s, dkv_s, dbias_s, dmix_s = refs[10:]
    wide = 256
    blocks = groups * ring
    set_bias(band_ref, bias_s, heads, block)
    set_spans(info, kv_refs, seg_s, span_s, groups, ring, block)
    set_keys(kv_refs, seg_s, heads, groups, block, 3, key_s, kt_s, 0, value_s)
    for i in range(groups):
        dmix_s[i, :, : heads * 64] = dmix_refs[i][...].astype(F32)
        dmix_s[i, :, heads * 64 :] = jnp.zeros((block, wide - heads * 64), F32)

    @pl.loop(0, blocks)
    def _(at):
        dkv_s[at] = jnp.zeros(dkv_s.shape[1:], F32)

    @pl.loop(0, heads)
    def _(h):
        dbias_s[h] = jnp.zeros(dbias_s.shape[1:], F32)

    @pl.loop(0, groups)
    def _(i):
        qb = (i ^ info[0]) * ring + info[1]
        rows = pl.ds(pl.multiple_of(i * block, block), block)
        seg_col = column(seg_s[pl.ds(i, 1), :], 128)
        dmix = dmix_s[i]
        dmix_t = dmix.T
        for h in range(heads):
            cut, lane = slice(h * 64, (h + 1) * 64), (h // 2) * 128
            delta = jnp.sum(dmix_t[cut, :] * ot_ref[i, cut, :], axis=0, keepdims=True)
            delta = three_parts(column(-delta, 128))
            lse = three_parts(column(-lse_ref[i, h : h + 1, :], 128))
            query = q_ref[rows, lane : lane + 128].astype(F32) * 0.125
            extras = [query_extras(seg_col)] + [(SEGMENTS + n, lse[n]) for n in range(3)]
            query_s[h] = with_extras(query, h % 2, extras).astype(BF16)
            plain_s[h] = with_extras(query, h % 2, []).astype(BF16)
            d_out = dmix[:, lane : lane + 128]
            extras = [(n, delta[n]) for n in range(3)]
            dout_s[h] = with_extras(d_out, h % 2, extras).astype(BF16)
            dplain_s[h] = with_extras(d_out, h % 2, []).astype(BF16)
        dqt_s[...] = jnp.zeros_like(dqt_s)

        @pl.loop(span_s[i, 0], span_s[i, 1])
        def _(kb):
            at = key_at(kb, info, ring, groups)
            d = jnp.clip(kb - qb, -2, 2) + 2
            softs = [
                jnp.exp(dot(key_s[at, h], query_s[h], NT) + bias_s[h, d]) for h in range(heads)
            ]
            d_scores = [
                (softs[h] * dot(value_s[at, h], dout_s[h], NT)).astype(BF16) for h in range(heads)
            ]
            for h in range(heads):
                lane = (h // 2) * 128
                dkv_s[at, :, wide + lane : wide + lane + 128] += dot(
                    softs[h].astype(BF16), dplain_s[h], NN
                )
                dkv_s[at, :, lane : lane + 128] += dot(d_scores[h], plain_s[h], NN)
                dqt_s[h * 64 : (h + 1) * 64, :] += dot(
                    kt_s[at, h * 64 : (h + 1) * 64, :], d_scores[h], NN
                )
                dbias_s[h, d] += d_scores[h].astype(F32)

        pad = jnp.zeros((wide - heads * 64, block), F32)
        dq_ref[rows, :] = (jnp.concatenate([dqt_s[...], pad], axis=0) * 0.125).T.astype(BF16)

    for r in range(ring):

        @pl.loop(0, groups)
        def _(g):
            at, rows = r * groups + g, pl.ds(pl.multiple_of(g * block, block), block)
            if r == 0:
                own_ref[rows, :] = dkv_s[at]
            else:
                other_refs[r - 1][rows, :] = dkv_s[at].astype(BF16)

    buckets = band_buckets(block)
    zero = jnp.zeros((block, block), F32)
    lane = lax.broadcasted_iota(jnp.int32, (1, 128), 1)
    column_at = lax.broadcasted_iota(jnp.int32, (1, 2 * block), 1)
    dband_ref[...] = jnp.zeros_like(dband_ref)

    @pl.loop(0, heads)
    def _(h):
        table = jnp.zeros((1, 128), F32)
        for d in range(5):
            if d in (0, 4):
                tile = jnp.sum(dbias_s[h, d], axis=0, keepdims=True)
                tile = jnp.concatenate([tile, zero[:1]], axis=1)
            else:
                tile = jnp.concatenate([zero, dbias_s[h, d]], axis=1)
                tall = block
                while tall > 1:
                    tall = tall // 2
                    tile = tile[:tall] + pltpu.roll(tile[tall:], 2 * block - tall, 1)
            for bucket in sorted(set(buckets[d].tolist())):
                held = np.nonzero(buckets[d] == bucket)[0]
                keep = (column_at >= int(held[0])) & (column_at <= int(held[-1]))
                held_sum = jnp.sum(jnp.where(keep, tile, 0.0), axis=1, keepdims=True)
                table += jnp.where(lane == bucket, held_sum, 0.0)
        dband_ref[pl.ds(h, 1), :] = table


def attend_back(q, kv_all, band, d_mix, out_t, lse, heads, groups, ring, block):
    own = groups * block
    blocks = groups * ring
    return kernel_call(
        functools.partial(attend_back_kernel, heads=heads, groups=groups, ring=ring, block=block),
        "attend_back",
        [q, *kv_all, band, *d_mix, out_t, lse],
        [((own, 256), BF16), ((own, 512), F32)]
        + [((own, 512), BF16)] * (ring - 1)
        + [((8, 128), F32)],
        [((heads, 5, block, block), F32), ((blocks, block), F32), ((groups, 2), jnp.int32)]
        + [((blocks, heads, block, 128), BF16)] * 2
        + [((blocks, 256, block), BF16)]
        + [((heads, block, 128), BF16)] * 4
        + [
            ((heads * 64, block), F32),
            ((blocks, block, 512), F32),
            ((heads, 5, block, block), F32),
            ((groups, block, 256), F32),
        ],
    )


def expert_kernel(*refs, experts, ring, batch):
    info = place(ring)
    piece_refs, refs = refs[:batch], refs[batch:]
    dz_ref, router_ref, w1_ref, w2_ref = refs[:4]
    prod_ref, back_ref, rpart_ref, rows_t, dret_ref, hidden_ref, d_pre_ref = refs[4:11]
    rows_ref, prob_s, prod_s, back_s = refs[11:]
    capacity = piece_refs[0].shape[0]
    step = pl.program_id(0)
    me = info[2]
    lane = lax.broadcasted_iota(jnp.int32, prob_s.shape, 1)

    @pl.when(step == 0)
    def _():
        for m, ref in enumerate(piece_refs):
            start = pl.multiple_of((me ^ m) * capacity, capacity)
            rows_ref[pl.ds(start, capacity), :] = ref[...]
        rows = rows_ref[...]
        rows_t[...] = rows.astype(F32).T.astype(BF16)
        logits = dot(rows, router_ref[...], NN)
        logits = jnp.where(lane < experts, logits, MASKED)
        expo = jnp.exp(logits - jnp.max(logits, axis=1, keepdims=True))
        probs = expo / jnp.sum(expo, axis=1, keepdims=True)
        prob_s[...] = probs
        gate = jnp.sum(jnp.where(lane == me, probs, 0.0), axis=1, keepdims=True)
        dret_ref[...] = (gate * dz_ref[...].astype(F32)).astype(BF16)
        prod_s[...] = jnp.zeros_like(prod_s)
        back_s[...] = jnp.zeros_like(back_s)

    w1 = w1_ref[...]
    w2 = w2_ref[...]
    pre = dot(rows_ref[...], w1, NN)
    cumulative = 0.5 * (1.0 + lax.erf(pre * (1.0 / math.sqrt(2.0))))
    density = jnp.exp(-0.5 * pre * pre) * (1.0 / math.sqrt(2.0 * math.pi))
    hidden = (pre * cumulative).astype(BF16)
    d_hidden = dot(dret_ref[...], w2, NT)
    d_pre = (d_hidden * (cumulative + pre * density)).astype(BF16)
    hidden_ref[...] = hidden
    d_pre_ref[...] = d_pre
    prod_s[...] += dot(hidden, w2, NN)
    back_s[...] += dot(d_pre, w1, NT)

    @pl.when(step == pl.num_programs(0) - 1)
    def _():
        probs = prob_s[...]
        gate = jnp.sum(jnp.where(lane == me, probs, 0.0), axis=1, keepdims=True)
        chosen = jnp.where(lane == me, 1.0, 0.0)
        produced = prod_s[...].astype(BF16)
        prod_ref[...] = produced
        d_gate = jnp.sum(
            dz_ref[...].astype(F32) * produced.astype(F32), axis=1, keepdims=True
        )
        d_logits = (d_gate * probs * (chosen - gate)).astype(BF16)
        back = back_s[...].astype(BF16).astype(F32) + dot(d_logits, router_ref[...], NT)
        back_ref[...] = back.astype(BF16)
        rpart_ref[...] = dot(rows_t[...], d_logits, NN)


def expert_layer(pieces, dz, w_both, w1, w2, ring):
    batch = len(pieces)
    capacity, width = pieces[0].shape
    slots = batch * capacity
    lanes = 128
    hidden = w1.shape[1]
    cut = width
    fixed = lambda j: (0, 0)
    whole = pl.BlockSpec((slots, width), fixed)
    return pl.pallas_call(
        functools.partial(expert_kernel, experts=batch, ring=ring, batch=batch),
        grid=(hidden // cut,),
        in_specs=[pl.BlockSpec((capacity, width), fixed)] * batch
        + [
            whole,
            pl.BlockSpec((width, lanes), lambda j: (0, width // lanes)),
            pl.BlockSpec((width, cut), lambda j: (0, j)),
            pl.BlockSpec((cut, width), lambda j: (j, 0)),
        ],
        out_specs=[
            whole,
            whole,
            pl.BlockSpec((width, lanes), fixed),
            pl.BlockSpec((width, slots), fixed),
            whole,
            pl.BlockSpec((slots, cut), lambda j: (0, j)),
            pl.BlockSpec((slots, cut), lambda j: (0, j)),
        ],
        scratch_shapes=[
            pltpu.VMEM((slots, width), BF16),
            pltpu.VMEM((slots, lanes), F32),
            pltpu.VMEM((slots, width), F32),
            pltpu.VMEM((slots, width), F32),
        ],
        out_shape=(
            jax.ShapeDtypeStruct((slots, width), BF16),
            jax.ShapeDtypeStruct((slots, width), BF16),
            jax.ShapeDtypeStruct((width, lanes), F32),
            jax.ShapeDtypeStruct((width, slots), BF16),
            jax.ShapeDtypeStruct((slots, width), BF16),
            jax.ShapeDtypeStruct((slots, hidden), BF16),
            jax.ShapeDtypeStruct((slots, hidden), BF16),
        ),
        compiler_params=pltpu.CompilerParams(
            dimension_semantics=("arbitrary",), vmem_limit_bytes=56 << 20
        ),
        name="experts",
    )(*pieces, dz, w_both, w1, w2)


def expert_grad_kernel(rows_t, dret_ref, hidden_ref, d_pre_ref, *refs, groups, ring):
    info = place(ring)
    g1_refs, g2_refs = refs[:ring], refs[ring:]
    g2 = dot(hidden_ref[...], dret_ref[...], TN).astype(BF16)
    share = g2.shape[0] // ring
    parts = [g2[c * share : (c + 1) * share, :] for c in range(ring)]
    for ref, rows in zip(g2_refs, xor_order(parts, info[1])):
        ref[...] = rows
    g1 = dot(rows_t[...], d_pre_ref[...], NN).astype(BF16)
    tall = g1.shape[0] // (groups * ring)
    for g in range(groups):
        parts = [
            g1[(g * ring + c) * tall : (g * ring + c + 1) * tall, :] for c in range(ring)
        ]
        for ref, rows in zip(g1_refs, xor_order(parts, info[1])):
            ref[g] = rows


def expert_grads(rows_t, d_ret, hidden, d_pre, groups, ring):
    width, slots = rows_t.shape
    devices = groups * ring
    share = hidden.shape[1] // devices
    cut = share * ring
    tall = width // devices
    tiles = hidden.shape[1] // cut
    return pl.pallas_call(
        functools.partial(expert_grad_kernel, groups=groups, ring=ring),
        grid=(tiles,),
        in_specs=[
            pl.BlockSpec((width, slots), lambda j: (0, 0)),
            pl.BlockSpec((slots, width), lambda j: (0, 0)),
            pl.BlockSpec((slots, cut), lambda j: (0, j)),
            pl.BlockSpec((slots, cut), lambda j: (0, j)),
        ],
        out_specs=[pl.BlockSpec((groups, tall, cut), lambda j: (0, j, 0))] * ring
        + [pl.BlockSpec((None, share, width), lambda j: (j, 0, 0))] * ring,
        out_shape=(jax.ShapeDtypeStruct((groups, tiles * tall, cut), BF16),) * ring
        + (jax.ShapeDtypeStruct((groups, share, width), BF16),) * ring,
        compiler_params=pltpu.CompilerParams(
            dimension_semantics=("arbitrary",), vmem_limit_bytes=56 << 20
        ),
        name="expert_grads",
    )(rows_t, d_ret, hidden, d_pre)


def body(
    tokens,
    seg_ids,
    routes,
    attn_gain,
    query_key_value_weight,
    attention_output_weight,
    bias_table,
    ffn_gain,
    router_weight,
    expert_in,
    expert_out,
    out_grad,
):
    n_ctx = lax.axis_size("ctx")
    n_batch = lax.axis_size("batch")
    per, width = tokens.shape[1:]
    head_count = bias_table.shape[1]
    groups = math.gcd(head_count, n_ctx)
    ring = n_ctx // groups
    heads = head_count // groups
    part = heads * 64
    tall = query_key_value_weight.shape[0]
    lanes = 128
    wide = 256
    rows_own = groups * per
    capacity = max(2, 2 * per // n_batch)
    slots = n_batch * capacity
    fine = tall % 8 == 0
    ctx = lax.axis_index("ctx").astype(jnp.int32)
    zed = lax.axis_index("batch").astype(jnp.int32)
    group, own = ctx // ring, ctx % ring

    def over_groups(parts):
        return [
            parts[m] if m == 0 else swap(parts[m], "ctx", n_ctx, ring * m) for m in range(groups)
        ]

    def over_ring(parts):
        return [parts[m] if m == 0 else swap(parts[m], "ctx", n_ctx, m) for m in range(ring)]

    def over_batch(parts):
        return [
            parts[m] if m == 0 else swap(parts[m], "batch", n_batch, m) for m in range(n_batch)
        ]

    def turn_batch(rows):
        rows = rows.reshape(n_batch, capacity, width)
        rows = lax.all_to_all(rows, "batch", split_axis=0, concat_axis=0, tiled=True)
        return rows.reshape(slots, width)

    def natural(pieces, columns):
        pieces = [p.reshape(n_batch, groups, tall, columns) for p in pieces]
        pieces = xor_order(pieces, own)
        pieces = [xor_order([c[z] for z in range(n_batch)], zed) for c in pieces]
        pieces = [[xor_order([b[g] for g in range(groups)], group) for b in c] for c in pieces]
        order = [(g, r, z) for g in range(groups) for r in range(ring) for z in range(n_batch)]
        return [jnp.concatenate([pieces[r][z][g] for g, r, z in order], axis=0)]

    first = kernel_call(
        functools.partial(first_kernel, part=part, ring=ring),
        "first",
        [tokens[0], seg_ids, attn_gain, query_key_value_weight],
        [((per + 16, width), BF16)] + [((tall, 3 * part), BF16)] * groups,
    )
    message, cuts = first[0], list(first[1:])
    cuts = over_groups(cuts)
    message, cuts = lax.optimization_barrier((message, cuts))
    arrived = over_groups([message] * groups)
    both = jnp.concatenate(
        [attention_output_weight, jnp.pad(router_weight, ((0, 0), (0, lanes - n_batch)))], axis=1
    )
    cuts = jnp.concatenate(cuts, axis=0)
    step = 1
    while step < n_batch:
        cuts = jnp.concatenate([cuts, swap(cuts, "batch", n_batch, step)], axis=0)
        cuts, both = lax.optimization_barrier((cuts, both)) if step == 1 else (cuts, both)
        step = step * 2
    both = jnp.concatenate([both, swap(both, "batch", n_batch, 1)], axis=0)

    route_row = routes.reshape(1, per)
    d_result = out_grad[0]
    pick, pick_t, dz_sent = kernel_call(
        functools.partial(dispatch_kernel, capacity=capacity),
        "dispatch",
        [route_row, d_result],
        [((slots, per), BF16), ((per, slots), BF16), ((slots, width), BF16)],
    )
    table = sum(
        jnp.where(group == g, bias_table[:, g * heads : (g + 1) * heads], 0) for g in range(groups)
    )
    band = jnp.einsum(
        "dbc,bh->hdc",
        jnp.asarray(band_onehot(per), BF16),
        table,
        preferred_element_type=F32,
    )
    band = jnp.pad(band, ((0, 0), (0, 3), (0, 0)))
    arrived, cuts, dz_sent, band, both = lax.optimization_barrier(
        (arrived, cuts, dz_sent, band, both)
    )
    cuts = over_ring([cuts] * ring)
    step = 2
    while step < n_batch:
        both = jnp.concatenate([both, swap(both, "batch", n_batch, step)], axis=0)
        step = step * 2
    dz_there = turn_batch(dz_sent)
    if not fine:
        cuts = natural(cuts, 3 * part)
    kv_rows = rows_own + 16
    q, kv_own, w_head = kernel_call(
        functools.partial(
            project_kernel,
            groups=groups,
            ring=ring,
            batch=n_batch,
            tall=tall,
            part=part,
            per=per,
            pieces=len(cuts),
        ),
        "project",
        [*arrived, *cuts],
        [
            ((rows_own, wide), BF16),
            ((kv_rows, 2 * wide), BF16),
            ((width, 3 * wide), BF16),
        ],
        [((width, 3 * part), F32)],
    )
    kv_own, both = lax.optimization_barrier((kv_own, both))
    kv_all = over_ring([kv_own] * ring)
    both = over_groups([both] * groups)

    out_t, lse, *mixed = attend(q, kv_all, band, heads, groups, ring, per)

    mixed, dz_there, both = lax.optimization_barrier((mixed, dz_there, both))
    both = jnp.stack([b.reshape(n_batch, tall, width + lanes) for b in both], axis=1)
    both = over_ring([both.reshape(n_batch * groups * tall, width + lanes)] * ring)
    if not fine:
        both = natural(both, width + lanes)
    mixed = over_groups(mixed)
    both, middle, gate, *rows_sent = kernel_call(
        functools.partial(
            middle_kernel,
            groups=groups,
            ring=ring,
            batch=n_batch,
            tall=tall,
            part=part,
            capacity=capacity,
            pieces=len(both),
        ),
        "middle",
        [*mixed, *both, tokens[0], ffn_gain, pick, route_row],
        [((width, width + lanes), BF16), ((per, width), F32), ((per, 1), F32)]
        + [((capacity, width), BF16)] * n_batch,
        [((width, width + lanes), F32)],
    )
    rows_there = over_batch(rows_sent)
    produced, back, router_part, *saved = expert_layer(
        rows_there, dz_there, both, expert_in[0], expert_out[0], ring
    )
    back = turn_batch(back)
    grads = expert_grads(*saved, groups, ring)
    g1, g2 = grads[:ring], grads[ring:]

    def turn_groups(grads):
        sets = [[g * ring + r for g in range(groups)] for r in range(ring)]
        return lax.all_to_all(
            grads, "ctx", split_axis=0, concat_axis=0, tiled=True, axis_index_groups=sets
        )

    back, g1, g2 = lax.optimization_barrier((back, g1, g2))
    g1, g2 = over_ring(g1), over_ring(g2)
    grads_one, grads_two = merge(g1, g2, g2[0].shape[1] // 4)
    sums_shape = (n_batch, groups, tall, width + lanes)
    sums_shape = (
        [(sums_shape, F32)] + [(sums_shape, BF16)] * (ring - 1)
        if fine
        else [((width, width + lanes), F32)]
    )
    d_middle, ffn_gain_part, *rest = kernel_call(
        functools.partial(
            branch_kernel,
            groups=groups,
            ring=ring,
            batch=n_batch,
            tall=tall,
            part=part,
        ),
        "branch",
        [back, *mixed, pick_t, middle, d_result, ffn_gain, both, router_part],
        [((per, width), F32), ((1, width), F32)] + [((per, part), BF16)] * groups + sums_shape,
    )
    d_mix, out_parts = rest[:groups], rest[groups:]

    def by_place(parts):
        if fine:
            return parts
        grad = parts[0].reshape(groups, ring, n_batch, tall, parts[0].shape[1])
        parts = xor_order([grad[:, r] for r in range(ring)], own)
        parts = [xor_order([p[:, z] for z in range(n_batch)], zed) for p in parts]
        parts = [[xor_order([z[g] for g in range(groups)], group) for z in p] for p in parts]
        parts = [jnp.stack([jnp.stack(z) for z in p]) for p in parts]
        return [parts[0]] + [p.astype(BF16) for p in parts[1:]]

    d_mix = over_groups(d_mix)
    out_parts = over_ring(by_place(out_parts))
    d_mix, grads_one, grads_two, out_parts = lax.optimization_barrier(
        (d_mix, grads_one, grads_two, out_parts)
    )
    shape = out_parts[0].shape[1:]
    out_parts = kernel_call(
        functools.partial(half_kernel, ring=ring),
        "half_out",
        out_parts,
        [(shape, F32)] + [(shape, BF16)] * (n_batch - 1),
    )
    out_parts = over_batch(out_parts)
    grads_one = turn_groups(grads_one)

    dq, dkv_own, *rest = attend_back(
        q, kv_all, band, d_mix, out_t, lse, heads, groups, ring, per
    )
    dkv_other, table_part = rest[: ring - 1], rest[ring - 1]
    dkv_other, grads_one, grads_two, out_parts, produced = lax.optimization_barrier(
        (dkv_other, grads_one, grads_two, out_parts, produced)
    )
    dkv_got = over_ring([dkv_own] + dkv_other)[1:]
    returned = turn_batch(produced)

    grads_shape = (
        [((n_batch, groups, tall, 3 * part), F32)]
        + [((n_batch, groups, tall, 3 * part), BF16)] * (ring - 1)
        if fine
        else [((width, 3 * part), F32)]
    )
    d_packed, *packed_parts = kernel_call(
        functools.partial(
            weight_kernel,
            groups=groups,
            ring=ring,
            batch=n_batch,
            tall=tall,
            part=part,
            per=per,
        ),
        "weight",
        [dq, dkv_own, *dkv_got, *arrived],
        [((rows_own, 3 * wide), BF16)] + grads_shape,
        [((rows_own, width), BF16)],
    )
    late_rows = -(-(2 * width // lanes + head_count) // 8) * 8
    *d_normed, late = kernel_call(
        functools.partial(unproject_kernel, per=per, ring=ring, heads=heads, groups=groups),
        "unproject",
        [d_packed, w_head, attn_gain, ffn_gain_part, table_part, *arrived],
        [((per, width), F32)]
        + [((per, width), BF16)] * (groups - 1)
        + [((n_ctx * n_batch, late_rows, lanes), F32)],
    )
    packed_parts = over_ring(by_place(packed_parts))
    packed_parts, d_normed = lax.optimization_barrier((packed_parts, d_normed))
    got = over_groups(d_normed)
    shape = packed_parts[0].shape[1:]
    packed_parts = kernel_call(
        functools.partial(half_kernel, ring=ring),
        "half_packed",
        packed_parts,
        [(shape, F32)] + [(shape, BF16)] * (n_batch - 1),
    )
    grads_two, got[1] = lax.optimization_barrier((grads_two, got[1]))
    grads_two = over_groups(grads_two)
    late, returned = lax.optimization_barrier((late, returned))
    packed_parts = over_batch(packed_parts)
    layer_out = kernel_call(
        combine_kernel,
        "combine",
        [returned, pick_t, middle, gate],
        [((per, width), BF16)],
    )[0][None]
    tokens_grad = kernel_call(
        functools.partial(tokens_kernel, groups=groups),
        "tokens",
        [*got, tokens[0], attn_gain, d_middle],
        [((per, width), BF16)],
    )[0][None]
    packed_parts, layer_out, tokens_grad = lax.optimization_barrier(
        (packed_parts, layer_out, tokens_grad)
    )
    parts = kernel_call(
        functools.partial(quarter_kernel, batch=n_batch),
        "quarter",
        [*packed_parts, *out_parts],
        [((tall, 3 * part + width + lanes), BF16)] * groups,
    )

    expert_in_grad, expert_out_grad = kernel_call(
        finish_kernel,
        "finish",
        [grads_one, *grads_two],
        [
            ((width // n_ctx, expert_in.shape[2]), F32),
            ((expert_out.shape[1] // n_ctx, width), F32),
        ],
    )

    late = lax.all_to_all(late, ("ctx", "batch"), split_axis=0, concat_axis=0, tiled=True)
    attn_gain_grad, ffn_gain_grad, d_table = kernel_call(
        late_kernel,
        "late",
        [late],
        [((width // lanes, lanes), F32)] * 2 + [((head_count, lanes), F32)],
    )
    attn_gain_grad = attn_gain_grad.reshape(width)
    ffn_gain_grad = ffn_gain_grad.reshape(width)
    bias_grad = d_table[:, : bias_table.shape[0]].T
    qkv_grad, out_weight_grad, router_grad = kernel_call(
        functools.partial(columns_kernel, groups=groups, ring=ring, part=part),
        "columns",
        over_groups(parts),
        [((tall, 3 * width), F32), ((tall, width), F32), ((tall, lanes), F32)],
    )
    router_grad = router_grad[:, :n_batch]
    return (
        layer_out,
        tokens_grad,
        attn_gain_grad,
        qkv_grad,
        out_weight_grad,
        bias_grad,
        ffn_gain_grad,
        router_grad,
        expert_in_grad[None],
        expert_out_grad[None],
    )


def solution(mesh):
    return jax.shard_map(
        body,
        mesh=mesh,
        in_specs=(
            P("batch", "ctx", None),
            P("batch", "ctx"),
            P("ctx", "batch", None, None),
            P(),
            P(("ctx", "batch"), None),
            P(("ctx", "batch"), None),
            P(),
            P(),
            P(("ctx", "batch"), None),
            P("batch", None, None),
            P("batch", None, None),
            P("batch", "ctx", None),
        ),
        out_specs=(
            P("batch", "ctx", None),
            P("batch", "ctx", None),
            P(),
            P(("ctx", "batch"), None),
            P(("ctx", "batch"), None),
            P(),
            P(),
            P(("ctx", "batch"), None),
            P("batch", "ctx", None),
            P("batch", "ctx", None),
        ),
        check_vma=False,
    )
```

time: 325 us -> 288 us (0.89)
  blocking collectives: 25.4 us -> 0 us
  other arithmetic: 20.9 us -> 1.72 us
  Pallas kernels: 115 us -> 126 us
    all_to_all x1 -> x0, blocking collectives: 25.4 us -> none  [turn_batch(): lax.all_to_all(rows, 'batch', split_axis=0, concat_axis=0, tiled=True)]
    ppermute x48 -> x45, waiting for transfers between devices: 63 us -> 49.4 us  [swap(): return lax.ppermute(value, axis, [(i, i ^ mask) for i in range(size)])]
    all_to_all x3, waiting for transfers between devices: 7.52 us -> 18.1 us  [turn_batch(): lax.all_to_all(rows, 'batch', split_axis=0, concat_axis=0, tiled=True)]
    pallas_call x10 -> x17, Pallas kernels: 84.8 us -> 92.2 us  [kernel_call(): pl.pallas_call(kernel, out_shape=tuple((jax.ShapeDtypeStruct(shape, kind)...]
    broadcast_in_dim x4 -> x0, other arithmetic: 6.67 us -> none  [the longest x2 5.54 us: group_sum(): return sum((g.astype(F32) for g in got))[None]]
    another operation x6 -> x1, other arithmetic: 5.76 us -> 0.11 us  [body(): jnp.stack([b.reshape(n_batch, tall, width + lanes) for b in both], axis=1)]
    convert_element_type x4 -> x0, other arithmetic: 5.47 us -> none  [the longest x2 4.77 us: ring_sum(): return sum((g.astype(F32) for g in over_ring(grads))).astype(BF16)]
    ppermute x48 -> x45, starting transfers between devices: 58.3 us -> 53.5 us  [swap(): return lax.ppermute(value, axis, [(i, i ^ mask) for i in range(size)])]
  transfers between devices with their start and end apart: 52 -> 50, of which waited for: 21 -> 16; matrix products, arithmetic and copies ran while one was open for 10% -> 3% of each run, Pallas kernels for 20% -> 34%
where the time goes in v1:
time: 288 us; the launch traced here: 287 us
  Pallas kernels  126 us (44%)
  starting transfers between devices  72.6 us (25%)
  waiting for transfers between devices  70.1 us (24%)
  local copies, waits for them, and re-layouts  13.9 us (5%)
    pallas_call x17, Pallas kernels, kernel_call(): pl.pallas_call(kernel, out_shape=tuple((jax.ShapeDtypeStruct(shape, kind)...  92.2 us
    ppermute x45, starting transfers between devices, swap(): return lax.ppermute(value, axis, [(i, i ^ mask) for i in range(size)])  53.5 us
    ppermute x45, waiting for transfers between devices, swap(): return lax.ppermute(value, axis, [(i, i ^ mask) for i in range(size)])  49.4 us
    all_to_all x3, waiting for transfers between devices, turn_batch(): lax.all_to_all(rows, 'batch', split_axis=0, concat_axis=0, tiled=True)  18.1 us
    pallas_call x1, Pallas kernels, expert_layer(): pl.pallas_call(functools.partial(expert_kernel, experts=batch, ring=ring,...  17.1 us
    all_to_all x3, starting transfers between devices, turn_batch(): lax.all_to_all(rows, 'batch', split_axis=0, concat_axis=0, tiled=True)  12.4 us
    unnamed x84, local copies, waits for them, and re-layouts  11.9 us
    pallas_call x1, Pallas kernels, expert_grads(): pl.pallas_call(functools.partial(expert_grad_kernel, groups=groups, ring=...  10 us
  transfers between devices with their start and end apart: 50, of which 16 were waited for; matrix products, arithmetic and copies ran while one was open for 3% of the time, Pallas kernels for 34%

profile of v1, /device:TPU:0, one launch (start us, length us, event | category | flops | bytes accessed | tf_op | source)
XLA Modules:
  0.0 286.7 jit_solution(2595404015531022214)
XLA Ops:
  2.6 2.9 %collective-permute-start = (bf16[24,576]{1,0:T(8,128)(2,1)}, bf16[24,576]{1,0:T(8,128)(2,1)S(1)}, u32[]{:S(2)}, u32[]{:S(2)}) collective-permute-start(bf16[24,576]{1,0:T(8,128)(2,1)} %get-tuple-element.164), channel_id=1, source_target_pairs={{0,8},{4,12},{8,0},{12,4},{16,24},{20,28},{24,16},{28,20},{1,9},{5... | collective-permute-start | bytes 82952 | tf_op jit(solution)/shard_map/ppermute | solution.py:107
  18.8 3.7 %collective-permute-done.6 = bf16[96,576]{1,0:T(8,128)(2,1)S(1)} collective-permute-done((bf16[96,576]{1,0:T(8,128)(2,1)S(1)}, bf16[96,576]{1,0:T(8,128)(2,1)S(1)}, u32[]{:S(2)}, u32[]{:S(2)}) %collective-permute-start.6) | collective-permute-done | bytes 110624 | tf_op jit(solution)/shard_map/ppermute | solution.py:107
  24.2 3.7 %collective-permute-start.7 = (bf16[192,576]{1,0:T(8,128)(2,1)S(1)}, bf16[192,576]{1,0:T(8,128)(2,1)S(1)}, u32[]{:S(2)}, u32[]{:S(2)}) collective-permute-start(bf16[192,576]{1,0:T(8,128)(2,1)S(1)} %constant_dynamic-update-slice_fusion), channel_id=1, source_target_pairs={{0,2},{1,3},{2,0},{3,1},{4,6},{5,7},{6,4},{7,5},{8,10},{9,11},{10,... | collective-permute-start | bytes 663560 | tf_op jit(solution)/shard_map/ppermute | solution.py:107
  35.3 3.9 %all-to-all-start = ((bf16[4,128,768]{2,1,0:T(8,128)(2,1)}), bf16[4,128,768]{2,1,0:T(8,128)(2,1)S(1)}, u32[]{:S(2)}, u32[]{:S(2)}) async-start(bf16[4,128,768]{2,1,0:T(8,128)(2,1)} %bitcast.49), calls=%async_computation | async-start | bytes 1572864 | tf_op jit(solution)/shard_map/all_to_all | solution.py:914
  39.2 3.1 %collective-permute-done.10 = bf16[48,896]{1,0:T(8,128)(2,1)S(1)} collective-permute-done((bf16[48,896]{1,0:T(8,128)(2,1)S(1)}, bf16[48,896]{1,0:T(8,128)(2,1)S(1)}, u32[]{:S(2)}, u32[]{:S(2)}) %collective-permute-start.10) | collective-permute-done | bytes 86048 | tf_op jit(solution)/shard_map/ppermute | solution.py:107
  43.2 4.6 %project.1 = (bf16[1024,256]{1,0:T(8,128)(2,1)}, bf16[1040,512]{1,0:T(8,128)(2,1)}, bf16[768,768]{1,0:T(8,128)(2,1)}) custom-call(bf16[272,768]{1,0:T(8,128)(2,1)} %get-tuple-element.175.refs_0_.refs_2_, bf16[272,768]{1,0:T(8,128)(2,1)} %copy-done.4, bf16[272,768]{1,0:T(8,128)(2,1)} %copy-done.3, bf16[272,768]{1,0:T(8,128)(2,1)} %copy-done.2, ...), custom_call_target="tpu_custom_call" | custom-call | tf_op jit(solution)/shard_map/project/pallas_call | solution.py:92
  52.4 17.3 %attend.1 = (f32[4,192,256]{2,1,0:T(8,128)}, f32[4,8,256]{2,1,0:T(8,128)}, bf16[256,192]{1,0:T(8,128)(2,1)}, bf16[256,192]{1,0:T(8,128)(2,1)}, bf16[256,192]{1,0:T(8,128)(2,1)}, /*index=5*/bf16[256,192]{1,0:T(8,128)(2,1)}) custom-call(bf16[1024,256]{1,0:T(8,128)(2,1)} %get-tuple-element.180.q_ref, bf16[1040,512]{1,0:T(8,128)(2,1)} %get-tuple-element.183.refs_0_, ...), custom_call_target="tpu_custom_call" | custom-call | tf_op jit(solution)/shard_map/attend/pallas_call | solution.py:92
  73.5 3.0 %collective-permute-done.15.refs_1_ = bf16[256,192]{1,0:T(8,128)(2,1)S(1)} collective-permute-done((bf16[256,192]{1,0:T(8,128)(2,1)}, bf16[256,192]{1,0:T(8,128)(2,1)S(1)}, u32[]{:S(2)}, u32[]{:S(2)}) %collective-permute-start.15) | collective-permute-done | bytes 98336 | tf_op jit(solution)/shard_map/ppermute | solution.py:107
  76.5 2.6 collective-permute-done.16.refs_2_
  80.1 4.4 %middle.1 = (bf16[768,896]{1,0:T(8,128)(2,1)}, f32[256,768]{1,0:T(8,128)}, f32[256,1]{1,0:T(8,128)}, bf16[128,768]{1,0:T(8,128)(2,1)}, bf16[128,768]{1,0:T(8,128...) custom-call(bf16[256,192]{1,0:T(8,128)(2,1)} %get-tuple-element.191.refs_0_, bf16[256,192]{1,0:T(8,128)(2,1)} %copy-done.13, ...), custom_call_target="tpu_custom_call" | custom-call | tf_op jit(solution)/shard_map/middle/pallas_call | solution.py:92
  88.8 4.9 %collective-permute-done.19.refs_1_ = bf16[128,768]{1,0:T(8,128)(2,1)S(1)} collective-permute-done((bf16[128,768]{1,0:T(8,128)(2,1)}, bf16[128,768]{1,0:T(8,128)(2,1)S(1)}, u32[]{:S(2)}, u32[]{:S(2)}) %collective-permute-start.19) | collective-permute-done | bytes 196640 | tf_op jit(solution)/shard_map/ppermute | solution.py:107
  93.8 8.1 %collective-permute-done.20.refs_2_ = bf16[128,768]{1,0:T(8,128)(2,1)S(1)} collective-permute-done((bf16[128,768]{1,0:T(8,128)(2,1)}, bf16[128,768]{1,0:T(8,128)(2,1)S(1)}, u32[]{:S(2)}, u32[]{:S(2)}) %collective-permute-start.20) | collective-permute-done | bytes 196640 | tf_op jit(solution)/shard_map/ppermute | solution.py:107
  102.7 17.1 %experts.1 = (bf16[512,768]{1,0:T(8,128)(2,1)}, bf16[512,768]{1,0:T(8,128)(2,1)}, f32[768,128]{1,0:T(8,128)}, bf16[768,512]{1,0:T(8,128)(2,1)}, bf16[512,768]{1,...) custom-call(bf16[128,768]{1,0:T(8,128)(2,1)} %get-tuple-element.200.refs_0_, ...), custom_call_target="tpu_custom_call" | custom-call | tf_op jit(solution)/shard_map/experts/pallas_call | solution.py:780
  119.8 4.4 %all-to-all-start.1 = ((bf16[4,128,768]{2,1,0:T(8,128)(2,1)}), bf16[4,128,768]{2,1,0:T(8,128)(2,1)S(1)}, u32[]{:S(2)}, u32[]{:S(2)}) async-start(bf16[4,128,768]{2,1,0:T(8,128)(2,1)} %bitcast.50), calls=%async_computation.1 | async-start | bytes 1572864 | tf_op jit(solution)/shard_map/all_to_all | solution.py:914
  124.1 10.0 %expert_grads.1 = (bf16[4,384,768]{2,1,0:T(8,128)(2,1)}, bf16[4,384,768]{2,1,0:T(8,128)(2,1)}, bf16[4,384,768]{2,1,0:T(8,128)(2,1)}, bf16[4,384,768]{2,1,0:T(8,128)(2,1)}) custom-call(bf16[768,512]{1,0:T(8,128)(2,1)} %get-tuple-element.207.rows_t, bf16[512,768]{1,0:T(8,128)(2,1)} %get-tuple-element.208.dret_ref, ...), custom_call_target="tpu_custom_call" | custom-call | tf_op jit(solution)/shard_map/expert_grads/pallas_call | solution.py:846
  134.2 8.7 %all-to-all-done.1 = bf16[4,128,768]{2,1,0:T(8,128)(2,1)S(1)} async-done(((bf16[4,128,768]{2,1,0:T(8,128)(2,1)}), bf16[4,128,768]{2,1,0:T(8,128)(2,1)S(1)}, u32[]{:S(2)}, u32[]{:S(2)}) %all-to-all-start.1) | async-done | bytes 786464 | tf_op jit(solution)/shard_map/all_to_all | solution.py:914
  143.8 5.5 %branch.1 = (f32[256,768]{1,0:T(8,128)}, f32[1,768]{1,0:T(1,128)}, bf16[256,192]{1,0:T(8,128)(2,1)}, bf16[256,192]{1,0:T(8,128)(2,1)}, bf16[256,192]{1,0:T(8,128...) custom-call(bf16[512,768]{1,0:T(8,128)(2,1)} %bitcast.43, ...), custom_call_target="tpu_custom_call" | custom-call | tf_op jit(solution)/shard_map/branch/pallas_call | solution.py:92
  154.2 6.9 %merge.1 = (bf16[4,480,768]{2,1,0:T(8,128)(2,1)}, bf16[288,768]{1,0:T(8,128)(2,1)}, bf16[288,768]{1,0:T(8,128)(2,1)}, bf16[288,768]{1,0:T(8,128)(2,1)}, bf16[288,768]{1,0:T(8,128)(2,1)}) custom-call(bf16[4,384,768]{2,1,0:T(8,128)(2,1)} %get-tuple-element.223.refs_0_, bf16[4,384,768]{2,1,0:T(8,128)(2,1)} %copy-done.8, ...), custom_call_target="tpu_custom_call" | custom-call | tf_op jit(solution)/shard_map/merge/pallas_call | solution.py:402
  161.1 3.7 %all-to-all-start.2 = ((bf16[4,480,768]{2,1,0:T(8,128)(2,1)}), bf16[4,480,768]{2,1,0:T(8,128)(2,1)S(1)}, u32[]{:S(2)}, u32[]{:S(2)}) async-start(bf16[4,480,768]{2,1,0:T(8,128)(2,1)} %get-tuple-element.243), calls=%async_computation.2 | async-start | bytes 5898240 | tf_op jit(solution)/shard_map/all_to_all | solution.py:1035
  167.3 2.9 %collective-permute-start.29 = (bf16[4,24,896]{2,1,0:T(8,128)(2,1)}, bf16[4,24,896]{2,1,0:T(8,128)(2,1)S(1)}, u32[]{:S(2)}, u32[]{:S(2)}) collective-permute-start(bf16[4,24,896]{2,1,0:T(8,128)(2,1)} %get-tuple-element.252), channel_id=1, source_target_pairs={{0,2},{1,3},{2,0},{3,1},{4,6},{5,7},{6,4},{7,5},{8,10},{9,11},{10,... | collective-permute-start | bytes 516104 | tf_op jit(solution)/shard_map/ppermute | solution.py:107
  171.6 24.8 %attend_back.1 = (bf16[1024,256]{1,0:T(8,128)(2,1)}, f32[1024,512]{1,0:T(8,128)}, bf16[1024,512]{1,0:T(8,128)(2,1)}, f32[8,128]{1,0:T(8,128)}) custom-call(bf16[1024,256]{1,0:T(8,128)(2,1)} %get-tuple-element.180.q_ref, bf16[1040,512]{1,0:T(8,128)(2,1)} %get-tuple-element.183.refs_0_, bf16[1040,512]{1,0:T(8,128)(2,1)} %copy-done.1, ...), custom_call_target="tpu_custom_call" | custom-call | tf_op jit(solution)/shard_map/attend_back/pallas_call | solution.py:92
  199.2 4.2 %all-to-all-start.3 = ((bf16[4,128,768]{2,1,0:T(8,128)(2,1)}), bf16[4,128,768]{2,1,0:T(8,128)(2,1)}, u32[]{:S(2)}, u32[]{:S(2)}) async-start(bf16[4,128,768]{2,1,0:T(8,128)(2,1)} %bitcast.48), calls=%async_computation.3 | async-start | bytes 1572864 | tf_op jit(solution)/shard_map/all_to_all | solution.py:914
  203.4 5.8 %weight.1 = (bf16[1024,768]{1,0:T(8,128)(2,1)}, f32[4,4,24,576]{3,2,1,0:T(8,128)}, bf16[4,4,24,576]{3,2,1,0:T(8,128)(2,1)}) custom-call(bf16[1024,256]{1,0:T(8,128)(2,1)} %get-tuple-element.240.dq_ref, f32[1024,512]{1,0:T(8,128)} %get-tuple-element.241.refs_0_, bf16[1024,512]{1,0:T(8,128)(2,1)} %collective-permute-done.31.refs_1_, ...), custom_call_target="tpu_custom_call" | custom-call | tf_op jit(solution)/shard_map/weight/pallas_call | solution.py:92
  209.8 5.3 %unproject.1 = (f32[256,768]{1,0:T(8,128)}, bf16[256,768]{1,0:T(8,128)(2,1)}, bf16[256,768]{1,0:T(8,128)(2,1)}, bf16[256,768]{1,0:T(8,128)(2,1)}, f32[32,24,128]{2,1,0:T(8,128)}) custom-call(bf16[1024,768]{1,0:T(8,128)(2,1)} %get-tuple-element.258.dp_ref, bf16[768,768]{1,0:T(8,128)(2,1)} %get-tuple-element.259.w_ref, bf16[768]{0:T(1024)(128)(2,1)} %refs_5_.1, ...), custom_call_target="tpu_custom_call" | custom-call | tf_op jit(solution)/shard_map/unproject/pallas_call | solution.py:92
  215.1 9.4 %all-to-all-done.3 = bf16[4,128,768]{2,1,0:T(8,128)(2,1)} async-done(((bf16[4,128,768]{2,1,0:T(8,128)(2,1)}), bf16[4,128,768]{2,1,0:T(8,128)(2,1)}, u32[]{:S(2)}, u32[]{:S(2)}) %all-to-all-start.3) | async-done | bytes 786464 | tf_op jit(solution)/shard_map/all_to_all | solution.py:914
  224.5 2.9 %all-to-all-start.4 = ((f32[32,24,128]{2,1,0:T(8,128)}), f32[32,24,128]{2,1,0:T(8,128)S(1)}, u32[]{:S(2)}, u32[]{:S(2)}) async-start(f32[32,24,128]{2,1,0:T(8,128)} %get-tuple-element.288), calls=%async_computation.4 | async-start | bytes 786432 | tf_op jit(solution)/shard_map/all_to_all | solution.py:1174
  234.8 8.4 %collective-permute-done.36.refs_1_ = bf16[256,768]{1,0:T(8,128)(2,1)S(1)} collective-permute-done((bf16[256,768]{1,0:T(8,128)(2,1)}, bf16[256,768]{1,0:T(8,128)(2,1)S(1)}, u32[]{:S(2)}, u32[]{:S(2)}) %collective-permute-start.36) | collective-permute-done | bytes 393248 | tf_op jit(solution)/shard_map/ppermute | solution.py:107
  249.0 3.5 %collective-permute-done.38.refs_3_ = bf16[256,768]{1,0:T(8,128)(2,1)S(1)} collective-permute-done((bf16[256,768]{1,0:T(8,128)(2,1)}, bf16[256,768]{1,0:T(8,128)(2,1)S(1)}, u32[]{:S(2)}, u32[]{:S(2)}) %collective-permute-start.38) | collective-permute-done | bytes 393248 | tf_op jit(solution)/shard_map/ppermute | solution.py:107
  252.5 3.2 %collective-permute-start.35 = (bf16[4,24,576]{2,1,0:T(8,128)(2,1)}, bf16[4,24,576]{2,1,0:T(8,128)(2,1)S(1)}, u32[]{:S(2)}, u32[]{:S(2)}) collective-permute-start(bf16[4,24,576]{2,1,0:T(8,128)(2,1)} %get-tuple-element.271), channel_id=1, source_target_pairs={{0,3},{1,2},{2,1},{3,0},{4,7},{5,6},{6,5},{7,4},{8,11},{9,10},{10,... | collective-permute-start | bytes 331784 | tf_op jit(solution)/shard_map/ppermute | solution.py:107
  258.3 3.1 %tokens.1 = bf16[256,768]{1,0:T(8,128)(2,1)} custom-call(f32[256,768]{1,0:T(8,128)} %get-tuple-element.276.refs_0_, bf16[256,768]{1,0:T(8,128)(2,1)} %copy-done.21, bf16[256,768]{1,0:T(8,128)(2,1)} %copy-done.22, bf16[256,768]{1,0:T(8,128)(2,1)} %copy-done.23, bf16[256,768]{1,0:T(8,128)(2,1)} %bitcast.41, bf16[768]{0:T(1024)(128)(2,1)} %refs_5_.1, ...), custom_call_target="tpu_custom_call" | custom-call | tf_op jit(solution)/shard_map/tokens/pallas_call | solution.py:92
  268.4 3.3 %collective-permute-done.39.refs_1_ = bf16[24,1472]{1,0:T(8,128)(2,1)S(1)} collective-permute-done((bf16[24,1472]{1,0:T(8,128)(2,1)}, bf16[24,1472]{1,0:T(8,128)(2,1)S(1)}, u32[]{:S(2)}, u32[]{:S(2)}) %collective-permute-start.39) | collective-permute-done | bytes 70688 | tf_op jit(solution)/shard_map/ppermute | solution.py:107
  282.8 4.0 %finish.1 = (f32[96,3072]{1,0:T(8,128)}, f32[384,768]{1,0:T(8,128)}) custom-call(bf16[4,480,768]{2,1,0:T(8,128)(2,1)} %copy-done, bf16[288,768]{1,0:T(8,128)(2,1)} %get-tuple-element.308.refs_0_, bf16[288,768]{1,0:T(8,128)(2,1)} %copy-done.18, bf16[288,768]{1,0:T(8,128)(2,1)} %copy-done.19, bf16[288,768]{1,0:T(8,128)(2,1)} %copy-done.20), custom_call_target="tpu_custom_call" | custom-call | tf_op jit(solution)/shard_map/finish/pallas_call | solution.py:92
  (183 shorter events, 86.2 us)
Async XLA Ops:
  12.1 22.5 %collective-permute-start.5 = (bf16[272,768]{1,0:T(8,128)(2,1)}, bf16[272,768]{1,0:T(8,128)(2,1)S(1)}, u32[]{:S(2)}, u32[]{:S(2)}) collective-permute-start(bf16[272,768]{1,0:T(8,128)(2,1)} %get-tuple-element.175.refs_0_.refs_2_), channel_id=1, source_target_pairs={{0,24},{4,28},{8,16},{12,20},{16,8},{20,12},{24,0},{28,4},{1,25},{... | collective-permute-start | bytes 1253384 | tf_op jit(solution)/shard_map/ppermute | solution.py:107
  12.1 22.5 %collective-permute-start.4 = (bf16[272,768]{1,0:T(8,128)(2,1)}, bf16[272,768]{1,0:T(8,128)(2,1)S(1)}, u32[]{:S(2)}, u32[]{:S(2)}) collective-permute-start(bf16[272,768]{1,0:T(8,128)(2,1)} %get-tuple-element.175.refs_0_.refs_2_), channel_id=1, source_target_pairs={{0,16},{4,20},{8,24},{12,28},{16,0},{20,4},{24,8},{28,12},{1,17},{... | collective-permute-start | bytes 1253384 | tf_op jit(solution)/shard_map/ppermute | solution.py:107
  14.1 20.6 %collective-permute-start.3 = (bf16[272,768]{1,0:T(8,128)(2,1)}, bf16[272,768]{1,0:T(8,128)(2,1)S(1)}, u32[]{:S(2)}, u32[]{:S(2)}) collective-permute-start(bf16[272,768]{1,0:T(8,128)(2,1)} %get-tuple-element.175.refs_0_.refs_2_), channel_id=1, source_target_pairs={{0,8},{4,12},{8,0},{12,4},{16,24},{20,28},{24,16},{28,20},{1,9},{5... | collective-permute-start | bytes 1253384 | tf_op jit(solution)/shard_map/ppermute | solution.py:107
  24.2 10.4 %collective-permute-start.7 = (bf16[192,576]{1,0:T(8,128)(2,1)S(1)}, bf16[192,576]{1,0:T(8,128)(2,1)S(1)}, u32[]{:S(2)}, u32[]{:S(2)}) collective-permute-start(bf16[192,576]{1,0:T(8,128)(2,1)S(1)} %constant_dynamic-update-slice_fusion), channel_id=1, source_target_pairs={{0,2},{1,3},{2,0},{3,1},{4,6},{5,7},{6,4},{7,5},{8,10},{9,11},{10,... | collective-permute-start | bytes 663560 | tf_op jit(solution)/shard_map/ppermute | solution.py:107
  35.3 34.4 %all-to-all-start = ((bf16[4,128,768]{2,1,0:T(8,128)(2,1)}), bf16[4,128,768]{2,1,0:T(8,128)(2,1)S(1)}, u32[]{:S(2)}, u32[]{:S(2)}) async-start(bf16[4,128,768]{2,1,0:T(8,128)(2,1)} %bitcast.49), calls=%async_computation | async-start | bytes 1572864 | tf_op jit(solution)/shard_map/all_to_all | solution.py:914
  47.9 21.8 %collective-permute-start.14 = (bf16[96,896]{1,0:T(8,128)(2,1)S(1)}, bf16[96,896]{1,0:T(8,128)(2,1)S(1)}, u32[]{:S(2)}, u32[]{:S(2)}) collective-permute-start(bf16[96,896]{1,0:T(8,128)(2,1)S(1)} %pad_maximum_fusion.2), channel_id=1, source_target_pairs={{0,24},{4,28},{8,16},{12,20},{16,8},{20,12},{24,0},{28,4},{1,25},{... | collective-permute-start | bytes 516104 | tf_op jit(solution)/shard_map/ppermute | solution.py:107
  48.4 21.3 %collective-permute-start.13 = (bf16[96,896]{1,0:T(8,128)(2,1)S(1)}, bf16[96,896]{1,0:T(8,128)(2,1)S(1)}, u32[]{:S(2)}, u32[]{:S(2)}) collective-permute-start(bf16[96,896]{1,0:T(8,128)(2,1)S(1)} %pad_maximum_fusion.2), channel_id=1, source_target_pairs={{0,16},{4,20},{8,24},{12,28},{16,0},{20,4},{24,8},{28,12},{1,17},{... | collective-permute-start | bytes 516104 | tf_op jit(solution)/shard_map/ppermute | solution.py:107
  49.9 19.8 %collective-permute-start.12 = (bf16[96,896]{1,0:T(8,128)(2,1)S(1)}, bf16[96,896]{1,0:T(8,128)(2,1)S(1)}, u32[]{:S(2)}, u32[]{:S(2)}) collective-permute-start(bf16[96,896]{1,0:T(8,128)(2,1)S(1)} %pad_maximum_fusion.2), channel_id=1, source_target_pairs={{0,8},{4,12},{8,0},{12,4},{16,24},{20,28},{24,16},{28,20},{1,9},{5... | collective-permute-start | bytes 516104 | tf_op jit(solution)/shard_map/ppermute | solution.py:107
  84.5 17.4 %collective-permute-start.20 = (bf16[128,768]{1,0:T(8,128)(2,1)}, bf16[128,768]{1,0:T(8,128)(2,1)S(1)}, u32[]{:S(2)}, u32[]{:S(2)}) collective-permute-start(bf16[128,768]{1,0:T(8,128)(2,1)} %get-tuple-element.202), channel_id=1, source_target_pairs={{0,2},{1,3},{2,0},{3,1},{4,6},{5,7},{6,4},{7,5},{8,10},{9,11},{10,... | collective-permute-start | bytes 589832 | tf_op jit(solution)/shard_map/ppermute | solution.py:107
  86.5 15.4 %collective-permute-start.21 = (bf16[128,768]{1,0:T(8,128)(2,1)}, bf16[128,768]{1,0:T(8,128)(2,1)S(1)}, u32[]{:S(2)}, u32[]{:S(2)}) collective-permute-start(bf16[128,768]{1,0:T(8,128)(2,1)} %get-tuple-element.203), channel_id=1, source_target_pairs={{0,3},{1,2},{2,1},{3,0},{4,7},{5,6},{6,5},{7,4},{8,11},{9,10},{10,... | collective-permute-start | bytes 589832 | tf_op jit(solution)/shard_map/ppermute | solution.py:107
  119.8 23.1 %all-to-all-start.1 = ((bf16[4,128,768]{2,1,0:T(8,128)(2,1)}), bf16[4,128,768]{2,1,0:T(8,128)(2,1)S(1)}, u32[]{:S(2)}, u32[]{:S(2)}) async-start(bf16[4,128,768]{2,1,0:T(8,128)(2,1)} %bitcast.50), calls=%async_computation.1 | async-start | bytes 1572864 | tf_op jit(solution)/shard_map/all_to_all | solution.py:914
  142.9 9.9 %collective-permute-start.26 = (bf16[4,384,768]{2,1,0:T(8,128)(2,1)}, bf16[4,384,768]{2,1,0:T(8,128)(2,1)S(1)}, u32[]{:S(2)}, u32[]{:S(2)}) collective-permute-start(bf16[4,384,768]{2,1,0:T(8,128)(2,1)} %get-tuple-element.226), channel_id=1, source_target_pairs={{0,4},{4,0},{8,12},{12,8},{16,20},{20,16},{24,28},{28,24},{1,5},{5... | collective-permute-start | bytes 7077896 | tf_op jit(solution)/shard_map/ppermute | solution.py:107
  149.2 11.9 %collective-permute-start.27 = (bf16[4,4,24,896]{3,2,1,0:T(8,128)(2,1)}, bf16[4,4,24,896]{3,2,1,0:T(8,128)(2,1)}, u32[]{:S(2)}, u32[]{:S(2)}) collective-permute-start(bf16[4,4,24,896]{3,2,1,0:T(8,128)(2,1)} %get-tuple-element.233), channel_id=1, source_target_pairs={{0,4},{4,0},{8,12},{12,8},{16,20},{20,16},{24,28},{28,24},{1,5},{5... | collective-permute-start | bytes 2064392 | tf_op jit(solution)/shard_map/ppermute | solution.py:107
  149.2 11.8 %collective-permute-start.22 = (bf16[256,192]{1,0:T(8,128)(2,1)}, bf16[256,192]{1,0:T(8,128)(2,1)}, u32[]{:S(2)}, u32[]{:S(2)}) collective-permute-start(bf16[256,192]{1,0:T(8,128)(2,1)} %get-tuple-element.220), channel_id=1, source_target_pairs={{0,8},{4,12},{8,0},{12,4},{16,24},{20,28},{24,16},{28,20},{1,9},{5... | collective-permute-start | bytes 294920 | tf_op jit(solution)/shard_map/ppermute | solution.py:107
  150.8 10.3 %collective-permute-start.23 = (bf16[256,192]{1,0:T(8,128)(2,1)}, bf16[256,192]{1,0:T(8,128)(2,1)}, u32[]{:S(2)}, u32[]{:S(2)}) collective-permute-start(bf16[256,192]{1,0:T(8,128)(2,1)} %get-tuple-element.221), channel_id=1, source_target_pairs={{0,16},{4,20},{8,24},{12,28},{16,0},{20,4},{24,8},{28,12},{1,17},{... | collective-permute-start | bytes 294920 | tf_op jit(solution)/shard_map/ppermute | solution.py:107
  151.2 9.9 %collective-permute-start.24 = (bf16[256,192]{1,0:T(8,128)(2,1)}, bf16[256,192]{1,0:T(8,128)(2,1)}, u32[]{:S(2)}, u32[]{:S(2)}) collective-permute-start(bf16[256,192]{1,0:T(8,128)(2,1)} %get-tuple-element.222), channel_id=1, source_target_pairs={{0,24},{4,28},{8,16},{12,20},{16,8},{20,12},{24,0},{28,4},{1,25},{... | collective-permute-start | bytes 294920 | tf_op jit(solution)/shard_map/ppermute | solution.py:107
  161.1 38.0 %all-to-all-start.2 = ((bf16[4,480,768]{2,1,0:T(8,128)(2,1)}), bf16[4,480,768]{2,1,0:T(8,128)(2,1)S(1)}, u32[]{:S(2)}, u32[]{:S(2)}) async-start(bf16[4,480,768]{2,1,0:T(8,128)(2,1)} %get-tuple-element.243), calls=%async_computation.2 | async-start | bytes 5898240 | tf_op jit(solution)/shard_map/all_to_all | solution.py:1035
  167.3 29.2 %collective-permute-start.28 = (bf16[4,24,896]{2,1,0:T(8,128)(2,1)}, bf16[4,24,896]{2,1,0:T(8,128)(2,1)S(1)}, u32[]{:S(2)}, u32[]{:S(2)}) collective-permute-start(bf16[4,24,896]{2,1,0:T(8,128)(2,1)} %get-tuple-element.251), channel_id=1, source_target_pairs={{0,1},{1,0},{2,3},{3,2},{4,5},{5,4},{6,7},{7,6},{8,9},{9,8},{10,11... | collective-permute-start | bytes 516104 | tf_op jit(solution)/shard_map/ppermute | solution.py:107
  167.3 29.2 %collective-permute-start.29 = (bf16[4,24,896]{2,1,0:T(8,128)(2,1)}, bf16[4,24,896]{2,1,0:T(8,128)(2,1)S(1)}, u32[]{:S(2)}, u32[]{:S(2)}) collective-permute-start(bf16[4,24,896]{2,1,0:T(8,128)(2,1)} %get-tuple-element.252), channel_id=1, source_target_pairs={{0,2},{1,3},{2,0},{3,1},{4,6},{5,7},{6,4},{7,5},{8,10},{9,11},{10,... | collective-permute-start | bytes 516104 | tf_op jit(solution)/shard_map/ppermute | solution.py:107
  170.1 26.4 %collective-permute-start.30 = (bf16[4,24,896]{2,1,0:T(8,128)(2,1)}, bf16[4,24,896]{2,1,0:T(8,128)(2,1)S(1)}, u32[]{:S(2)}, u32[]{:S(2)}) collective-permute-start(bf16[4,24,896]{2,1,0:T(8,128)(2,1)} %get-tuple-element.253), channel_id=1, source_target_pairs={{0,3},{1,2},{2,1},{3,0},{4,7},{5,6},{6,5},{7,4},{8,11},{9,10},{10,... | collective-permute-start | bytes 516104 | tf_op jit(solution)/shard_map/ppermute | solution.py:107
  199.2 25.3 %all-to-all-start.3 = ((bf16[4,128,768]{2,1,0:T(8,128)(2,1)}), bf16[4,128,768]{2,1,0:T(8,128)(2,1)}, u32[]{:S(2)}, u32[]{:S(2)}) async-start(bf16[4,128,768]{2,1,0:T(8,128)(2,1)} %bitcast.48), calls=%async_computation.3 | async-start | bytes 1572864 | tf_op jit(solution)/shard_map/all_to_all | solution.py:914
  209.2 18.2 %collective-permute-start.32 = (bf16[4,4,24,576]{3,2,1,0:T(8,128)(2,1)}, bf16[4,4,24,576]{3,2,1,0:T(8,128)(2,1)S(1)}, u32[]{:S(2)}, u32[]{:S(2)}) collective-permute-start(bf16[4,4,24,576]{3,2,1,0:T(8,128)(2,1)} %get-tuple-element.257), channel_id=1, source_target_pairs={{0,4},{4,0},{8,12},{12,8},{16,20},{20,16},{24,28},{28,24},{1,5},{5... | collective-permute-start | bytes 1327112 | tf_op jit(solution)/shard_map/ppermute | solution.py:107
  224.5 41.6 %all-to-all-start.4 = ((f32[32,24,128]{2,1,0:T(8,128)}), f32[32,24,128]{2,1,0:T(8,128)S(1)}, u32[]{:S(2)}, u32[]{:S(2)}) async-start(f32[32,24,128]{2,1,0:T(8,128)} %get-tuple-element.288), calls=%async_computation.4 | async-start | bytes 786432 | tf_op jit(solution)/shard_map/all_to_all | solution.py:1174
  227.4 15.7 %collective-permute-start.36 = (bf16[256,768]{1,0:T(8,128)(2,1)}, bf16[256,768]{1,0:T(8,128)(2,1)S(1)}, u32[]{:S(2)}, u32[]{:S(2)}) collective-permute-start(bf16[256,768]{1,0:T(8,128)(2,1)} %get-tuple-element.281), channel_id=1, source_target_pairs={{0,8},{4,12},{8,0},{12,4},{16,24},{20,28},{24,16},{28,20},{1,9},{5... | collective-permute-start | bytes 1179656 | tf_op jit(solution)/shard_map/ppermute | solution.py:107
  229.1 17.7 %collective-permute-start.37 = (bf16[256,768]{1,0:T(8,128)(2,1)}, bf16[256,768]{1,0:T(8,128)(2,1)S(1)}, u32[]{:S(2)}, u32[]{:S(2)}) collective-permute-start(bf16[256,768]{1,0:T(8,128)(2,1)} %get-tuple-element.283), channel_id=1, source_target_pairs={{0,16},{4,20},{8,24},{12,28},{16,0},{20,4},{24,8},{28,12},{1,17},{... | collective-permute-start | bytes 1179656 | tf_op jit(solution)/shard_map/ppermute | solution.py:107
  230.5 22.0 %collective-permute-start.38 = (bf16[256,768]{1,0:T(8,128)(2,1)}, bf16[256,768]{1,0:T(8,128)(2,1)S(1)}, u32[]{:S(2)}, u32[]{:S(2)}) collective-permute-start(bf16[256,768]{1,0:T(8,128)(2,1)} %get-tuple-element.284), channel_id=1, source_target_pairs={{0,24},{4,28},{8,16},{12,20},{16,8},{20,12},{24,0},{28,4},{1,25},{... | collective-permute-start | bytes 1179656 | tf_op jit(solution)/shard_map/ppermute | solution.py:107
  233.2 11.9 %collective-permute-start.33 = (bf16[4,24,576]{2,1,0:T(8,128)(2,1)}, bf16[4,24,576]{2,1,0:T(8,128)(2,1)S(1)}, u32[]{:S(2)}, u32[]{:S(2)}) collective-permute-start(bf16[4,24,576]{2,1,0:T(8,128)(2,1)} %get-tuple-element.269), channel_id=1, source_target_pairs={{0,1},{1,0},{2,3},{3,2},{4,5},{5,4},{6,7},{7,6},{8,9},{9,8},{10,11... | collective-permute-start | bytes 331784 | tf_op jit(solution)/shard_map/ppermute | solution.py:107
  243.2 37.9 %collective-permute-start.42 = (bf16[288,768]{1,0:T(8,128)(2,1)S(1)}, bf16[288,768]{1,0:T(8,128)(2,1)S(1)}, u32[]{:S(2)}, u32[]{:S(2)}) collective-permute-start(bf16[288,768]{1,0:T(8,128)(2,1)S(1)} %copy-done.38), channel_id=1, source_target_pairs={{0,8},{4,12},{8,0},{12,4},{16,24},{20,28},{24,16},{28,20},{1,9},{5... | collective-permute-start | bytes 1327112 | tf_op jit(solution)/shard_map/ppermute | solution.py:107
  243.7 37.4 %collective-permute-start.43 = (bf16[288,768]{1,0:T(8,128)(2,1)S(1)}, bf16[288,768]{1,0:T(8,128)(2,1)S(1)}, u32[]{:S(2)}, u32[]{:S(2)}) collective-permute-start(bf16[288,768]{1,0:T(8,128)(2,1)S(1)} %copy-done.37), channel_id=1, source_target_pairs={{0,16},{4,20},{8,24},{12,28},{16,0},{20,4},{24,8},{28,12},{1,17},{... | collective-permute-start | bytes 1327112 | tf_op jit(solution)/shard_map/ppermute | solution.py:107
  245.2 35.9 %collective-permute-start.44 = (bf16[288,768]{1,0:T(8,128)(2,1)S(1)}, bf16[288,768]{1,0:T(8,128)(2,1)S(1)}, u32[]{:S(2)}, u32[]{:S(2)}) collective-permute-start(bf16[288,768]{1,0:T(8,128)(2,1)S(1)} %copy-done.36), channel_id=1, source_target_pairs={{0,24},{4,28},{8,16},{12,20},{16,8},{20,12},{24,0},{28,4},{1,25},{... | collective-permute-start | bytes 1327112 | tf_op jit(solution)/shard_map/ppermute | solution.py:107
  246.7 14.7 %collective-permute-start.34 = (bf16[4,24,576]{2,1,0:T(8,128)(2,1)}, bf16[4,24,576]{2,1,0:T(8,128)(2,1)S(1)}, u32[]{:S(2)}, u32[]{:S(2)}) collective-permute-start(bf16[4,24,576]{2,1,0:T(8,128)(2,1)} %get-tuple-element.270), channel_id=1, source_target_pairs={{0,2},{1,3},{2,0},{3,1},{4,6},{5,7},{6,4},{7,5},{8,10},{9,11},{10,... | collective-permute-start | bytes 331784 | tf_op jit(solution)/shard_map/ppermute | solution.py:107
  264.9 9.7 %collective-permute-start.40 = (bf16[24,1472]{1,0:T(8,128)(2,1)}, bf16[24,1472]{1,0:T(8,128)(2,1)S(1)}, u32[]{:S(2)}, u32[]{:S(2)}) collective-permute-start(bf16[24,1472]{1,0:T(8,128)(2,1)} %get-tuple-element.300), channel_id=1, source_target_pairs={{0,16},{4,20},{8,24},{12,28},{16,0},{20,4},{24,8},{28,12},{1,17},{... | collective-permute-start | bytes 211976 | tf_op jit(solution)/shard_map/ppermute | solution.py:107
  (57 other events, 433.9 us)

commit v2 on v1

--- a/solution.py
+++ b/solution.py
@@ -195,18 +195,18 @@
     sent_ref[...] = dot(pick.astype(BF16), dz_ref[...], NN).astype(BF16)
 
 
-def middle_kernel(*refs, groups, ring, batch, tall, part, capacity, pieces):
+def gather_kernel(*refs, groups, ring, batch, tall):
+    w_refs, w_ref, w_s = refs[:-2], refs[-2], refs[-1]
+    assemble(place(ring), w_refs, w_s, groups, batch, tall)
+    w_ref[...] = w_s[...].astype(BF16)
+
+
+def middle_kernel(*refs, groups, ring, batch, part, capacity):
     info = place(ring)
     mixed_refs, refs = refs[:groups], refs[groups:]
-    w_refs, refs = refs[:pieces], refs[pieces:]
-    tokens_ref, gain_ref, pick_ref, route_ref, w_ref, middle_ref, gate_ref = refs[:7]
-    sent_refs, w_s = refs[7:-1], refs[-1]
+    w_ref, tokens_ref, gain_ref, pick_ref, route_ref, middle_ref, gate_ref = refs[:7]
+    sent_refs = refs[7:]
     width = tokens_ref.shape[1]
-    if tall % 8 == 0:
-        assemble(info, w_refs, w_s, groups, batch, tall)
-    else:
-        w_s[...] = w_refs[0][...].astype(F32)
-    w_ref[...] = w_s[...].astype(BF16)
     middle = tokens_ref[...].astype(F32)
     for m in range(groups):
         start = pl.multiple_of((info[0] ^ m) * part, 16)
@@ -255,18 +255,18 @@
         grad = dot(mixed_refs[m][...], d_branch, TN)
         grad = jnp.concatenate([grad, rpart_ref[pl.ds(start, part), :]], axis=1)
         if tall % 8 == 0:
-            scatter_rows(info, grad, m, grad_refs, ring, batch, tall)
+            scatter_rows(info, grad, m, grad_refs, ring, batch, tall, info[2])
         else:
             grad_refs[0][pl.ds(start, part), :] = grad
 
 
-def scatter_rows(info, grad, g, grad_refs, ring, batch, tall):
+def scatter_rows(info, grad, g, grad_refs, ring, batch, tall, turn):
     for z in range(batch):
         rows = [
             grad[(r * batch + z) * tall : (r * batch + z + 1) * tall, :] for r in range(ring)
         ]
         for ref, row in zip(grad_refs, xor_order(rows, info[1])):
-            ref[z ^ info[2], g] = row.astype(ref.dtype)
+            ref[z ^ turn, g] = row.astype(ref.dtype)
 
 
 def weight_kernel(dq_ref, *refs, groups, ring, batch, tall, part, per):
@@ -287,7 +287,7 @@
         grad = dot(x_s[:, g * share : (g + 1) * share], dp_ref[...], TN)
         grad = jnp.concatenate([grad[:, k * wide : k * wide + part] for k in range(3)], axis=1)
         if tall % 8 == 0:
-            scatter_rows(info, grad, g ^ info[0], grad_refs, ring, batch, tall)
+            scatter_rows(info, grad, g ^ info[0], grad_refs, ring, batch, tall, info[2])
         else:
             grad_refs[0][g * share : (g + 1) * share, :] = grad
 
@@ -381,51 +381,88 @@
     out_ref[...] = (middle_ref[...] + gate_ref[...] * returned).astype(BF16)
 
 
-def merge_kernel(*refs, groups, ring):
-    g1_refs, g2_refs, one_ref = refs[:ring], refs[ring : 2 * ring], refs[2 * ring]
-    g1 = sum(ref[...].astype(F32) for ref in g1_refs)
-    g2 = sum(ref[...].astype(F32) for ref in g2_refs)
-    rows, more = g1.shape[0], one_ref.shape[0] - g1.shape[0]
-    one_ref[:rows, :] = g1.astype(BF16)
-    one_ref[rows:, :] = g2[:more, :].astype(BF16)
-    for m, ref in enumerate(refs[2 * ring + 1 :]):
-
-        @pl.when((pl.program_id(0) ^ place(ring)[0]) == m)
-        def _():
-            ref[...] = g2[more:, :].astype(BF16)
-
-
-def merge(g1, g2, more):
+def merge_kernel(*refs, ring):
+    g1_refs, g2_refs = refs[:ring], refs[ring : 2 * ring]
+    own_ref, left_ref, right_ref, one_ref, two_ref = refs[2 * ring :]
+    step = pl.program_id(0)
+    g1 = sum(ref[...].astype(F32) for ref in g1_refs).astype(BF16)
+    g2 = sum(ref[...].astype(F32) for ref in g2_refs).astype(BF16)
+    rows, half = g1.shape[0], g1.shape[1] // 2
+
+    def put(ref, cut):
+        ref[:rows, :] = g1[:, cut]
+        ref[rows:, :] = g2[:, cut]
+
+    left, right = slice(0, half), slice(half, 2 * half)
+    pl.when(step <= 1)(lambda: put(one_ref, left))
+    pl.when((step == 1) | (step == 2))(lambda: put(two_ref, right))
+    pl.when(step == 0)(lambda: put(right_ref, right))
+    pl.when(step == 2)(lambda: put(left_ref, left))
+    pl.when(step == 3)(lambda: put(own_ref, slice(0, 2 * half)))
+
+
+def merge(g1, g2):
     groups, rows, width = g1[0].shape
+    assert groups == 4
     ring = len(g1)
-    left = g2[0].shape[1] - more
-    outs = pl.pallas_call(
-        functools.partial(merge_kernel, groups=groups, ring=ring),
+    tall, half = 2 * rows, width // 2
+    order = lambda s: (jnp.where(s == 0, 1, jnp.where(s == 1, 3, jnp.where(s == 2, 2, 0))), 0, 0)
+    block = lambda columns: pl.BlockSpec((tall, columns), lambda s: (0, 0))
+    return pl.pallas_call(
+        functools.partial(merge_kernel, ring=ring),
         grid=(groups,),
-        out_shape=(jax.ShapeDtypeStruct((groups, rows + more, width), BF16),)
-        + (jax.ShapeDtypeStruct((left, width), BF16),) * groups,
-        in_specs=[pl.BlockSpec((None, rows, width), lambda g: (g, 0, 0))] * ring
-        + [pl.BlockSpec((None, left + more, width), lambda g: (g, 0, 0))] * ring,
-        out_specs=[pl.BlockSpec((None, rows + more, width), lambda g: (g, 0, 0))]
-        + [pl.BlockSpec((left, width), lambda g: (0, 0))] * groups,
+        out_shape=(
+            jax.ShapeDtypeStruct((tall, width), BF16),
+            jax.ShapeDtypeStruct((tall, half), BF16),
+            jax.ShapeDtypeStruct((tall, half), BF16),
+            jax.ShapeDtypeStruct((2, tall, half), BF16),
+            jax.ShapeDtypeStruct((2, tall, half), BF16),
+        ),
+        in_specs=[pl.BlockSpec((None, rows, width), order)] * (2 * ring),
+        out_specs=[
+            block(width),
+            block(half),
+            block(half),
+            pl.BlockSpec((None, tall, half), lambda s: (jnp.minimum(s, 1), 0, 0)),
+            pl.BlockSpec((None, tall, half), lambda s: (jnp.where(s <= 1, 1, 0), 0, 0)),
+        ],
         compiler_params=pltpu.CompilerParams(
             dimension_semantics=("arbitrary",), vmem_limit_bytes=56 << 20
         ),
         name="merge",
     )(*g1, *g2)
-    return outs[0], list(outs[1:])
-
-
-def finish_kernel(one_ref, *refs):
-    two_refs, in_ref, out_ref = refs[:-2], *refs[-2:]
-    one = jnp.sum(one_ref[...].astype(F32), axis=0)
+
+
+def fold_kernel(left_ref, right_ref, one_ref, two_ref, left_out, right_out):
+    left_out[...] = (left_ref[...].astype(F32) + one_ref[...].astype(F32)).astype(BF16)
+    right_out[...] = (right_ref[...].astype(F32) + two_ref[...].astype(F32)).astype(BF16)
+
+
+def fold(left, right, one, two):
+    tall, half = left.shape
+    steps = 2
+    plain = pl.BlockSpec((tall // steps, half), lambda s: (s, 0))
+    second = pl.BlockSpec((None, tall // steps, half), lambda s: (1, s, 0))
+    return pl.pallas_call(
+        fold_kernel,
+        grid=(steps,),
+        out_shape=(jax.ShapeDtypeStruct((tall, half), BF16),) * 2,
+        in_specs=[plain, plain, second, second],
+        out_specs=[plain, plain],
+        compiler_params=pltpu.CompilerParams(dimension_semantics=("arbitrary",)),
+        name="fold",
+    )(left, right, one, two)
+
+
+def finish_kernel(own_ref, one_ref, two_ref, left_ref, right_ref, in_ref, out_ref):
     tall, width = in_ref.shape[0], out_ref.shape[1]
-    tiles = in_ref.shape[1] // width
-    for j in range(tiles):
-        in_ref[:, j * width : (j + 1) * width] = one[j * tall : (j + 1) * tall, :]
-    more = one.shape[0] - tiles * tall
-    out_ref[:more, :] = one[tiles * tall :, :]
-    out_ref[more:, :] = sum(ref[...].astype(F32) for ref in two_refs)
+    half, rows = width // 2, out_ref.shape[0]
+    for at, first_ref, last_ref in ((0, one_ref, left_ref), (half, two_ref, right_ref)):
+        cut = slice(at, at + half)
+        total = own_ref[:, cut].astype(F32) + first_ref[0].astype(F32) + last_ref[...].astype(F32)
+        for j in range(in_ref.shape[1] // width):
+            in_ref[:, j * width + at : j * width + at + half] = total[j * tall : (j + 1) * tall, :]
+        out_ref[:, cut] = total[rows:, :]
 
 
 SEGMENTS = 8
@@ -507,12 +544,27 @@
                     value_s[at, h] = value.astype(BF16)
 
 
+def two_step(first, last, start, finish, even, odd):
+    start(first, even)
+
+    @pl.loop(0, (last - first + 1) // 2)
+    def _(j):
+        kb = first + 2 * j
+        start(jnp.minimum(kb + 1, last - 1), odd)
+        finish(kb, even)
+
+        @pl.when(kb + 1 < last)
+        def _():
+            start(jnp.minimum(kb + 2, last - 1), even)
+            finish(kb + 1, odd)
+
+
 def attend_kernel(q_ref, *refs, heads, groups, ring, block):
     info = place(ring)
     kv_refs, refs = refs[:ring], refs[ring:]
     band_ref, ot_ref, lse_ref = refs[:3]
     mixed_refs, refs = refs[3 : 3 + groups], refs[3 + groups :]
-    bias_s, seg_s, span_s, key_s, vt_s, query_s, stat_s, acc_s = refs
+    bias_s, seg_s, span_s, key_s, vt_s, query_s, stat_s, acc_s, even_s, odd_s = refs
     set_bias(band_ref, bias_s, heads, block)
     set_spans(info, kv_refs, seg_s, span_s, groups, ring, block)
     set_keys(kv_refs, seg_s, heads, groups, block, 0, key_s, vt_s, 256)
@@ -530,16 +582,19 @@
         stat_s[heads : 2 * heads] = jnp.zeros((heads, 1, block), F32)
         acc_s[...] = jnp.zeros_like(acc_s)
 
-        @pl.loop(span_s[i, 0], span_s[i, 1])
-        def _(kb):
+        def start(kb, score_s):
             at = key_at(kb, info, ring, groups)
             d = jnp.clip(kb - qb, -2, 2) + 2
-            scores = [dot(key_s[at, h], query_s[h], NT) + bias_s[h, d] for h in range(heads)]
+            for h in range(heads):
+                score_s[h] = dot(key_s[at, h], query_s[h], NT) + bias_s[h, d]
+
+        def finish(kb, score_s):
+            at = key_at(kb, info, ring, groups)
             tops = [
-                jnp.maximum(stat_s[h], jnp.max(scores[h], axis=0, keepdims=True))
+                jnp.maximum(stat_s[h], jnp.max(score_s[h], axis=0, keepdims=True))
                 for h in range(heads)
             ]
-            expos = [jnp.exp(scores[h] - tops[h]) for h in range(heads)]
+            expos = [jnp.exp(score_s[h] - tops[h]) for h in range(heads)]
             for h in range(heads):
                 decay = jnp.exp(stat_s[h] - tops[h])
                 stat_s[h] = tops[h]
@@ -548,6 +603,8 @@
                 )
                 value_t = vt_s[at, h * 64 : (h + 1) * 64, :]
                 acc_s[h] = acc_s[h] * decay + dot(value_t, expos[h].astype(BF16), NN)
+
+        two_step(span_s[i, 0], span_s[i, 1], start, finish, even_s, odd_s)
 
         for h in range(heads):
             total = stat_s[heads + h]
@@ -575,6 +632,8 @@
             ((heads, block, 128), BF16),
             ((2 * heads, 1, block), F32),
             ((heads, 64, block), F32),
+            ((heads, block, block), F32),
+            ((heads, block, block), F32),
         ],
     )
 
@@ -715,8 +774,8 @@
     info = place(ring)
     piece_refs, refs = refs[:batch], refs[batch:]
     dz_ref, router_ref, w1_ref, w2_ref = refs[:4]
-    prod_ref, back_ref, rpart_ref, rows_t, dret_ref, hidden_ref, d_pre_ref = refs[4:11]
-    rows_ref, prob_s, prod_s, back_s = refs[11:]
+    prod_ref, back_ref, d_logits_ref, rows_ref, dret_ref, hidden_ref, d_pre_ref = refs[4:11]
+    prob_s, prod_s, back_s = refs[11:]
     capacity = piece_refs[0].shape[0]
     step = pl.program_id(0)
     me = info[2]
@@ -727,9 +786,7 @@
         for m, ref in enumerate(piece_refs):
             start = pl.multiple_of((me ^ m) * capacity, capacity)
             rows_ref[pl.ds(start, capacity), :] = ref[...]
-        rows = rows_ref[...]
-        rows_t[...] = rows.astype(F32).T.astype(BF16)
-        logits = dot(rows, router_ref[...], NN)
+        logits = dot(rows_ref[...], router_ref[...], NN)
         logits = jnp.where(lane < experts, logits, MASKED)
         expo = jnp.exp(logits - jnp.max(logits, axis=1, keepdims=True))
         probs = expo / jnp.sum(expo, axis=1, keepdims=True)
@@ -765,7 +822,7 @@
         d_logits = (d_gate * probs * (chosen - gate)).astype(BF16)
         back = back_s[...].astype(BF16).astype(F32) + dot(d_logits, router_ref[...], NT)
         back_ref[...] = back.astype(BF16)
-        rpart_ref[...] = dot(rows_t[...], d_logits, NN)
+        d_logits_ref[...] = d_logits
 
 
 def expert_layer(pieces, dz, w_both, w1, w2, ring):
@@ -790,14 +847,13 @@
         out_specs=[
             whole,
             whole,
-            pl.BlockSpec((width, lanes), fixed),
-            pl.BlockSpec((width, slots), fixed),
+            pl.BlockSpec((slots, lanes), fixed),
+            whole,
             whole,
             pl.BlockSpec((slots, cut), lambda j: (0, j)),
             pl.BlockSpec((slots, cut), lambda j: (0, j)),
         ],
         scratch_shapes=[
-            pltpu.VMEM((slots, width), BF16),
             pltpu.VMEM((slots, lanes), F32),
             pltpu.VMEM((slots, width), F32),
             pltpu.VMEM((slots, width), F32),
@@ -805,8 +861,8 @@
         out_shape=(
             jax.ShapeDtypeStruct((slots, width), BF16),
             jax.ShapeDtypeStruct((slots, width), BF16),
-            jax.ShapeDtypeStruct((width, lanes), F32),
-            jax.ShapeDtypeStruct((width, slots), BF16),
+            jax.ShapeDtypeStruct((slots, lanes), BF16),
+            jax.ShapeDtypeStruct((slots, width), BF16),
             jax.ShapeDtypeStruct((slots, width), BF16),
             jax.ShapeDtypeStruct((slots, hidden), BF16),
             jax.ShapeDtypeStruct((slots, hidden), BF16),
@@ -818,14 +874,22 @@
     )(*pieces, dz, w_both, w1, w2)
 
 
-def expert_grad_kernel(rows_t, dret_ref, hidden_ref, d_pre_ref, *refs, groups, ring):
+def expert_grad_kernel(
+    d_logits_ref, rows_ref, dret_ref, hidden_ref, d_pre_ref, *refs, groups, ring
+):
     info = place(ring)
-    g1_refs, g2_refs = refs[:ring], refs[ring:]
+    router_ref, g1_refs, g2_refs, rows_t = refs[0], refs[1 : 1 + ring], refs[1 + ring : -1], refs[-1]
+
+    @pl.when(pl.program_id(0) == 0)
+    def _():
+        rows_t[...] = rows_ref[...].astype(F32).T.astype(BF16)
+        router_ref[...] = dot(rows_t[...], d_logits_ref[...], NN)
+
     g2 = dot(hidden_ref[...], dret_ref[...], TN).astype(BF16)
     share = g2.shape[0] // ring
     parts = [g2[c * share : (c + 1) * share, :] for c in range(ring)]
     for ref, rows in zip(g2_refs, xor_order(parts, info[1])):
-        ref[...] = rows
+        ref[pl.program_id(0) ^ info[0]] = rows
     g1 = dot(rows_t[...], d_pre_ref[...], NN).astype(BF16)
     tall = g1.shape[0] // (groups * ring)
     for g in range(groups):
@@ -833,11 +897,12 @@
             g1[(g * ring + c) * tall : (g * ring + c + 1) * tall, :] for c in range(ring)
         ]
         for ref, rows in zip(g1_refs, xor_order(parts, info[1])):
-            ref[g] = rows
-
-
-def expert_grads(rows_t, d_ret, hidden, d_pre, groups, ring):
-    width, slots = rows_t.shape
+            ref[g ^ info[0]] = rows
+
+
+def expert_grads(d_logits, rows, d_ret, hidden, d_pre, groups, ring):
+    slots, width = rows.shape
+    lanes = d_logits.shape[1]
     devices = groups * ring
     share = hidden.shape[1] // devices
     cut = share * ring
@@ -847,20 +912,24 @@
         functools.partial(expert_grad_kernel, groups=groups, ring=ring),
         grid=(tiles,),
         in_specs=[
-            pl.BlockSpec((width, slots), lambda j: (0, 0)),
+            pl.BlockSpec((slots, lanes), lambda j: (0, 0)),
+            pl.BlockSpec((slots, width), lambda j: (0, 0)),
             pl.BlockSpec((slots, width), lambda j: (0, 0)),
             pl.BlockSpec((slots, cut), lambda j: (0, j)),
             pl.BlockSpec((slots, cut), lambda j: (0, j)),
         ],
-        out_specs=[pl.BlockSpec((groups, tall, cut), lambda j: (0, j, 0))] * ring
-        + [pl.BlockSpec((None, share, width), lambda j: (j, 0, 0))] * ring,
-        out_shape=(jax.ShapeDtypeStruct((groups, tiles * tall, cut), BF16),) * ring
+        out_specs=[pl.BlockSpec((width, lanes), lambda j: (0, 0))]
+        + [pl.BlockSpec((groups, tall, cut), lambda j: (0, j, 0))] * ring
+        + [pl.BlockSpec((groups, share, width), lambda j: (0, 0, 0))] * ring,
+        scratch_shapes=[pltpu.VMEM((width, slots), BF16)],
+        out_shape=(jax.ShapeDtypeStruct((width, lanes), F32),)
+        + (jax.ShapeDtypeStruct((groups, tiles * tall, cut), BF16),) * ring
         + (jax.ShapeDtypeStruct((groups, share, width), BF16),) * ring,
         compiler_params=pltpu.CompilerParams(
             dimension_semantics=("arbitrary",), vmem_limit_bytes=56 << 20
         ),
         name="expert_grads",
-    )(rows_t, d_ret, hidden, d_pre)
+    )(d_logits, rows, d_ret, hidden, d_pre)
 
 
 def body(
@@ -941,7 +1010,10 @@
         cuts = jnp.concatenate([cuts, swap(cuts, "batch", n_batch, step)], axis=0)
         cuts, both = lax.optimization_barrier((cuts, both)) if step == 1 else (cuts, both)
         step = step * 2
-    both = jnp.concatenate([both, swap(both, "batch", n_batch, 1)], axis=0)
+    step = 1
+    while step < n_batch:
+        both = jnp.concatenate([both, swap(both, "batch", n_batch, step)], axis=0)
+        step = step * 2
 
     route_row = routes.reshape(1, per)
     d_result = out_grad[0]
@@ -965,10 +1037,6 @@
         (arrived, cuts, dz_sent, band, both)
     )
     cuts = over_ring([cuts] * ring)
-    step = 2
-    while step < n_batch:
-        both = jnp.concatenate([both, swap(both, "batch", n_batch, step)], axis=0)
-        step = step * 2
     dz_there = turn_batch(dz_sent)
     if not fine:
         cuts = natural(cuts, 3 * part)
@@ -1002,43 +1070,37 @@
     mixed, dz_there, both = lax.optimization_barrier((mixed, dz_there, both))
     both = jnp.stack([b.reshape(n_batch, tall, width + lanes) for b in both], axis=1)
     both = over_ring([both.reshape(n_batch * groups * tall, width + lanes)] * ring)
-    if not fine:
-        both = natural(both, width + lanes)
+    if fine:
+        both = kernel_call(
+            functools.partial(gather_kernel, groups=groups, ring=ring, batch=n_batch, tall=tall),
+            "gather",
+            both,
+            [((width, width + lanes), BF16)],
+            [((width, width + lanes), F32)],
+        )[0]
+    else:
+        both = natural(both, width + lanes)[0]
     mixed = over_groups(mixed)
-    both, middle, gate, *rows_sent = kernel_call(
+    mixed, both = lax.optimization_barrier((mixed, both))
+    middle, gate, *rows_sent = kernel_call(
         functools.partial(
-            middle_kernel,
-            groups=groups,
-            ring=ring,
-            batch=n_batch,
-            tall=tall,
-            part=part,
-            capacity=capacity,
-            pieces=len(both),
+            middle_kernel, groups=groups, ring=ring, batch=n_batch, part=part, capacity=capacity
         ),
         "middle",
-        [*mixed, *both, tokens[0], ffn_gain, pick, route_row],
-        [((width, width + lanes), BF16), ((per, width), F32), ((per, 1), F32)]
-        + [((capacity, width), BF16)] * n_batch,
-        [((width, width + lanes), F32)],
+        [*mixed, both, tokens[0], ffn_gain, pick, route_row],
+        [((per, width), F32), ((per, 1), F32)] + [((capacity, width), BF16)] * n_batch,
     )
     rows_there = over_batch(rows_sent)
-    produced, back, router_part, *saved = expert_layer(
+    produced, back, *saved = expert_layer(
         rows_there, dz_there, both, expert_in[0], expert_out[0], ring
     )
     back = turn_batch(back)
-    grads = expert_grads(*saved, groups, ring)
+    router_part, *grads = expert_grads(*saved, groups, ring)
     g1, g2 = grads[:ring], grads[ring:]
-
-    def turn_groups(grads):
-        sets = [[g * ring + r for g in range(groups)] for r in range(ring)]
-        return lax.all_to_all(
-            grads, "ctx", split_axis=0, concat_axis=0, tiled=True, axis_index_groups=sets
-        )
 
     back, g1, g2 = lax.optimization_barrier((back, g1, g2))
     g1, g2 = over_ring(g1), over_ring(g2)
-    grads_one, grads_two = merge(g1, g2, g2[0].shape[1] // 4)
+    kept, kept_left, kept_right, grads_one, grads_two = merge(g1, g2)
     sums_shape = (n_batch, groups, tall, width + lanes)
     sums_shape = (
         [(sums_shape, F32)] + [(sums_shape, BF16)] * (ring - 1)
@@ -1083,7 +1145,8 @@
         [(shape, F32)] + [(shape, BF16)] * (n_batch - 1),
     )
     out_parts = over_batch(out_parts)
-    grads_one = turn_groups(grads_one)
+    grads_one = swap(grads_one, "ctx", n_ctx, ring)
+    grads_two = swap(grads_two, "ctx", n_ctx, 2 * ring)
 
     dq, dkv_own, *rest = attend_back(
         q, kv_all, band, d_mix, out_t, lse, heads, groups, ring, per
@@ -1094,6 +1157,9 @@
     )
     dkv_got = over_ring([dkv_own] + dkv_other)[1:]
     returned = turn_batch(produced)
+    last_left, last_right = fold(kept_left, kept_right, grads_one, grads_two)
+    last_left = swap(last_left, "ctx", n_ctx, 2 * ring)
+    last_right = swap(last_right, "ctx", n_ctx, ring)
 
     grads_shape = (
         [((n_batch, groups, tall, 3 * part), F32)]
@@ -1126,7 +1192,9 @@
         + [((n_ctx * n_batch, late_rows, lanes), F32)],
     )
     packed_parts = over_ring(by_place(packed_parts))
-    packed_parts, d_normed = lax.optimization_barrier((packed_parts, d_normed))
+    packed_parts, d_normed, last_left, last_right, returned = lax.optimization_barrier(
+        (packed_parts, d_normed, last_left, last_right, returned)
+    )
     got = over_groups(d_normed)
     shape = packed_parts[0].shape[1:]
     packed_parts = kernel_call(
@@ -1135,40 +1203,42 @@
         packed_parts,
         [(shape, F32)] + [(shape, BF16)] * (n_batch - 1),
     )
-    grads_two, got[1] = lax.optimization_barrier((grads_two, got[1]))
-    grads_two = over_groups(grads_two)
-    late, returned = lax.optimization_barrier((late, returned))
-    packed_parts = over_batch(packed_parts)
+    packed_parts = list(packed_parts)
     layer_out = kernel_call(
         combine_kernel,
         "combine",
         [returned, pick_t, middle, gate],
         [((per, width), BF16)],
     )[0][None]
+    expert_in_grad, expert_out_grad = kernel_call(
+        finish_kernel,
+        "finish",
+        [kept, grads_one, grads_two, last_left, last_right],
+        [
+            ((width // n_ctx, expert_in.shape[2]), F32),
+            ((expert_out.shape[1] // n_ctx, width), F32),
+        ],
+    )
+    packed_parts[-1], layer_out, expert_in_grad, expert_out_grad = lax.optimization_barrier(
+        (packed_parts[-1], layer_out, expert_in_grad, expert_out_grad)
+    )
+    packed_parts = over_batch(packed_parts)
     tokens_grad = kernel_call(
         functools.partial(tokens_kernel, groups=groups),
         "tokens",
         [*got, tokens[0], attn_gain, d_middle],
         [((per, width), BF16)],
     )[0][None]
-    packed_parts, layer_out, tokens_grad = lax.optimization_barrier(
-        (packed_parts, layer_out, tokens_grad)
+    packed_parts, layer_out, expert_in_grad, expert_out_grad, tokens_grad = (
+        lax.optimization_barrier(
+            (packed_parts, layer_out, expert_in_grad, expert_out_grad, tokens_grad)
+        )
     )
     parts = kernel_call(
         functools.partial(quarter_kernel, batch=n_batch),
         "quarter",
         [*packed_parts, *out_parts],
         [((tall, 3 * part + width + lanes), BF16)] * groups,
-    )
-
-    expert_in_grad, expert_out_grad = kernel_call(
-        finish_kernel,
-        "finish",
-        [grads_one, *grads_two],
-        [
-            ((width // n_ctx, expert_in.shape[2]), F32),
-            ((expert_out.shape[1] // n_ctx, width), F32),
-        ],
     )
 
     late = lax.all_to_all(late, ("ctx", "batch"), split_axis=0, concat_axis=0, tiled=True)

time: 288 us -> 267 us (0.927)
  waiting for transfers between devices: 70.1 us -> 51.2 us
  starting transfers between devices: 72.6 us -> 66.1 us
  Pallas kernels: 126 us -> 131 us
    ppermute x45 -> x46, waiting for transfers between devices: 49.4 us -> 38.2 us  [swap(): return lax.ppermute(value, axis, [(i, i ^ mask) for i in range(size)])]
    all_to_all x3, waiting for transfers between devices: 18.1 us -> 12.9 us  [turn_batch(): lax.all_to_all(rows, 'batch', split_axis=0, concat_axis=0, tiled=True)]
    all_to_all x1 -> x0, starting transfers between devices: 3.69 us -> none  [turn_groups(): lax.all_to_all(grads, 'ctx', split_axis=0, concat_axis=0, tiled=True, axi...]
    pallas_call x1 -> x2, Pallas kernels: 6.87 us -> 9.8 us  [the longest x1 7.28 us: merge(): pl.pallas_call(functools.partial(merge_kernel, ring=ring), grid=(groups,)...]
    ppermute x45 -> x46, starting transfers between devices: 53.5 us -> 51.2 us  [swap(): return lax.ppermute(value, axis, [(i, i ^ mask) for i in range(size)])]
    pallas_call x17 -> x18, Pallas kernels: 92.2 us -> 93.3 us  [kernel_call(): pl.pallas_call(kernel, out_shape=tuple((jax.ShapeDtypeStruct(shape, kind)...]
    unnamed x84 -> x94, local copies, waits for them, and re-layouts: 11.9 us -> 11.7 us
  transfers between devices with their start and end apart: 50 -> 50, of which waited for: 16 -> 14; matrix products, arithmetic and copies ran while one was open for 3% -> 1% of each run, Pallas kernels for 34% -> 39%
where the time goes in v2:
time: 267 us; the launch traced here: 265 us
  Pallas kernels  131 us (49%)
  starting transfers between devices  66.1 us (25%)
  waiting for transfers between devices  51.2 us (19%)
  local copies, waits for them, and re-layouts  13 us (5%)
    pallas_call x18, Pallas kernels, kernel_call(): pl.pallas_call(kernel, out_shape=tuple((jax.ShapeDtypeStruct(shape, kind)...  93.3 us
    ppermute x46, starting transfers between devices, swap(): return lax.ppermute(value, axis, [(i, i ^ mask) for i in range(size)])  51.2 us
    ppermute x46, waiting for transfers between devices, swap(): return lax.ppermute(value, axis, [(i, i ^ mask) for i in range(size)])  38.2 us
    pallas_call x1, Pallas kernels, expert_layer(): pl.pallas_call(functools.partial(expert_kernel, experts=batch, ring=ring,...  16.9 us
    all_to_all x3, waiting for transfers between devices, turn_batch(): lax.all_to_all(rows, 'batch', split_axis=0, concat_axis=0, tiled=True)  12.9 us
    all_to_all x3, starting transfers between devices, turn_batch(): lax.all_to_all(rows, 'batch', split_axis=0, concat_axis=0, tiled=True)  12.1 us
    unnamed x94, local copies, waits for them, and re-layouts  11.7 us
    pallas_call x1, Pallas kernels, expert_grads(): pl.pallas_call(functools.partial(expert_grad_kernel, groups=groups, ring=...  11.2 us
  transfers between devices with their start and end apart: 50, of which 14 were waited for; matrix products, arithmetic and copies ran while one was open for 1% of the time, Pallas kernels for 39%

profile of v2, /device:TPU:0, one launch (start us, length us, event | category | flops | bytes accessed | tf_op | source)
XLA Modules:
  0.0 265.3 jit_solution(8076765626561746571)
XLA Ops:
  2.7 2.9 %collective-permute-start = (bf16[24,576]{1,0:T(8,128)(2,1)}, bf16[24,576]{1,0:T(8,128)(2,1)S(1)}, u32[]{:S(2)}, u32[]{:S(2)}) collective-permute-start(bf16[24,576]{1,0:T(8,128)(2,1)} %get-tuple-element.167), channel_id=1, source_target_pairs={{0,8},{4,12},{8,0},{12,4},{16,24},{20,28},{24,16},{28,20},{1,9},{5... | collective-permute-start | bytes 82952 | tf_op jit(solution)/shard_map/ppermute | solution.py:107
  15.4 3.6 %collective-permute-done.6 = bf16[96,576]{1,0:T(8,128)(2,1)S(1)} collective-permute-done((bf16[96,576]{1,0:T(8,128)(2,1)S(1)}, bf16[96,576]{1,0:T(8,128)(2,1)S(1)}, u32[]{:S(2)}, u32[]{:S(2)}) %collective-permute-start.6) | collective-permute-done | bytes 110624 | tf_op jit(solution)/shard_map/ppermute | solution.py:107
  24.1 2.6 collective-permute-start.7
  28.7 2.5 dispatch.1
  31.2 6.0 %collective-permute-done.9 = bf16[48,896]{1,0:T(8,128)(2,1)S(1)} collective-permute-done((bf16[48,896]{1,0:T(8,128)(2,1)S(1)}, bf16[48,896]{1,0:T(8,128)(2,1)S(1)}, u32[]{:S(2)}, u32[]{:S(2)}) %collective-permute-start.9) | collective-permute-done | bytes 86048 | tf_op jit(solution)/shard_map/ppermute | solution.py:107
  38.0 3.9 %all-to-all-start = ((bf16[4,128,768]{2,1,0:T(8,128)(2,1)}), bf16[4,128,768]{2,1,0:T(8,128)(2,1)S(1)}, u32[]{:S(2)}, u32[]{:S(2)}) async-start(bf16[4,128,768]{2,1,0:T(8,128)(2,1)} %bitcast.50), calls=%async_computation | async-start | bytes 1572864 | tf_op jit(solution)/shard_map/all_to_all | solution.py:983
  42.7 4.6 %project.1 = (bf16[1024,256]{1,0:T(8,128)(2,1)}, bf16[1040,512]{1,0:T(8,128)(2,1)}, bf16[768,768]{1,0:T(8,128)(2,1)}) custom-call(bf16[272,768]{1,0:T(8,128)(2,1)} %get-tuple-element.178.refs_0_.refs_2_, bf16[272,768]{1,0:T(8,128)(2,1)} %copy-done.5, bf16[272,768]{1,0:T(8,128)(2,1)} %copy-done.4, bf16[272,768]{1,0:T(8,128)(2,1)} %copy-done.3, ...), custom_call_target="tpu_custom_call" | custom-call | tf_op jit(solution)/shard_map/project/pallas_call | solution.py:92
  52.0 15.7 %attend.1 = (f32[4,192,256]{2,1,0:T(8,128)}, f32[4,8,256]{2,1,0:T(8,128)}, bf16[256,192]{1,0:T(8,128)(2,1)}, bf16[256,192]{1,0:T(8,128)(2,1)}, bf16[256,192]{1,0:T(8,128)(2,1)}, /*index=5*/bf16[256,192]{1,0:T(8,128)(2,1)}) custom-call(bf16[1024,256]{1,0:T(8,128)(2,1)} %get-tuple-element.183.q_ref, bf16[1040,512]{1,0:T(8,128)(2,1)} %get-tuple-element.186.refs_0_, ...), custom_call_target="tpu_custom_call" | custom-call | tf_op jit(solution)/shard_map/attend/pallas_call | solution.py:92
  72.5 2.8 %gather.1.refs_4_.refs_5_.refs_8_ = bf16[768,896]{1,0:T(8,128)(2,1)} custom-call(bf16[384,896]{1,0:T(8,128)(2,1)} %bitcast.46, bf16[384,896]{1,0:T(8,128)(2,1)} %copy-done.15), custom_call_target="tpu_custom_call" | custom-call | tf_op jit(solution)/shard_map/gather/pallas_call | solution.py:92
  75.2 2.7 %collective-permute-done.16.refs_2_ = bf16[256,192]{1,0:T(8,128)(2,1)S(1)} collective-permute-done((bf16[256,192]{1,0:T(8,128)(2,1)}, bf16[256,192]{1,0:T(8,128)(2,1)S(1)}, u32[]{:S(2)}, u32[]{:S(2)}) %collective-permute-start.16) | collective-permute-done | bytes 98336 | tf_op jit(solution)/shard_map/ppermute | solution.py:107
  78.6 4.1 %middle.1 = (f32[256,768]{1,0:T(8,128)}, f32[256,1]{1,0:T(8,128)}, bf16[128,768]{1,0:T(8,128)(2,1)}, bf16[128,768]{1,0:T(8,128)(2,1)}, bf16[128,768]{1,0:T(8,128)(2,1)}, /*index=5*/bf16[128,768]{1,0:T(8,128)(2,1)}) custom-call(bf16[256,192]{1,0:T(8,128)(2,1)} %get-tuple-element.202.refs_0_, bf16[256,192]{1,0:T(8,128)(2,1)} %copy-done.18, ...), custom_call_target="tpu_custom_call" | custom-call | tf_op jit(solution)/shard_map/middle/pallas_call | solution.py:92
  87.1 4.9 %collective-permute-done.19.refs_1_ = bf16[128,768]{1,0:T(8,128)(2,1)S(1)} collective-permute-done((bf16[128,768]{1,0:T(8,128)(2,1)}, bf16[128,768]{1,0:T(8,128)(2,1)S(1)}, u32[]{:S(2)}, u32[]{:S(2)}) %collective-permute-start.19) | collective-permute-done | bytes 196640 | tf_op jit(solution)/shard_map/ppermute | solution.py:107
  92.0 9.9 %collective-permute-done.20.refs_2_ = bf16[128,768]{1,0:T(8,128)(2,1)S(1)} collective-permute-done((bf16[128,768]{1,0:T(8,128)(2,1)}, bf16[128,768]{1,0:T(8,128)(2,1)S(1)}, u32[]{:S(2)}, u32[]{:S(2)}) %collective-permute-start.20) | collective-permute-done | bytes 196640 | tf_op jit(solution)/shard_map/ppermute | solution.py:107
  102.7 16.9 %experts.1 = (bf16[512,768]{1,0:T(8,128)(2,1)}, bf16[512,768]{1,0:T(8,128)(2,1)}, bf16[512,128]{1,0:T(8,128)(2,1)}, bf16[512,768]{1,0:T(8,128)(2,1)}, bf16[512,7...) custom-call(bf16[128,768]{1,0:T(8,128)(2,1)} %get-tuple-element.208.refs_0_, ...), custom_call_target="tpu_custom_call" | custom-call | tf_op jit(solution)/shard_map/experts/pallas_call | solution.py:837
  119.5 4.7 %all-to-all-start.1 = ((bf16[4,128,768]{2,1,0:T(8,128)(2,1)}), bf16[4,128,768]{2,1,0:T(8,128)(2,1)S(1)}, u32[]{:S(2)}, u32[]{:S(2)}) async-start(bf16[4,128,768]{2,1,0:T(8,128)(2,1)} %bitcast.51), calls=%async_computation.1 | async-start | bytes 1572864 | tf_op jit(solution)/shard_map/all_to_all | solution.py:983
  124.3 11.2 %expert_grads.1 = (f32[768,128]{1,0:T(8,128)}, bf16[4,384,768]{2,1,0:T(8,128)(2,1)}, bf16[4,384,768]{2,1,0:T(8,128)(2,1)}, bf16[4,384,768]{2,1,0:T(8,128)(2,1)}, bf16[4,384,768]{2,1,0:T(8,128)(2,1)}) custom-call(bf16[512,128]{1,0:T(8,128)(2,1)} %get-tuple-element.214.d_logits_ref, bf16[512,768]{1,0:T(8,128)(2,1)} %get-tuple-element.215.rows_ref, ...), custom_call_target="tpu_custom_call" | custom-call | tf_op jit(solution)/shard_map/expert_grads/pallas_call | solution.py:911
  135.5 7.6 %all-to-all-done.1 = bf16[4,128,768]{2,1,0:T(8,128)(2,1)S(1)} async-done(((bf16[4,128,768]{2,1,0:T(8,128)(2,1)}), bf16[4,128,768]{2,1,0:T(8,128)(2,1)S(1)}, u32[]{:S(2)}, u32[]{:S(2)}) %all-to-all-start.1) | async-done | bytes 786464 | tf_op jit(solution)/shard_map/all_to_all | solution.py:983
  144.0 5.5 %branch.1 = (f32[256,768]{1,0:T(8,128)}, f32[1,768]{1,0:T(1,128)}, bf16[256,192]{1,0:T(8,128)(2,1)}, bf16[256,192]{1,0:T(8,128)(2,1)}, bf16[256,192]{1,0:T(8,128...) custom-call(bf16[512,768]{1,0:T(8,128)(2,1)} %bitcast.44, ...), custom_call_target="tpu_custom_call" | custom-call | tf_op jit(solution)/shard_map/branch/pallas_call | solution.py:92
  154.4 7.3 %merge.1 = (bf16[768,768]{1,0:T(8,128)(2,1)}, bf16[768,384]{1,0:T(8,128)(2,1)}, bf16[768,384]{1,0:T(8,128)(2,1)}, bf16[2,768,384]{2,1,0:T(8,128)(2,1)}, bf16[2,768,384]{2,1,0:T(8,128)(2,1)}) custom-call(bf16[4,384,768]{2,1,0:T(8,128)(2,1)} %get-tuple-element.231.refs_0_, bf16[4,384,768]{2,1,0:T(8,128)(2,1)} %copy-done.10, ...), custom_call_target="tpu_custom_call" | custom-call | tf_op jit(solution)/shard_map/merge/pallas_call | solution.py:411
  164.0 2.4 half_out.1
  170.8 24.9 %attend_back.1 = (bf16[1024,256]{1,0:T(8,128)(2,1)}, f32[1024,512]{1,0:T(8,128)}, bf16[1024,512]{1,0:T(8,128)(2,1)}, f32[8,128]{1,0:T(8,128)}) custom-call(bf16[1024,256]{1,0:T(8,128)(2,1)} %get-tuple-element.183.q_ref, bf16[1040,512]{1,0:T(8,128)(2,1)} %get-tuple-element.186.refs_0_, bf16[1040,512]{1,0:T(8,128)(2,1)} %copy-done.2, ...), custom_call_target="tpu_custom_call" | custom-call | tf_op jit(solution)/shard_map/attend_back/pallas_call | solution.py:92
  196.5 3.5 %all-to-all-start.2 = ((bf16[4,128,768]{2,1,0:T(8,128)(2,1)}), bf16[4,128,768]{2,1,0:T(8,128)(2,1)S(1)}, u32[]{:S(2)}, u32[]{:S(2)}) async-start(bf16[4,128,768]{2,1,0:T(8,128)(2,1)} %bitcast.49), calls=%async_computation.2 | async-start | bytes 1572864 | tf_op jit(solution)/shard_map/all_to_all | solution.py:983
  200.0 2.5 fold.1
  204.5 5.9 %weight.1 = (bf16[1024,768]{1,0:T(8,128)(2,1)}, f32[4,4,24,576]{3,2,1,0:T(8,128)}, bf16[4,4,24,576]{3,2,1,0:T(8,128)(2,1)}) custom-call(bf16[1024,256]{1,0:T(8,128)(2,1)} %get-tuple-element.245.dq_ref, f32[1024,512]{1,0:T(8,128)} %get-tuple-element.246.refs_0_, bf16[1024,512]{1,0:T(8,128)(2,1)} %collective-permute-done.33.refs_1_, ...), custom_call_target="tpu_custom_call" | custom-call | tf_op jit(solution)/shard_map/weight/pallas_call | solution.py:92
  210.4 5.3 %unproject.1 = (f32[256,768]{1,0:T(8,128)}, bf16[256,768]{1,0:T(8,128)(2,1)}, bf16[256,768]{1,0:T(8,128)(2,1)}, bf16[256,768]{1,0:T(8,128)(2,1)}, f32[32,24,128]{2,1,0:T(8,128)}) custom-call(bf16[1024,768]{1,0:T(8,128)(2,1)} %get-tuple-element.260.dp_ref, bf16[768,768]{1,0:T(8,128)(2,1)} %get-tuple-element.261.w_ref, bf16[768]{0:T(1024)(128)(2,1)} %refs_5_.1, ...), custom_call_target="tpu_custom_call" | custom-call | tf_op jit(solution)/shard_map/unproject/pallas_call | solution.py:92
  215.6 5.3 %all-to-all-done.2 = bf16[4,128,768]{2,1,0:T(8,128)(2,1)S(1)} async-done(((bf16[4,128,768]{2,1,0:T(8,128)(2,1)}), bf16[4,128,768]{2,1,0:T(8,128)(2,1)S(1)}, u32[]{:S(2)}, u32[]{:S(2)}) %all-to-all-start.2) | async-done | bytes 786464 | tf_op jit(solution)/shard_map/all_to_all | solution.py:983
  221.0 2.9 %all-to-all-start.3 = ((f32[32,24,128]{2,1,0:T(8,128)}), f32[32,24,128]{2,1,0:T(8,128)S(1)}, u32[]{:S(2)}, u32[]{:S(2)}) async-start(f32[32,24,128]{2,1,0:T(8,128)} %get-tuple-element.299), calls=%async_computation.3 | async-start | bytes 786432 | tf_op jit(solution)/shard_map/all_to_all | solution.py:1244
  227.5 2.6 combine.1
  232.3 4.0 %finish.1 = (f32[96,3072]{1,0:T(8,128)}, f32[384,768]{1,0:T(8,128)}) custom-call(bf16[768,768]{1,0:T(8,128)(2,1)} %get-tuple-element.283.own_ref, bf16[2,768,384]{2,1,0:T(8,128)(2,1)} %copy-done, bf16[2,768,384]{2,1,0:T(8,128)(2,1)} %copy-done.1, bf16[768,384]{1,0:T(8,128)(2,1)} %copy-done.16, bf16[768,384]{1,0:T(8,128)(2,1)} %copy-done.17), custom_call_target="tpu_custom_call" | custom-call | tf_op jit(solution)/shard_map/finish/pallas_call | solution.py:92
  236.4 3.4 %collective-permute-start.39 = (bf16[4,24,576]{2,1,0:T(8,128)(2,1)S(1)}, bf16[4,24,576]{2,1,0:T(8,128)(2,1)S(1)}, u32[]{:S(2)}, u32[]{:S(2)}) collective-permute-start(bf16[4,24,576]{2,1,0:T(8,128)(2,1)S(1)} %copy-done.43), channel_id=1, source_target_pairs={{0,3},{1,2},{2,1},{3,0},{4,7},{5,6},{6,5},{7,4},{8,11},{9,10},{10,... | collective-permute-start | bytes 331784 | tf_op jit(solution)/shard_map/ppermute | solution.py:107
  244.3 4.3 %collective-permute-done.42.refs_3_ = bf16[256,768]{1,0:T(8,128)(2,1)} collective-permute-done((bf16[256,768]{1,0:T(8,128)(2,1)}, bf16[256,768]{1,0:T(8,128)(2,1)}, u32[]{:S(2)}, u32[]{:S(2)}) %collective-permute-start.42) | collective-permute-done | bytes 393248 | tf_op jit(solution)/shard_map/ppermute | solution.py:107
  248.6 3.1 %tokens.1 = bf16[256,768]{1,0:T(8,128)(2,1)} custom-call(f32[256,768]{1,0:T(8,128)} %get-tuple-element.292.refs_0_, bf16[256,768]{1,0:T(8,128)(2,1)} %copy-done.23, bf16[256,768]{1,0:T(8,128)(2,1)} %collective-permute-done.41.refs_2_, bf16[256,768]{1,0:T(8,128)(2,1)} %collective-permute-done.42.refs_3_, bf16[256,768]{1,0:T(8,128)(2,1)} %bitcast.41, ...), custom_call_target="tpu_custom_call" | custom-call | tf_op jit(solution)/shard_map/tokens/pallas_call | solution.py:92
  (195 shorter events, 74.7 us)
Async XLA Ops:
  20.6 16.7 %collective-permute-start.5 = (bf16[272,768]{1,0:T(8,128)(2,1)}, bf16[272,768]{1,0:T(8,128)(2,1)S(1)}, u32[]{:S(2)}, u32[]{:S(2)}) collective-permute-start(bf16[272,768]{1,0:T(8,128)(2,1)} %get-tuple-element.178.refs_0_.refs_2_), channel_id=1, source_target_pairs={{0,24},{4,28},{8,16},{12,20},{16,8},{20,12},{24,0},{28,4},{1,25},{... | collective-permute-start | bytes 1253384 | tf_op jit(solution)/shard_map/ppermute | solution.py:107
  21.1 16.8 %collective-permute-start.4 = (bf16[272,768]{1,0:T(8,128)(2,1)}, bf16[272,768]{1,0:T(8,128)(2,1)S(1)}, u32[]{:S(2)}, u32[]{:S(2)}) collective-permute-start(bf16[272,768]{1,0:T(8,128)(2,1)} %get-tuple-element.178.refs_0_.refs_2_), channel_id=1, source_target_pairs={{0,16},{4,20},{8,24},{12,28},{16,0},{20,4},{24,8},{28,12},{1,17},{... | collective-permute-start | bytes 1253384 | tf_op jit(solution)/shard_map/ppermute | solution.py:107
  22.6 15.3 %collective-permute-start.3 = (bf16[272,768]{1,0:T(8,128)(2,1)}, bf16[272,768]{1,0:T(8,128)(2,1)S(1)}, u32[]{:S(2)}, u32[]{:S(2)}) collective-permute-start(bf16[272,768]{1,0:T(8,128)(2,1)} %get-tuple-element.178.refs_0_.refs_2_), channel_id=1, source_target_pairs={{0,8},{4,12},{8,0},{12,4},{16,24},{20,28},{24,16},{28,20},{1,9},{5... | collective-permute-start | bytes 1253384 | tf_op jit(solution)/shard_map/ppermute | solution.py:107
  24.1 13.1 %collective-permute-start.7 = (bf16[192,576]{1,0:T(8,128)(2,1)S(1)}, bf16[192,576]{1,0:T(8,128)(2,1)S(1)}, u32[]{:S(2)}, u32[]{:S(2)}) collective-permute-start(bf16[192,576]{1,0:T(8,128)(2,1)S(1)} %constant_dynamic-update-slice_fusion), channel_id=1, source_target_pairs={{0,2},{1,3},{2,0},{3,1},{4,6},{5,7},{6,4},{7,5},{8,10},{9,11},{10,... | collective-permute-start | bytes 663560 | tf_op jit(solution)/shard_map/ppermute | solution.py:107
  26.7 10.5 %collective-permute-start.9 = (bf16[48,896]{1,0:T(8,128)(2,1)S(1)}, bf16[48,896]{1,0:T(8,128)(2,1)S(1)}, u32[]{:S(2)}, u32[]{:S(2)}) collective-permute-start(bf16[48,896]{1,0:T(8,128)(2,1)S(1)} %pad_maximum_fusion.4), channel_id=1, source_target_pairs={{0,2},{1,3},{2,0},{3,1},{4,6},{5,7},{6,4},{7,5},{8,10},{9,11},{10,... | collective-permute-start | bytes 258056 | tf_op jit(solution)/shard_map/ppermute | solution.py:107
  38.0 29.8 %all-to-all-start = ((bf16[4,128,768]{2,1,0:T(8,128)(2,1)}), bf16[4,128,768]{2,1,0:T(8,128)(2,1)S(1)}, u32[]{:S(2)}, u32[]{:S(2)}) async-start(bf16[4,128,768]{2,1,0:T(8,128)(2,1)} %bitcast.50), calls=%async_computation | async-start | bytes 1572864 | tf_op jit(solution)/shard_map/all_to_all | solution.py:983
  47.6 20.2 %collective-permute-start.14 = (bf16[96,896]{1,0:T(8,128)(2,1)S(1)}, bf16[96,896]{1,0:T(8,128)(2,1)S(1)}, u32[]{:S(2)}, u32[]{:S(2)}) collective-permute-start(bf16[96,896]{1,0:T(8,128)(2,1)S(1)} %pad_maximum_fusion.2), channel_id=1, source_target_pairs={{0,24},{4,28},{8,16},{12,20},{16,8},{20,12},{24,0},{28,4},{1,25},{... | collective-permute-start | bytes 516104 | tf_op jit(solution)/shard_map/ppermute | solution.py:107
  48.8 19.0 %collective-permute-start.13 = (bf16[96,896]{1,0:T(8,128)(2,1)S(1)}, bf16[96,896]{1,0:T(8,128)(2,1)S(1)}, u32[]{:S(2)}, u32[]{:S(2)}) collective-permute-start(bf16[96,896]{1,0:T(8,128)(2,1)S(1)} %pad_maximum_fusion.2), channel_id=1, source_target_pairs={{0,16},{4,20},{8,24},{12,28},{16,0},{20,4},{24,8},{28,12},{1,17},{... | collective-permute-start | bytes 516104 | tf_op jit(solution)/shard_map/ppermute | solution.py:107
  50.3 17.5 %collective-permute-start.12 = (bf16[96,896]{1,0:T(8,128)(2,1)S(1)}, bf16[96,896]{1,0:T(8,128)(2,1)S(1)}, u32[]{:S(2)}, u32[]{:S(2)}) collective-permute-start(bf16[96,896]{1,0:T(8,128)(2,1)S(1)} %pad_maximum_fusion.2), channel_id=1, source_target_pairs={{0,8},{4,12},{8,0},{12,4},{16,24},{20,28},{24,16},{28,20},{1,9},{5... | collective-permute-start | bytes 516104 | tf_op jit(solution)/shard_map/ppermute | solution.py:107
  84.5 17.4 %collective-permute-start.20 = (bf16[128,768]{1,0:T(8,128)(2,1)}, bf16[128,768]{1,0:T(8,128)(2,1)S(1)}, u32[]{:S(2)}, u32[]{:S(2)}) collective-permute-start(bf16[128,768]{1,0:T(8,128)(2,1)} %get-tuple-element.210), channel_id=1, source_target_pairs={{0,2},{1,3},{2,0},{3,1},{4,6},{5,7},{6,4},{7,5},{8,10},{9,11},{10,... | collective-permute-start | bytes 589832 | tf_op jit(solution)/shard_map/ppermute | solution.py:107
  86.9 15.0 %collective-permute-start.21 = (bf16[128,768]{1,0:T(8,128)(2,1)}, bf16[128,768]{1,0:T(8,128)(2,1)S(1)}, u32[]{:S(2)}, u32[]{:S(2)}) collective-permute-start(bf16[128,768]{1,0:T(8,128)(2,1)} %get-tuple-element.211), channel_id=1, source_target_pairs={{0,3},{1,2},{2,1},{3,0},{4,7},{5,6},{6,5},{7,4},{8,11},{9,10},{10,... | collective-permute-start | bytes 589832 | tf_op jit(solution)/shard_map/ppermute | solution.py:107
  119.5 23.5 %all-to-all-start.1 = ((bf16[4,128,768]{2,1,0:T(8,128)(2,1)}), bf16[4,128,768]{2,1,0:T(8,128)(2,1)S(1)}, u32[]{:S(2)}, u32[]{:S(2)}) async-start(bf16[4,128,768]{2,1,0:T(8,128)(2,1)} %bitcast.51), calls=%async_computation.1 | async-start | bytes 1572864 | tf_op jit(solution)/shard_map/all_to_all | solution.py:983
  149.4 12.3 %collective-permute-start.27 = (bf16[4,4,24,896]{3,2,1,0:T(8,128)(2,1)}, bf16[4,4,24,896]{3,2,1,0:T(8,128)(2,1)S(1)}, u32[]{:S(2)}, u32[]{:S(2)}) collective-permute-start(bf16[4,4,24,896]{3,2,1,0:T(8,128)(2,1)} %get-tuple-element.238), channel_id=1, source_target_pairs={{0,4},{4,0},{8,12},{12,8},{16,20},{20,16},{24,28},{28,24},{1,5},{5... | collective-permute-start | bytes 2064392 | tf_op jit(solution)/shard_map/ppermute | solution.py:107
  149.4 12.3 %collective-permute-start.22 = (bf16[256,192]{1,0:T(8,128)(2,1)}, bf16[256,192]{1,0:T(8,128)(2,1)S(1)}, u32[]{:S(2)}, u32[]{:S(2)}) collective-permute-start(bf16[256,192]{1,0:T(8,128)(2,1)} %get-tuple-element.228), channel_id=1, source_target_pairs={{0,8},{4,12},{8,0},{12,4},{16,24},{20,28},{24,16},{28,20},{1,9},{5... | collective-permute-start | bytes 294920 | tf_op jit(solution)/shard_map/ppermute | solution.py:107
  149.9 11.9 %collective-permute-start.23 = (bf16[256,192]{1,0:T(8,128)(2,1)}, bf16[256,192]{1,0:T(8,128)(2,1)S(1)}, u32[]{:S(2)}, u32[]{:S(2)}) collective-permute-start(bf16[256,192]{1,0:T(8,128)(2,1)} %get-tuple-element.229), channel_id=1, source_target_pairs={{0,16},{4,20},{8,24},{12,28},{16,0},{20,4},{24,8},{28,12},{1,17},{... | collective-permute-start | bytes 294920 | tf_op jit(solution)/shard_map/ppermute | solution.py:107
  151.6 10.2 %collective-permute-start.24 = (bf16[256,192]{1,0:T(8,128)(2,1)}, bf16[256,192]{1,0:T(8,128)(2,1)S(1)}, u32[]{:S(2)}, u32[]{:S(2)}) collective-permute-start(bf16[256,192]{1,0:T(8,128)(2,1)} %get-tuple-element.230), channel_id=1, source_target_pairs={{0,24},{4,28},{8,16},{12,20},{16,8},{20,12},{24,0},{28,4},{1,25},{... | collective-permute-start | bytes 294920 | tf_op jit(solution)/shard_map/ppermute | solution.py:107
  161.8 33.9 %collective-permute-start.28 = (bf16[2,768,384]{2,1,0:T(8,128)(2,1)}, bf16[2,768,384]{2,1,0:T(8,128)(2,1)S(1)}, u32[]{:S(2)}, u32[]{:S(2)}) collective-permute-start(bf16[2,768,384]{2,1,0:T(8,128)(2,1)} %get-tuple-element.248), channel_id=1, source_target_pairs={{0,8},{4,12},{8,0},{12,4},{16,24},{20,28},{24,16},{28,20},{1,9},{5... | collective-permute-start | bytes 3538952 | tf_op jit(solution)/shard_map/ppermute | solution.py:107
  162.9 32.9 %collective-permute-start.29 = (bf16[2,768,384]{2,1,0:T(8,128)(2,1)}, bf16[2,768,384]{2,1,0:T(8,128)(2,1)S(1)}, u32[]{:S(2)}, u32[]{:S(2)}) collective-permute-start(bf16[2,768,384]{2,1,0:T(8,128)(2,1)} %get-tuple-element.249), channel_id=1, source_target_pairs={{0,16},{4,20},{8,24},{12,28},{16,0},{20,4},{24,8},{28,12},{1,17},{... | collective-permute-start | bytes 3538952 | tf_op jit(solution)/shard_map/ppermute | solution.py:107
  166.4 29.3 %collective-permute-start.30 = (bf16[4,24,896]{2,1,0:T(8,128)(2,1)}, bf16[4,24,896]{2,1,0:T(8,128)(2,1)S(1)}, u32[]{:S(2)}, u32[]{:S(2)}) collective-permute-start(bf16[4,24,896]{2,1,0:T(8,128)(2,1)} %get-tuple-element.253), channel_id=1, source_target_pairs={{0,1},{1,0},{2,3},{3,2},{4,5},{5,4},{6,7},{7,6},{8,9},{9,8},{10,11... | collective-permute-start | bytes 516104 | tf_op jit(solution)/shard_map/ppermute | solution.py:107
  166.4 29.3 %collective-permute-start.31 = (bf16[4,24,896]{2,1,0:T(8,128)(2,1)}, bf16[4,24,896]{2,1,0:T(8,128)(2,1)S(1)}, u32[]{:S(2)}, u32[]{:S(2)}) collective-permute-start(bf16[4,24,896]{2,1,0:T(8,128)(2,1)} %get-tuple-element.254), channel_id=1, source_target_pairs={{0,2},{1,3},{2,0},{3,1},{4,6},{5,7},{6,4},{7,5},{8,10},{9,11},{10,... | collective-permute-start | bytes 516104 | tf_op jit(solution)/shard_map/ppermute | solution.py:107
  168.4 27.3 %collective-permute-start.32 = (bf16[4,24,896]{2,1,0:T(8,128)(2,1)}, bf16[4,24,896]{2,1,0:T(8,128)(2,1)S(1)}, u32[]{:S(2)}, u32[]{:S(2)}) collective-permute-start(bf16[4,24,896]{2,1,0:T(8,128)(2,1)} %get-tuple-element.255), channel_id=1, source_target_pairs={{0,3},{1,2},{2,1},{3,0},{4,7},{5,6},{6,5},{7,4},{8,11},{9,10},{10,... | collective-permute-start | bytes 516104 | tf_op jit(solution)/shard_map/ppermute | solution.py:107
  196.5 24.5 %all-to-all-start.2 = ((bf16[4,128,768]{2,1,0:T(8,128)(2,1)}), bf16[4,128,768]{2,1,0:T(8,128)(2,1)S(1)}, u32[]{:S(2)}, u32[]{:S(2)}) async-start(bf16[4,128,768]{2,1,0:T(8,128)(2,1)} %bitcast.49), calls=%async_computation.2 | async-start | bytes 1572864 | tf_op jit(solution)/shard_map/all_to_all | solution.py:983
  202.5 21.4 %collective-permute-start.35 = (bf16[768,384]{1,0:T(8,128)(2,1)}, bf16[768,384]{1,0:T(8,128)(2,1)S(1)}, u32[]{:S(2)}, u32[]{:S(2)}) collective-permute-start(bf16[768,384]{1,0:T(8,128)(2,1)} %get-tuple-element.272), channel_id=1, source_target_pairs={{0,16},{4,20},{8,24},{12,28},{16,0},{20,4},{24,8},{28,12},{1,17},{... | collective-permute-start | bytes 1769480 | tf_op jit(solution)/shard_map/ppermute | solution.py:107
  203.5 20.4 %collective-permute-start.36 = (bf16[768,384]{1,0:T(8,128)(2,1)}, bf16[768,384]{1,0:T(8,128)(2,1)S(1)}, u32[]{:S(2)}, u32[]{:S(2)}) collective-permute-start(bf16[768,384]{1,0:T(8,128)(2,1)} %get-tuple-element.273), channel_id=1, source_target_pairs={{0,8},{4,12},{8,0},{12,4},{16,24},{20,28},{24,16},{28,20},{1,9},{5... | collective-permute-start | bytes 1769480 | tf_op jit(solution)/shard_map/ppermute | solution.py:107
  210.4 13.5 %collective-permute-start.34 = (bf16[4,4,24,576]{3,2,1,0:T(8,128)(2,1)}, bf16[4,4,24,576]{3,2,1,0:T(8,128)(2,1)S(1)}, u32[]{:S(2)}, u32[]{:S(2)}) collective-permute-start(bf16[4,4,24,576]{3,2,1,0:T(8,128)(2,1)} %get-tuple-element.259), channel_id=1, source_target_pairs={{0,4},{4,0},{8,12},{12,8},{16,20},{20,16},{24,28},{28,24},{1,5},{5... | collective-permute-start | bytes 1327112 | tf_op jit(solution)/shard_map/ppermute | solution.py:107
  221.0 20.9 %all-to-all-start.3 = ((f32[32,24,128]{2,1,0:T(8,128)}), f32[32,24,128]{2,1,0:T(8,128)S(1)}, u32[]{:S(2)}, u32[]{:S(2)}) async-start(f32[32,24,128]{2,1,0:T(8,128)} %get-tuple-element.299), calls=%async_computation.3 | async-start | bytes 786432 | tf_op jit(solution)/shard_map/all_to_all | solution.py:1244
  223.9 15.8 %collective-permute-start.40 = (bf16[256,768]{1,0:T(8,128)(2,1)}, bf16[256,768]{1,0:T(8,128)(2,1)S(1)}, u32[]{:S(2)}, u32[]{:S(2)}) collective-permute-start(bf16[256,768]{1,0:T(8,128)(2,1)} %get-tuple-element.293), channel_id=1, source_target_pairs={{0,8},{4,12},{8,0},{12,4},{16,24},{20,28},{24,16},{28,20},{1,9},{5... | collective-permute-start | bytes 1179656 | tf_op jit(solution)/shard_map/ppermute | solution.py:107
  225.6 18.8 %collective-permute-start.41 = (bf16[256,768]{1,0:T(8,128)(2,1)}, bf16[256,768]{1,0:T(8,128)(2,1)}, u32[]{:S(2)}, u32[]{:S(2)}) collective-permute-start(bf16[256,768]{1,0:T(8,128)(2,1)} %get-tuple-element.294), channel_id=1, source_target_pairs={{0,16},{4,20},{8,24},{12,28},{16,0},{20,4},{24,8},{28,12},{1,17},{... | collective-permute-start | bytes 1179656 | tf_op jit(solution)/shard_map/ppermute | solution.py:107
  227.0 21.6 %collective-permute-start.42 = (bf16[256,768]{1,0:T(8,128)(2,1)}, bf16[256,768]{1,0:T(8,128)(2,1)}, u32[]{:S(2)}, u32[]{:S(2)}) collective-permute-start(bf16[256,768]{1,0:T(8,128)(2,1)} %get-tuple-element.295), channel_id=1, source_target_pairs={{0,24},{4,28},{8,16},{12,20},{16,8},{20,12},{24,0},{28,4},{1,25},{... | collective-permute-start | bytes 1179656 | tf_op jit(solution)/shard_map/ppermute | solution.py:107
  236.4 15.3 %collective-permute-start.39 = (bf16[4,24,576]{2,1,0:T(8,128)(2,1)S(1)}, bf16[4,24,576]{2,1,0:T(8,128)(2,1)S(1)}, u32[]{:S(2)}, u32[]{:S(2)}) collective-permute-start(bf16[4,24,576]{2,1,0:T(8,128)(2,1)S(1)} %copy-done.43), channel_id=1, source_target_pairs={{0,3},{1,2},{2,1},{3,0},{4,7},{5,6},{6,5},{7,4},{8,11},{9,10},{10,... | collective-permute-start | bytes 331784 | tf_op jit(solution)/shard_map/ppermute | solution.py:107
  239.8 11.9 %collective-permute-start.37 = (bf16[4,24,576]{2,1,0:T(8,128)(2,1)S(1)}, bf16[4,24,576]{2,1,0:T(8,128)(2,1)S(1)}, u32[]{:S(2)}, u32[]{:S(2)}) collective-permute-start(bf16[4,24,576]{2,1,0:T(8,128)(2,1)S(1)} %copy-done.42), channel_id=1, source_target_pairs={{0,1},{1,0},{2,3},{3,2},{4,5},{5,4},{6,7},{7,6},{8,9},{9,8},{10,11... | collective-permute-start | bytes 331784 | tf_op jit(solution)/shard_map/ppermute | solution.py:107
  239.8 11.9 %collective-permute-start.38 = (bf16[4,24,576]{2,1,0:T(8,128)(2,1)S(1)}, bf16[4,24,576]{2,1,0:T(8,128)(2,1)S(1)}, u32[]{:S(2)}, u32[]{:S(2)}) collective-permute-start(bf16[4,24,576]{2,1,0:T(8,128)(2,1)S(1)} %copy-done.41), channel_id=1, source_target_pairs={{0,2},{1,3},{2,0},{3,1},{4,6},{5,7},{6,4},{7,5},{8,10},{9,11},{10,... | collective-permute-start | bytes 331784 | tf_op jit(solution)/shard_map/ppermute | solution.py:107
  (62 other events, 309.5 us)

commit v3 on v2

--- a/solution.py
+++ b/solution.py
@@ -255,7 +255,7 @@
         grad = dot(mixed_refs[m][...], d_branch, TN)
         grad = jnp.concatenate([grad, rpart_ref[pl.ds(start, part), :]], axis=1)
         if tall % 8 == 0:
-            scatter_rows(info, grad, m, grad_refs, ring, batch, tall, info[2])
+            scatter_rows(info, grad, m, grad_refs, ring, batch, tall, 0)
         else:
             grad_refs[0][pl.ds(start, part), :] = grad
 
@@ -331,18 +331,20 @@
     total = refs[0][...]
     for ref in refs[1:ring]:
         total += ref[...].astype(F32)
-    for m, ref in enumerate(refs[ring:]):
-        ref[...] = total[m].astype(ref.dtype)
-
-
-def quarter_kernel(*refs, batch):
-    one, two = refs[0][...], refs[batch][...]
+    if len(refs) == ring + 1:
+        refs[ring][...] = total.astype(BF16)
+    else:
+        for m, ref in enumerate(refs[ring:]):
+            ref[...] = total[m].astype(ref.dtype)
+
+
+def quarter_kernel(two_ref, *refs, batch):
+    one = refs[0][...]
     for ref in refs[1:batch]:
         one += ref[...].astype(F32)
-    for ref in refs[batch + 1 : 2 * batch]:
-        two += ref[...].astype(F32)
+    two = jnp.sum(two_ref[...].astype(F32), axis=0)
     cut = one.shape[2]
-    for m, ref in enumerate(refs[2 * batch :]):
+    for m, ref in enumerate(refs[batch:]):
         ref[:, :cut] = one[m].astype(BF16)
         ref[:, cut:] = two[m].astype(BF16)
 
@@ -356,7 +358,10 @@
     )
     total = sum(ref[:, cut:].astype(F32) for ref in refs[:groups])
     out_ref[...] = total[:, :width]
-    router_ref[...] = total[:, width:]
+    router = total[:, width:]
+    spare = jnp.zeros((router.shape[1] - router.shape[0], router.shape[1]), F32)
+    router = jnp.concatenate([router, spare], axis=0).T
+    router_ref[...] = router[: router_ref.shape[0], : router_ref.shape[1]]
 
 
 def tokens_kernel(*refs, groups):
@@ -1122,29 +1127,28 @@
     )
     d_mix, out_parts = rest[:groups], rest[groups:]
 
-    def by_place(parts):
+    def by_place(parts, turn):
         if fine:
             return parts
         grad = parts[0].reshape(groups, ring, n_batch, tall, parts[0].shape[1])
         parts = xor_order([grad[:, r] for r in range(ring)], own)
-        parts = [xor_order([p[:, z] for z in range(n_batch)], zed) for p in parts]
+        parts = [xor_order([p[:, z] for z in range(n_batch)], turn) for p in parts]
         parts = [[xor_order([z[g] for g in range(groups)], group) for z in p] for p in parts]
         parts = [jnp.stack([jnp.stack(z) for z in p]) for p in parts]
         return [parts[0]] + [p.astype(BF16) for p in parts[1:]]
 
     d_mix = over_groups(d_mix)
-    out_parts = over_ring(by_place(out_parts))
+    out_parts = over_ring(by_place(out_parts, zed * 0))
     d_mix, grads_one, grads_two, out_parts = lax.optimization_barrier(
         (d_mix, grads_one, grads_two, out_parts)
     )
-    shape = out_parts[0].shape[1:]
-    out_parts = kernel_call(
+    out_part = kernel_call(
         functools.partial(half_kernel, ring=ring),
         "half_out",
         out_parts,
-        [(shape, F32)] + [(shape, BF16)] * (n_batch - 1),
-    )
-    out_parts = over_batch(out_parts)
+        [(out_parts[0].shape, BF16)],
+    )[0]
+    returned = turn_batch(produced)
     grads_one = swap(grads_one, "ctx", n_ctx, ring)
     grads_two = swap(grads_two, "ctx", n_ctx, 2 * ring)
 
@@ -1152,11 +1156,11 @@
         q, kv_all, band, d_mix, out_t, lse, heads, groups, ring, per
     )
     dkv_other, table_part = rest[: ring - 1], rest[ring - 1]
-    dkv_other, grads_one, grads_two, out_parts, produced = lax.optimization_barrier(
-        (dkv_other, grads_one, grads_two, out_parts, produced)
+    dkv_other, grads_one, grads_two, out_part, returned = lax.optimization_barrier(
+        (dkv_other, grads_one, grads_two, out_part, returned)
     )
     dkv_got = over_ring([dkv_own] + dkv_other)[1:]
-    returned = turn_batch(produced)
+    out_part = lax.all_to_all(out_part, "batch", split_axis=0, concat_axis=0, tiled=True)
     last_left, last_right = fold(kept_left, kept_right, grads_one, grads_two)
     last_left = swap(last_left, "ctx", n_ctx, 2 * ring)
     last_right = swap(last_right, "ctx", n_ctx, ring)
@@ -1191,9 +1195,9 @@
         + [((per, width), BF16)] * (groups - 1)
         + [((n_ctx * n_batch, late_rows, lanes), F32)],
     )
-    packed_parts = over_ring(by_place(packed_parts))
-    packed_parts, d_normed, last_left, last_right, returned = lax.optimization_barrier(
-        (packed_parts, d_normed, last_left, last_right, returned)
+    packed_parts = over_ring(by_place(packed_parts, zed))
+    packed_parts, d_normed, last_left, last_right, out_part = lax.optimization_barrier(
+        (packed_parts, d_normed, last_left, last_right, out_part)
     )
     got = over_groups(d_normed)
     shape = packed_parts[0].shape[1:]
@@ -1237,7 +1241,7 @@
     parts = kernel_call(
         functools.partial(quarter_kernel, batch=n_batch),
         "quarter",
-        [*packed_parts, *out_parts],
+        [out_part, *packed_parts],
         [((tall, 3 * part + width + lanes), BF16)] * groups,
     )
 
@@ -1255,9 +1259,9 @@
         functools.partial(columns_kernel, groups=groups, ring=ring, part=part),
         "columns",
         over_groups(parts),
-        [((tall, 3 * width), F32), ((tall, width), F32), ((tall, lanes), F32)],
-    )
-    router_grad = router_grad[:, :n_batch]
+        [((tall, 3 * width), F32), ((tall, width), F32), ((n_batch, tall), F32)],
+    )
+    router_grad = router_grad.T
     return (
         layer_out,
         tokens_grad,

time: 267 us -> 261 us (0.978)
  local copies, waits for them, and re-layouts: 13 us -> 10.2 us
    all_to_all x3, waiting for transfers between devices: 12.9 us -> 7.59 us  [turn_batch(): lax.all_to_all(rows, 'batch', split_axis=0, concat_axis=0, tiled=True)]
    ppermute x46 -> x43, starting transfers between devices: 51.2 us -> 46.9 us  [swap(): return lax.ppermute(value, axis, [(i, i ^ mask) for i in range(size)])]
    all_to_all x0 -> x1, starting transfers between devices: none -> 4.2 us  [body(): lax.all_to_all(out_part, 'batch', split_axis=0, concat_axis=0, tiled=True)]
    all_to_all x0 -> x1, waiting for transfers between devices: none -> 3.63 us  [body(): lax.all_to_all(out_part, 'batch', split_axis=0, concat_axis=0, tiled=True)]
    unnamed x94 -> x87, local copies, waits for them, and re-layouts: 11.7 us -> 8.91 us
    ppermute x46 -> x43, waiting for transfers between devices: 38.2 us -> 38.3 us  [swap(): return lax.ppermute(value, axis, [(i, i ^ mask) for i in range(size)])]
  transfers between devices with their start and end apart: 50 -> 48, of which waited for: 14 -> 14; matrix products, arithmetic and copies ran while one was open for 1% -> 1% of each run, Pallas kernels for 39% -> 40%
where the time goes in v3:
time: 261 us; the launch traced here: 260 us
  Pallas kernels  131 us (50%)
  starting transfers between devices  66.2 us (25%)
  waiting for transfers between devices  49.5 us (19%)
  local copies, waits for them, and re-layouts  10.2 us (4%)
    pallas_call x18, Pallas kernels, kernel_call(): pl.pallas_call(kernel, out_shape=tuple((jax.ShapeDtypeStruct(shape, kind)...  92.9 us
    ppermute x43, starting transfers between devices, swap(): return lax.ppermute(value, axis, [(i, i ^ mask) for i in range(size)])  46.9 us
    ppermute x43, waiting for transfers between devices, swap(): return lax.ppermute(value, axis, [(i, i ^ mask) for i in range(size)])  38.3 us
    pallas_call x1, Pallas kernels, expert_layer(): pl.pallas_call(functools.partial(expert_kernel, experts=batch, ring=ring,...  16.9 us
    all_to_all x3, starting transfers between devices, turn_batch(): lax.all_to_all(rows, 'batch', split_axis=0, concat_axis=0, tiled=True)  12.3 us
    pallas_call x1, Pallas kernels, expert_grads(): pl.pallas_call(functools.partial(expert_grad_kernel, groups=groups, ring=...  11.2 us
    unnamed x87, local copies, waits for them, and re-layouts  8.91 us
    all_to_all x3, waiting for transfers between devices, turn_batch(): lax.all_to_all(rows, 'batch', split_axis=0, concat_axis=0, tiled=True)  7.59 us
  transfers between devices with their start and end apart: 48, of which 14 were waited for; matrix products, arithmetic and copies ran while one was open for 1% of the time, Pallas kernels for 40%

profile of v3, /device:TPU:0, one launch (start us, length us, event | category | flops | bytes accessed | tf_op | source)
XLA Modules:
  0.0 260.5 jit_solution(426354953916275527)
XLA Ops:
  2.7 2.9 %collective-permute-start = (bf16[24,576]{1,0:T(8,128)(2,1)}, bf16[24,576]{1,0:T(8,128)(2,1)S(1)}, u32[]{:S(2)}, u32[]{:S(2)}) collective-permute-start(bf16[24,576]{1,0:T(8,128)(2,1)} %get-tuple-element.160), channel_id=1, source_target_pairs={{0,8},{4,12},{8,0},{12,4},{16,24},{20,28},{24,16},{28,20},{1,9},{5... | collective-permute-start | bytes 82952 | tf_op jit(solution)/shard_map/ppermute | solution.py:107
  15.4 3.6 %collective-permute-done.6 = bf16[96,576]{1,0:T(8,128)(2,1)S(1)} collective-permute-done((bf16[96,576]{1,0:T(8,128)(2,1)S(1)}, bf16[96,576]{1,0:T(8,128)(2,1)S(1)}, u32[]{:S(2)}, u32[]{:S(2)}) %collective-permute-start.6) | collective-permute-done | bytes 110624 | tf_op jit(solution)/shard_map/ppermute | solution.py:107
  24.1 2.6 collective-permute-start.7
  31.2 6.0 %collective-permute-done.9 = bf16[48,896]{1,0:T(8,128)(2,1)S(1)} collective-permute-done((bf16[48,896]{1,0:T(8,128)(2,1)S(1)}, bf16[48,896]{1,0:T(8,128)(2,1)S(1)}, u32[]{:S(2)}, u32[]{:S(2)}) %collective-permute-start.9) | collective-permute-done | bytes 86048 | tf_op jit(solution)/shard_map/ppermute | solution.py:107
  38.0 3.9 %all-to-all-start = ((bf16[4,128,768]{2,1,0:T(8,128)(2,1)}), bf16[4,128,768]{2,1,0:T(8,128)(2,1)S(1)}, u32[]{:S(2)}, u32[]{:S(2)}) async-start(bf16[4,128,768]{2,1,0:T(8,128)(2,1)} %bitcast.50), calls=%async_computation | async-start | bytes 1572864 | tf_op jit(solution)/shard_map/all_to_all | solution.py:988
  42.7 4.6 %project.1 = (bf16[1024,256]{1,0:T(8,128)(2,1)}, bf16[1040,512]{1,0:T(8,128)(2,1)}, bf16[768,768]{1,0:T(8,128)(2,1)}) custom-call(bf16[272,768]{1,0:T(8,128)(2,1)} %get-tuple-element.171.refs_0_.refs_2_, bf16[272,768]{1,0:T(8,128)(2,1)} %copy-done.5, bf16[272,768]{1,0:T(8,128)(2,1)} %copy-done.4, bf16[272,768]{1,0:T(8,128)(2,1)} %copy-done.3, ...), custom_call_target="tpu_custom_call" | custom-call | tf_op jit(solution)/shard_map/project/pallas_call | solution.py:92
  52.0 15.7 %attend.1 = (f32[4,192,256]{2,1,0:T(8,128)}, f32[4,8,256]{2,1,0:T(8,128)}, bf16[256,192]{1,0:T(8,128)(2,1)}, bf16[256,192]{1,0:T(8,128)(2,1)}, bf16[256,192]{1,0:T(8,128)(2,1)}, /*index=5*/bf16[256,192]{1,0:T(8,128)(2,1)}) custom-call(bf16[1024,256]{1,0:T(8,128)(2,1)} %get-tuple-element.176.q_ref, bf16[1040,512]{1,0:T(8,128)(2,1)} %get-tuple-element.179.refs_0_, ...), custom_call_target="tpu_custom_call" | custom-call | tf_op jit(solution)/shard_map/attend/pallas_call | solution.py:92
  72.5 2.8 %gather.1.refs_4_.refs_5_.refs_8_ = bf16[768,896]{1,0:T(8,128)(2,1)} custom-call(bf16[384,896]{1,0:T(8,128)(2,1)} %bitcast.46, bf16[384,896]{1,0:T(8,128)(2,1)} %copy-done.13), custom_call_target="tpu_custom_call" | custom-call | tf_op jit(solution)/shard_map/gather/pallas_call | solution.py:92
  75.2 2.7 %collective-permute-done.16.refs_2_ = bf16[256,192]{1,0:T(8,128)(2,1)S(1)} collective-permute-done((bf16[256,192]{1,0:T(8,128)(2,1)}, bf16[256,192]{1,0:T(8,128)(2,1)S(1)}, u32[]{:S(2)}, u32[]{:S(2)}) %collective-permute-start.16) | collective-permute-done | bytes 98336 | tf_op jit(solution)/shard_map/ppermute | solution.py:107
  78.6 4.1 %middle.1 = (f32[256,768]{1,0:T(8,128)}, f32[256,1]{1,0:T(8,128)}, bf16[128,768]{1,0:T(8,128)(2,1)}, bf16[128,768]{1,0:T(8,128)(2,1)}, bf16[128,768]{1,0:T(8,128)(2,1)}, /*index=5*/bf16[128,768]{1,0:T(8,128)(2,1)}) custom-call(bf16[256,192]{1,0:T(8,128)(2,1)} %get-tuple-element.195.refs_0_, bf16[256,192]{1,0:T(8,128)(2,1)} %copy-done.16, ...), custom_call_target="tpu_custom_call" | custom-call | tf_op jit(solution)/shard_map/middle/pallas_call | solution.py:92
  87.1 4.9 %collective-permute-done.19.refs_1_ = bf16[128,768]{1,0:T(8,128)(2,1)S(1)} collective-permute-done((bf16[128,768]{1,0:T(8,128)(2,1)}, bf16[128,768]{1,0:T(8,128)(2,1)S(1)}, u32[]{:S(2)}, u32[]{:S(2)}) %collective-permute-start.19) | collective-permute-done | bytes 196640 | tf_op jit(solution)/shard_map/ppermute | solution.py:107
  92.0 9.9 %collective-permute-done.20.refs_2_ = bf16[128,768]{1,0:T(8,128)(2,1)S(1)} collective-permute-done((bf16[128,768]{1,0:T(8,128)(2,1)}, bf16[128,768]{1,0:T(8,128)(2,1)S(1)}, u32[]{:S(2)}, u32[]{:S(2)}) %collective-permute-start.20) | collective-permute-done | bytes 196640 | tf_op jit(solution)/shard_map/ppermute | solution.py:107
  102.6 16.9 %experts.1 = (bf16[512,768]{1,0:T(8,128)(2,1)}, bf16[512,768]{1,0:T(8,128)(2,1)}, bf16[512,128]{1,0:T(8,128)(2,1)}, bf16[512,768]{1,0:T(8,128)(2,1)}, bf16[512,7...) custom-call(bf16[128,768]{1,0:T(8,128)(2,1)} %get-tuple-element.201.refs_0_, ...), custom_call_target="tpu_custom_call" | custom-call | tf_op jit(solution)/shard_map/experts/pallas_call | solution.py:842
  119.5 4.9 %all-to-all-start.1 = ((bf16[4,128,768]{2,1,0:T(8,128)(2,1)}), bf16[4,128,768]{2,1,0:T(8,128)(2,1)S(1)}, u32[]{:S(2)}, u32[]{:S(2)}) async-start(bf16[4,128,768]{2,1,0:T(8,128)(2,1)} %bitcast.51), calls=%async_computation.1 | async-start | bytes 1572864 | tf_op jit(solution)/shard_map/all_to_all | solution.py:988
  124.5 11.2 %expert_grads.1 = (f32[768,128]{1,0:T(8,128)}, bf16[4,384,768]{2,1,0:T(8,128)(2,1)}, bf16[4,384,768]{2,1,0:T(8,128)(2,1)}, bf16[4,384,768]{2,1,0:T(8,128)(2,1)}, bf16[4,384,768]{2,1,0:T(8,128)(2,1)}) custom-call(bf16[512,128]{1,0:T(8,128)(2,1)} %get-tuple-element.207.d_logits_ref, bf16[512,768]{1,0:T(8,128)(2,1)} %get-tuple-element.208.rows_ref, ...), custom_call_target="tpu_custom_call" | custom-call | tf_op jit(solution)/shard_map/expert_grads/pallas_call | solution.py:916
  135.6 7.6 %all-to-all-done.1 = bf16[4,128,768]{2,1,0:T(8,128)(2,1)S(1)} async-done(((bf16[4,128,768]{2,1,0:T(8,128)(2,1)}), bf16[4,128,768]{2,1,0:T(8,128)(2,1)S(1)}, u32[]{:S(2)}, u32[]{:S(2)}) %all-to-all-start.1) | async-done | bytes 786464 | tf_op jit(solution)/shard_map/all_to_all | solution.py:988
  144.1 5.2 %branch.1 = (f32[256,768]{1,0:T(8,128)}, f32[1,768]{1,0:T(1,128)}, bf16[256,192]{1,0:T(8,128)(2,1)}, bf16[256,192]{1,0:T(8,128)(2,1)}, bf16[256,192]{1,0:T(8,128...) custom-call(bf16[512,768]{1,0:T(8,128)(2,1)} %bitcast.44, ...), custom_call_target="tpu_custom_call" | custom-call | tf_op jit(solution)/shard_map/branch/pallas_call | solution.py:92
  152.9 3.5 %all-to-all-start.2 = ((bf16[4,128,768]{2,1,0:T(8,128)(2,1)}), bf16[4,128,768]{2,1,0:T(8,128)(2,1)S(1)}, u32[]{:S(2)}, u32[]{:S(2)}) async-start(bf16[4,128,768]{2,1,0:T(8,128)(2,1)} %bitcast.49), calls=%async_computation.2 | async-start | bytes 1572864 | tf_op jit(solution)/shard_map/all_to_all | solution.py:988
  156.4 7.3 %merge.1 = (bf16[768,768]{1,0:T(8,128)(2,1)}, bf16[768,384]{1,0:T(8,128)(2,1)}, bf16[768,384]{1,0:T(8,128)(2,1)}, bf16[2,768,384]{2,1,0:T(8,128)(2,1)}, bf16[2,768,384]{2,1,0:T(8,128)(2,1)}) custom-call(bf16[4,384,768]{2,1,0:T(8,128)(2,1)} %get-tuple-element.224.refs_0_, bf16[4,384,768]{2,1,0:T(8,128)(2,1)} %copy-done.10, ...), custom_call_target="tpu_custom_call" | custom-call | tf_op jit(solution)/shard_map/merge/pallas_call | solution.py:416
  165.9 2.5 half_out.1
  168.4 24.8 %attend_back.1 = (bf16[1024,256]{1,0:T(8,128)(2,1)}, f32[1024,512]{1,0:T(8,128)}, bf16[1024,512]{1,0:T(8,128)(2,1)}, f32[8,128]{1,0:T(8,128)}) custom-call(bf16[1024,256]{1,0:T(8,128)(2,1)} %get-tuple-element.176.q_ref, bf16[1040,512]{1,0:T(8,128)(2,1)} %get-tuple-element.179.refs_0_, bf16[1040,512]{1,0:T(8,128)(2,1)} %copy-done.2, ...), custom_call_target="tpu_custom_call" | custom-call | tf_op jit(solution)/shard_map/attend_back/pallas_call | solution.py:92
  193.4 4.2 %all-to-all-start.3 = ((bf16[4,4,24,896]{3,2,1,0:T(8,128)(2,1)}), bf16[4,4,24,896]{3,2,1,0:T(8,128)(2,1)}, u32[]{:S(2)}, u32[]{:S(2)}) async-start(bf16[4,4,24,896]{3,2,1,0:T(8,128)(2,1)} %half_out.1), calls=%async_computation.3 | async-start | bytes 1376256 | tf_op jit(solution)/shard_map/all_to_all | solution.py:1163
  197.6 2.5 fold.1
  202.1 5.8 %weight.1 = (bf16[1024,768]{1,0:T(8,128)(2,1)}, f32[4,4,24,576]{3,2,1,0:T(8,128)}, bf16[4,4,24,576]{3,2,1,0:T(8,128)(2,1)}) custom-call(bf16[1024,256]{1,0:T(8,128)(2,1)} %get-tuple-element.238.dq_ref, f32[1024,512]{1,0:T(8,128)} %get-tuple-element.239.refs_0_, bf16[1024,512]{1,0:T(8,128)(2,1)} %collective-permute-done.30.refs_1_, ...), custom_call_target="tpu_custom_call" | custom-call | tf_op jit(solution)/shard_map/weight/pallas_call | solution.py:92
  207.9 5.3 %unproject.1 = (f32[256,768]{1,0:T(8,128)}, bf16[256,768]{1,0:T(8,128)(2,1)}, bf16[256,768]{1,0:T(8,128)(2,1)}, bf16[256,768]{1,0:T(8,128)(2,1)}, f32[32,24,128]{2,1,0:T(8,128)}) custom-call(bf16[1024,768]{1,0:T(8,128)(2,1)} %get-tuple-element.249.dp_ref, bf16[768,768]{1,0:T(8,128)(2,1)} %get-tuple-element.250.w_ref, bf16[768]{0:T(1024)(128)(2,1)} %refs_5_.1, ...), custom_call_target="tpu_custom_call" | custom-call | tf_op jit(solution)/shard_map/unproject/pallas_call | solution.py:92
  213.2 3.6 %all-to-all-done.3.two_ref = bf16[4,4,24,896]{3,2,1,0:T(8,128)(2,1)} async-done(((bf16[4,4,24,896]{3,2,1,0:T(8,128)(2,1)}), bf16[4,4,24,896]{3,2,1,0:T(8,128)(2,1)}, u32[]{:S(2)}, u32[]{:S(2)}) %all-to-all-start.3) | async-done | bytes 688160 | tf_op jit(solution)/shard_map/all_to_all | solution.py:1163
  216.8 2.9 %all-to-all-start.4 = ((f32[32,24,128]{2,1,0:T(8,128)}), f32[32,24,128]{2,1,0:T(8,128)S(1)}, u32[]{:S(2)}, u32[]{:S(2)}) async-start(f32[32,24,128]{2,1,0:T(8,128)} %get-tuple-element.288), calls=%async_computation.4 | async-start | bytes 786432 | tf_op jit(solution)/shard_map/all_to_all | solution.py:1248
  223.3 2.6 combine.1
  228.1 4.0 %finish.1 = (f32[96,3072]{1,0:T(8,128)}, f32[384,768]{1,0:T(8,128)}) custom-call(bf16[768,768]{1,0:T(8,128)(2,1)} %get-tuple-element.272.own_ref, bf16[2,768,384]{2,1,0:T(8,128)(2,1)} %copy-done, bf16[2,768,384]{2,1,0:T(8,128)(2,1)} %copy-done.1, bf16[768,384]{1,0:T(8,128)(2,1)} %copy-done.14, bf16[768,384]{1,0:T(8,128)(2,1)} %copy-done.15), custom_call_target="tpu_custom_call" | custom-call | tf_op jit(solution)/shard_map/finish/pallas_call | solution.py:92
  232.2 3.4 %collective-permute-start.36 = (bf16[4,24,576]{2,1,0:T(8,128)(2,1)S(1)}, bf16[4,24,576]{2,1,0:T(8,128)(2,1)S(1)}, u32[]{:S(2)}, u32[]{:S(2)}) collective-permute-start(bf16[4,24,576]{2,1,0:T(8,128)(2,1)S(1)} %copy-done.40), channel_id=1, source_target_pairs={{0,3},{1,2},{2,1},{3,0},{4,7},{5,6},{6,5},{7,4},{8,11},{9,10},{10,... | collective-permute-start | bytes 331784 | tf_op jit(solution)/shard_map/ppermute | solution.py:107
  240.2 4.2 %collective-permute-done.39.refs_3_ = bf16[256,768]{1,0:T(8,128)(2,1)S(1)} collective-permute-done((bf16[256,768]{1,0:T(8,128)(2,1)}, bf16[256,768]{1,0:T(8,128)(2,1)S(1)}, u32[]{:S(2)}, u32[]{:S(2)}) %collective-permute-start.39) | collective-permute-done | bytes 393248 | tf_op jit(solution)/shard_map/ppermute | solution.py:107
  245.1 3.1 %tokens.1 = bf16[256,768]{1,0:T(8,128)(2,1)} custom-call(f32[256,768]{1,0:T(8,128)} %get-tuple-element.281.refs_0_, bf16[256,768]{1,0:T(8,128)(2,1)} %copy-done.21, bf16[256,768]{1,0:T(8,128)(2,1)} %copy-done.22, bf16[256,768]{1,0:T(8,128)(2,1)} %copy-done.23, bf16[256,768]{1,0:T(8,128)(2,1)} %bitcast.41, bf16[768]{0:T(1024)(128)(2,1)} %refs_5_.1, ...), custom_call_target="tpu_custom_call" | custom-call | tf_op jit(solution)/shard_map/tokens/pallas_call | solution.py:92
  (184 shorter events, 70.1 us)
Async XLA Ops:
  20.6 16.7 %collective-permute-start.5 = (bf16[272,768]{1,0:T(8,128)(2,1)}, bf16[272,768]{1,0:T(8,128)(2,1)S(1)}, u32[]{:S(2)}, u32[]{:S(2)}) collective-permute-start(bf16[272,768]{1,0:T(8,128)(2,1)} %get-tuple-element.171.refs_0_.refs_2_), channel_id=1, source_target_pairs={{0,24},{4,28},{8,16},{12,20},{16,8},{20,12},{24,0},{28,4},{1,25},{... | collective-permute-start | bytes 1253384 | tf_op jit(solution)/shard_map/ppermute | solution.py:107
  21.1 16.8 %collective-permute-start.4 = (bf16[272,768]{1,0:T(8,128)(2,1)}, bf16[272,768]{1,0:T(8,128)(2,1)S(1)}, u32[]{:S(2)}, u32[]{:S(2)}) collective-permute-start(bf16[272,768]{1,0:T(8,128)(2,1)} %get-tuple-element.171.refs_0_.refs_2_), channel_id=1, source_target_pairs={{0,16},{4,20},{8,24},{12,28},{16,0},{20,4},{24,8},{28,12},{1,17},{... | collective-permute-start | bytes 1253384 | tf_op jit(solution)/shard_map/ppermute | solution.py:107
  22.6 15.3 %collective-permute-start.3 = (bf16[272,768]{1,0:T(8,128)(2,1)}, bf16[272,768]{1,0:T(8,128)(2,1)S(1)}, u32[]{:S(2)}, u32[]{:S(2)}) collective-permute-start(bf16[272,768]{1,0:T(8,128)(2,1)} %get-tuple-element.171.refs_0_.refs_2_), channel_id=1, source_target_pairs={{0,8},{4,12},{8,0},{12,4},{16,24},{20,28},{24,16},{28,20},{1,9},{5... | collective-permute-start | bytes 1253384 | tf_op jit(solution)/shard_map/ppermute | solution.py:107
  24.1 13.1 %collective-permute-start.7 = (bf16[192,576]{1,0:T(8,128)(2,1)S(1)}, bf16[192,576]{1,0:T(8,128)(2,1)S(1)}, u32[]{:S(2)}, u32[]{:S(2)}) collective-permute-start(bf16[192,576]{1,0:T(8,128)(2,1)S(1)} %constant_dynamic-update-slice_fusion), channel_id=1, source_target_pairs={{0,2},{1,3},{2,0},{3,1},{4,6},{5,7},{6,4},{7,5},{8,10},{9,11},{10,... | collective-permute-start | bytes 663560 | tf_op jit(solution)/shard_map/ppermute | solution.py:107
  26.7 10.5 %collective-permute-start.9 = (bf16[48,896]{1,0:T(8,128)(2,1)S(1)}, bf16[48,896]{1,0:T(8,128)(2,1)S(1)}, u32[]{:S(2)}, u32[]{:S(2)}) collective-permute-start(bf16[48,896]{1,0:T(8,128)(2,1)S(1)} %pad_maximum_fusion.4), channel_id=1, source_target_pairs={{0,2},{1,3},{2,0},{3,1},{4,6},{5,7},{6,4},{7,5},{8,10},{9,11},{10,... | collective-permute-start | bytes 258056 | tf_op jit(solution)/shard_map/ppermute | solution.py:107
  38.0 29.8 %all-to-all-start = ((bf16[4,128,768]{2,1,0:T(8,128)(2,1)}), bf16[4,128,768]{2,1,0:T(8,128)(2,1)S(1)}, u32[]{:S(2)}, u32[]{:S(2)}) async-start(bf16[4,128,768]{2,1,0:T(8,128)(2,1)} %bitcast.50), calls=%async_computation | async-start | bytes 1572864 | tf_op jit(solution)/shard_map/all_to_all | solution.py:988
  47.6 20.2 %collective-permute-start.14 = (bf16[96,896]{1,0:T(8,128)(2,1)S(1)}, bf16[96,896]{1,0:T(8,128)(2,1)S(1)}, u32[]{:S(2)}, u32[]{:S(2)}) collective-permute-start(bf16[96,896]{1,0:T(8,128)(2,1)S(1)} %pad_maximum_fusion.2), channel_id=1, source_target_pairs={{0,24},{4,28},{8,16},{12,20},{16,8},{20,12},{24,0},{28,4},{1,25},{... | collective-permute-start | bytes 516104 | tf_op jit(solution)/shard_map/ppermute | solution.py:107
  48.8 19.0 %collective-permute-start.13 = (bf16[96,896]{1,0:T(8,128)(2,1)S(1)}, bf16[96,896]{1,0:T(8,128)(2,1)S(1)}, u32[]{:S(2)}, u32[]{:S(2)}) collective-permute-start(bf16[96,896]{1,0:T(8,128)(2,1)S(1)} %pad_maximum_fusion.2), channel_id=1, source_target_pairs={{0,16},{4,20},{8,24},{12,28},{16,0},{20,4},{24,8},{28,12},{1,17},{... | collective-permute-start | bytes 516104 | tf_op jit(solution)/shard_map/ppermute | solution.py:107
  50.3 17.5 %collective-permute-start.12 = (bf16[96,896]{1,0:T(8,128)(2,1)S(1)}, bf16[96,896]{1,0:T(8,128)(2,1)S(1)}, u32[]{:S(2)}, u32[]{:S(2)}) collective-permute-start(bf16[96,896]{1,0:T(8,128)(2,1)S(1)} %pad_maximum_fusion.2), channel_id=1, source_target_pairs={{0,8},{4,12},{8,0},{12,4},{16,24},{20,28},{24,16},{28,20},{1,9},{5... | collective-permute-start | bytes 516104 | tf_op jit(solution)/shard_map/ppermute | solution.py:107
  82.7 9.2 %collective-permute-start.19 = (bf16[128,768]{1,0:T(8,128)(2,1)}, bf16[128,768]{1,0:T(8,128)(2,1)S(1)}, u32[]{:S(2)}, u32[]{:S(2)}) collective-permute-start(bf16[128,768]{1,0:T(8,128)(2,1)} %get-tuple-element.202), channel_id=1, source_target_pairs={{0,1},{1,0},{2,3},{3,2},{4,5},{5,4},{6,7},{7,6},{8,9},{9,8},{10,11... | collective-permute-start | bytes 589832 | tf_op jit(solution)/shard_map/ppermute | solution.py:107
  84.5 17.4 %collective-permute-start.20 = (bf16[128,768]{1,0:T(8,128)(2,1)}, bf16[128,768]{1,0:T(8,128)(2,1)S(1)}, u32[]{:S(2)}, u32[]{:S(2)}) collective-permute-start(bf16[128,768]{1,0:T(8,128)(2,1)} %get-tuple-element.203), channel_id=1, source_target_pairs={{0,2},{1,3},{2,0},{3,1},{4,6},{5,7},{6,4},{7,5},{8,10},{9,11},{10,... | collective-permute-start | bytes 589832 | tf_op jit(solution)/shard_map/ppermute | solution.py:107
  85.5 16.4 %collective-permute-start.21 = (bf16[128,768]{1,0:T(8,128)(2,1)}, bf16[128,768]{1,0:T(8,128)(2,1)S(1)}, u32[]{:S(2)}, u32[]{:S(2)}) collective-permute-start(bf16[128,768]{1,0:T(8,128)(2,1)} %get-tuple-element.204), channel_id=1, source_target_pairs={{0,3},{1,2},{2,1},{3,0},{4,7},{5,6},{6,5},{7,4},{8,11},{9,10},{10,... | collective-permute-start | bytes 589832 | tf_op jit(solution)/shard_map/ppermute | solution.py:107
  119.5 23.7 %all-to-all-start.1 = ((bf16[4,128,768]{2,1,0:T(8,128)(2,1)}), bf16[4,128,768]{2,1,0:T(8,128)(2,1)S(1)}, u32[]{:S(2)}, u32[]{:S(2)}) async-start(bf16[4,128,768]{2,1,0:T(8,128)(2,1)} %bitcast.51), calls=%async_computation.1 | async-start | bytes 1572864 | tf_op jit(solution)/shard_map/all_to_all | solution.py:988
  143.2 13.1 %collective-permute-start.26 = (bf16[4,384,768]{2,1,0:T(8,128)(2,1)}, bf16[4,384,768]{2,1,0:T(8,128)(2,1)}, u32[]{:S(2)}, u32[]{:S(2)}) collective-permute-start(bf16[4,384,768]{2,1,0:T(8,128)(2,1)} %get-tuple-element.227), channel_id=1, source_target_pairs={{0,4},{4,0},{8,12},{12,8},{16,20},{20,16},{24,28},{28,24},{1,5},{5... | collective-permute-start | bytes 7077896 | tf_op jit(solution)/shard_map/ppermute | solution.py:107
  149.3 14.5 %collective-permute-start.27 = (bf16[4,4,24,896]{3,2,1,0:T(8,128)(2,1)}, bf16[4,4,24,896]{3,2,1,0:T(8,128)(2,1)}, u32[]{:S(2)}, u32[]{:S(2)}) collective-permute-start(bf16[4,4,24,896]{3,2,1,0:T(8,128)(2,1)} %get-tuple-element.231), channel_id=1, source_target_pairs={{0,4},{4,0},{8,12},{12,8},{16,20},{20,16},{24,28},{28,24},{1,5},{5... | collective-permute-start | bytes 2064392 | tf_op jit(solution)/shard_map/ppermute | solution.py:107
  149.3 14.4 %collective-permute-start.22 = (bf16[256,192]{1,0:T(8,128)(2,1)}, bf16[256,192]{1,0:T(8,128)(2,1)S(1)}, u32[]{:S(2)}, u32[]{:S(2)}) collective-permute-start(bf16[256,192]{1,0:T(8,128)(2,1)} %get-tuple-element.221), channel_id=1, source_target_pairs={{0,8},{4,12},{8,0},{12,4},{16,24},{20,28},{24,16},{28,20},{1,9},{5... | collective-permute-start | bytes 294920 | tf_op jit(solution)/shard_map/ppermute | solution.py:107
  149.7 14.1 %collective-permute-start.23 = (bf16[256,192]{1,0:T(8,128)(2,1)}, bf16[256,192]{1,0:T(8,128)(2,1)S(1)}, u32[]{:S(2)}, u32[]{:S(2)}) collective-permute-start(bf16[256,192]{1,0:T(8,128)(2,1)} %get-tuple-element.222), channel_id=1, source_target_pairs={{0,16},{4,20},{8,24},{12,28},{16,0},{20,4},{24,8},{28,12},{1,17},{... | collective-permute-start | bytes 294920 | tf_op jit(solution)/shard_map/ppermute | solution.py:107
  151.5 12.3 %collective-permute-start.24 = (bf16[256,192]{1,0:T(8,128)(2,1)}, bf16[256,192]{1,0:T(8,128)(2,1)S(1)}, u32[]{:S(2)}, u32[]{:S(2)}) collective-permute-start(bf16[256,192]{1,0:T(8,128)(2,1)} %get-tuple-element.223), channel_id=1, source_target_pairs={{0,24},{4,28},{8,16},{12,20},{16,8},{20,12},{24,0},{28,4},{1,25},{... | collective-permute-start | bytes 294920 | tf_op jit(solution)/shard_map/ppermute | solution.py:107
  152.9 40.4 %all-to-all-start.2 = ((bf16[4,128,768]{2,1,0:T(8,128)(2,1)}), bf16[4,128,768]{2,1,0:T(8,128)(2,1)S(1)}, u32[]{:S(2)}, u32[]{:S(2)}) async-start(bf16[4,128,768]{2,1,0:T(8,128)(2,1)} %bitcast.49), calls=%async_computation.2 | async-start | bytes 1572864 | tf_op jit(solution)/shard_map/all_to_all | solution.py:988
  163.8 29.5 %collective-permute-start.28 = (bf16[2,768,384]{2,1,0:T(8,128)(2,1)}, bf16[2,768,384]{2,1,0:T(8,128)(2,1)S(1)}, u32[]{:S(2)}, u32[]{:S(2)}) collective-permute-start(bf16[2,768,384]{2,1,0:T(8,128)(2,1)} %get-tuple-element.241), channel_id=1, source_target_pairs={{0,8},{4,12},{8,0},{12,4},{16,24},{20,28},{24,16},{28,20},{1,9},{5... | collective-permute-start | bytes 3538952 | tf_op jit(solution)/shard_map/ppermute | solution.py:107
  164.6 28.7 %collective-permute-start.29 = (bf16[2,768,384]{2,1,0:T(8,128)(2,1)}, bf16[2,768,384]{2,1,0:T(8,128)(2,1)S(1)}, u32[]{:S(2)}, u32[]{:S(2)}) collective-permute-start(bf16[2,768,384]{2,1,0:T(8,128)(2,1)} %get-tuple-element.242), channel_id=1, source_target_pairs={{0,16},{4,20},{8,24},{12,28},{16,0},{20,4},{24,8},{28,12},{1,17},{... | collective-permute-start | bytes 3538952 | tf_op jit(solution)/shard_map/ppermute | solution.py:107
  193.4 23.4 %all-to-all-start.3 = ((bf16[4,4,24,896]{3,2,1,0:T(8,128)(2,1)}), bf16[4,4,24,896]{3,2,1,0:T(8,128)(2,1)}, u32[]{:S(2)}, u32[]{:S(2)}) async-start(bf16[4,4,24,896]{3,2,1,0:T(8,128)(2,1)} %half_out.1), calls=%async_computation.3 | async-start | bytes 1376256 | tf_op jit(solution)/shard_map/all_to_all | solution.py:1163
  200.2 19.6 %collective-permute-start.32 = (bf16[768,384]{1,0:T(8,128)(2,1)}, bf16[768,384]{1,0:T(8,128)(2,1)S(1)}, u32[]{:S(2)}, u32[]{:S(2)}) collective-permute-start(bf16[768,384]{1,0:T(8,128)(2,1)} %get-tuple-element.261), channel_id=1, source_target_pairs={{0,16},{4,20},{8,24},{12,28},{16,0},{20,4},{24,8},{28,12},{1,17},{... | collective-permute-start | bytes 1769480 | tf_op jit(solution)/shard_map/ppermute | solution.py:107
  200.8 18.9 %collective-permute-start.33 = (bf16[768,384]{1,0:T(8,128)(2,1)}, bf16[768,384]{1,0:T(8,128)(2,1)S(1)}, u32[]{:S(2)}, u32[]{:S(2)}) collective-permute-start(bf16[768,384]{1,0:T(8,128)(2,1)} %get-tuple-element.262), channel_id=1, source_target_pairs={{0,8},{4,12},{8,0},{12,4},{16,24},{20,28},{24,16},{28,20},{1,9},{5... | collective-permute-start | bytes 1769480 | tf_op jit(solution)/shard_map/ppermute | solution.py:107
  207.9 11.8 %collective-permute-start.31 = (bf16[4,4,24,576]{3,2,1,0:T(8,128)(2,1)}, bf16[4,4,24,576]{3,2,1,0:T(8,128)(2,1)S(1)}, u32[]{:S(2)}, u32[]{:S(2)}) collective-permute-start(bf16[4,4,24,576]{3,2,1,0:T(8,128)(2,1)} %get-tuple-element.248), channel_id=1, source_target_pairs={{0,4},{4,0},{8,12},{12,8},{16,20},{20,16},{24,28},{28,24},{1,5},{5... | collective-permute-start | bytes 1327112 | tf_op jit(solution)/shard_map/ppermute | solution.py:107
  216.8 20.9 %all-to-all-start.4 = ((f32[32,24,128]{2,1,0:T(8,128)}), f32[32,24,128]{2,1,0:T(8,128)S(1)}, u32[]{:S(2)}, u32[]{:S(2)}) async-start(f32[32,24,128]{2,1,0:T(8,128)} %get-tuple-element.288), calls=%async_computation.4 | async-start | bytes 786432 | tf_op jit(solution)/shard_map/all_to_all | solution.py:1248
  219.8 15.8 %collective-permute-start.37 = (bf16[256,768]{1,0:T(8,128)(2,1)}, bf16[256,768]{1,0:T(8,128)(2,1)S(1)}, u32[]{:S(2)}, u32[]{:S(2)}) collective-permute-start(bf16[256,768]{1,0:T(8,128)(2,1)} %get-tuple-element.282), channel_id=1, source_target_pairs={{0,8},{4,12},{8,0},{12,4},{16,24},{20,28},{24,16},{28,20},{1,9},{5... | collective-permute-start | bytes 1179656 | tf_op jit(solution)/shard_map/ppermute | solution.py:107
  221.4 18.8 %collective-permute-start.38 = (bf16[256,768]{1,0:T(8,128)(2,1)}, bf16[256,768]{1,0:T(8,128)(2,1)S(1)}, u32[]{:S(2)}, u32[]{:S(2)}) collective-permute-start(bf16[256,768]{1,0:T(8,128)(2,1)} %get-tuple-element.283), channel_id=1, source_target_pairs={{0,16},{4,20},{8,24},{12,28},{16,0},{20,4},{24,8},{28,12},{1,17},{... | collective-permute-start | bytes 1179656 | tf_op jit(solution)/shard_map/ppermute | solution.py:107
  222.9 21.5 %collective-permute-start.39 = (bf16[256,768]{1,0:T(8,128)(2,1)}, bf16[256,768]{1,0:T(8,128)(2,1)S(1)}, u32[]{:S(2)}, u32[]{:S(2)}) collective-permute-start(bf16[256,768]{1,0:T(8,128)(2,1)} %get-tuple-element.284), channel_id=1, source_target_pairs={{0,24},{4,28},{8,16},{12,20},{16,8},{20,12},{24,0},{28,4},{1,25},{... | collective-permute-start | bytes 1179656 | tf_op jit(solution)/shard_map/ppermute | solution.py:107
  232.2 16.0 %collective-permute-start.36 = (bf16[4,24,576]{2,1,0:T(8,128)(2,1)S(1)}, bf16[4,24,576]{2,1,0:T(8,128)(2,1)S(1)}, u32[]{:S(2)}, u32[]{:S(2)}) collective-permute-start(bf16[4,24,576]{2,1,0:T(8,128)(2,1)S(1)} %copy-done.40), channel_id=1, source_target_pairs={{0,3},{1,2},{2,1},{3,0},{4,7},{5,6},{6,5},{7,4},{8,11},{9,10},{10,... | collective-permute-start | bytes 331784 | tf_op jit(solution)/shard_map/ppermute | solution.py:107
  235.6 12.6 %collective-permute-start.34 = (bf16[4,24,576]{2,1,0:T(8,128)(2,1)S(1)}, bf16[4,24,576]{2,1,0:T(8,128)(2,1)S(1)}, u32[]{:S(2)}, u32[]{:S(2)}) collective-permute-start(bf16[4,24,576]{2,1,0:T(8,128)(2,1)S(1)} %copy-done.39), channel_id=1, source_target_pairs={{0,1},{1,0},{2,3},{3,2},{4,5},{5,4},{6,7},{7,6},{8,9},{9,8},{10,11... | collective-permute-start | bytes 331784 | tf_op jit(solution)/shard_map/ppermute | solution.py:107
  235.6 12.6 %collective-permute-start.35 = (bf16[4,24,576]{2,1,0:T(8,128)(2,1)S(1)}, bf16[4,24,576]{2,1,0:T(8,128)(2,1)S(1)}, u32[]{:S(2)}, u32[]{:S(2)}) collective-permute-start(bf16[4,24,576]{2,1,0:T(8,128)(2,1)S(1)} %copy-done.38), channel_id=1, source_target_pairs={{0,2},{1,3},{2,0},{3,1},{4,6},{5,7},{6,4},{7,5},{8,10},{9,11},{10,... | collective-permute-start | bytes 331784 | tf_op jit(solution)/shard_map/ppermute | solution.py:107
  (57 other events, 283.4 us)

commit v4 on v3

--- a/solution.py
+++ b/solution.py
@@ -386,50 +386,38 @@
     out_ref[...] = (middle_ref[...] + gate_ref[...] * returned).astype(BF16)
 
 
+def ring_total(refs):
+    return sum(ref[...].astype(F32) for ref in refs)
+
+
 def merge_kernel(*refs, ring):
-    g1_refs, g2_refs = refs[:ring], refs[ring : 2 * ring]
-    own_ref, left_ref, right_ref, one_ref, two_ref = refs[2 * ring :]
-    step = pl.program_id(0)
-    g1 = sum(ref[...].astype(F32) for ref in g1_refs).astype(BF16)
-    g2 = sum(ref[...].astype(F32) for ref in g2_refs).astype(BF16)
-    rows, half = g1.shape[0], g1.shape[1] // 2
-
-    def put(ref, cut):
-        ref[:rows, :] = g1[:, cut]
-        ref[rows:, :] = g2[:, cut]
-
-    left, right = slice(0, half), slice(half, 2 * half)
-    pl.when(step <= 1)(lambda: put(one_ref, left))
-    pl.when((step == 1) | (step == 2))(lambda: put(two_ref, right))
-    pl.when(step == 0)(lambda: put(right_ref, right))
-    pl.when(step == 2)(lambda: put(left_ref, left))
-    pl.when(step == 3)(lambda: put(own_ref, slice(0, 2 * half)))
+    one_ref, two_ref = refs[2 * ring :]
+    g1, g2 = ring_total(refs[:ring]).astype(BF16), ring_total(refs[ring : 2 * ring]).astype(BF16)
+    rows = g1.shape[0]
+
+    def put(ref):
+        ref[:rows, :] = g1
+        ref[rows:, :] = g2
+
+    pl.when(pl.program_id(0) <= 1)(lambda: put(one_ref))
+    pl.when(pl.program_id(0) >= 2)(lambda: put(two_ref))
 
 
 def merge(g1, g2):
     groups, rows, width = g1[0].shape
     assert groups == 4
     ring = len(g1)
-    tall, half = 2 * rows, width // 2
-    order = lambda s: (jnp.where(s == 0, 1, jnp.where(s == 1, 3, jnp.where(s == 2, 2, 0))), 0, 0)
-    block = lambda columns: pl.BlockSpec((tall, columns), lambda s: (0, 0))
+    half = width // 2
+    order = lambda s: (jnp.where(s == 0, 1, jnp.where(s == 3, 2, 3)), 0, jnp.where(s >= 2, 1, 0))
+    message = jax.ShapeDtypeStruct((2, 2 * rows, half), BF16)
     return pl.pallas_call(
         functools.partial(merge_kernel, ring=ring),
         grid=(groups,),
-        out_shape=(
-            jax.ShapeDtypeStruct((tall, width), BF16),
-            jax.ShapeDtypeStruct((tall, half), BF16),
-            jax.ShapeDtypeStruct((tall, half), BF16),
-            jax.ShapeDtypeStruct((2, tall, half), BF16),
-            jax.ShapeDtypeStruct((2, tall, half), BF16),
-        ),
-        in_specs=[pl.BlockSpec((None, rows, width), order)] * (2 * ring),
+        out_shape=(message, message),
+        in_specs=[pl.BlockSpec((None, rows, half), order)] * (2 * ring),
         out_specs=[
-            block(width),
-            block(half),
-            block(half),
-            pl.BlockSpec((None, tall, half), lambda s: (jnp.minimum(s, 1), 0, 0)),
-            pl.BlockSpec((None, tall, half), lambda s: (jnp.where(s <= 1, 1, 0), 0, 0)),
+            pl.BlockSpec((None, 2 * rows, half), lambda s: (jnp.minimum(s, 1), 0, 0)),
+            pl.BlockSpec((None, 2 * rows, half), lambda s: (jnp.where(s <= 2, 1, 0), 0, 0)),
         ],
         compiler_params=pltpu.CompilerParams(
             dimension_semantics=("arbitrary",), vmem_limit_bytes=56 << 20
@@ -438,36 +426,69 @@
     )(*g1, *g2)
 
 
-def fold_kernel(left_ref, right_ref, one_ref, two_ref, left_out, right_out):
-    left_out[...] = (left_ref[...].astype(F32) + one_ref[...].astype(F32)).astype(BF16)
-    right_out[...] = (right_ref[...].astype(F32) + two_ref[...].astype(F32)).astype(BF16)
-
-
-def fold(left, right, one, two):
-    tall, half = left.shape
-    steps = 2
-    plain = pl.BlockSpec((tall // steps, half), lambda s: (s, 0))
-    second = pl.BlockSpec((None, tall // steps, half), lambda s: (1, s, 0))
+def fold_kernel(*refs, ring):
+    one_ref, two_ref, left_out, right_out = refs[4 * ring :]
+    rows = refs[0].shape[0]
+    for k, (add_ref, ref) in enumerate(((one_ref, left_out), (two_ref, right_out))):
+        for part in range(2):
+            at = (2 * k + part) * ring
+            cut = slice(part * rows, (part + 1) * rows)
+            ref[cut, :] = (ring_total(refs[at : at + ring]) + add_ref[cut, :].astype(F32)).astype(BF16)
+
+
+def fold(g1, g2, one, two):
+    rows, half = g1[0].shape[1], one.shape[2]
+    ring = len(g1)
+    left = pl.BlockSpec((None, rows, half), lambda s: (2, 0, 0))
+    right = pl.BlockSpec((None, rows, half), lambda s: (1, 0, 1))
+    second = pl.BlockSpec((None, 2 * rows, half), lambda s: (1, 0, 0))
+    whole = pl.BlockSpec((2 * rows, half), lambda s: (0, 0))
     return pl.pallas_call(
-        fold_kernel,
-        grid=(steps,),
-        out_shape=(jax.ShapeDtypeStruct((tall, half), BF16),) * 2,
-        in_specs=[plain, plain, second, second],
-        out_specs=[plain, plain],
-        compiler_params=pltpu.CompilerParams(dimension_semantics=("arbitrary",)),
+        functools.partial(fold_kernel, ring=ring),
+        grid=(1,),
+        out_shape=(jax.ShapeDtypeStruct((2 * rows, half), BF16),) * 2,
+        in_specs=[left] * (2 * ring) + [right] * (2 * ring) + [second] * 2,
+        out_specs=[whole] * 2,
+        compiler_params=pltpu.CompilerParams(vmem_limit_bytes=56 << 20),
         name="fold",
-    )(left, right, one, two)
-
-
-def finish_kernel(own_ref, one_ref, two_ref, left_ref, right_ref, in_ref, out_ref):
+    )(*g1, *g2, *g1, *g2, one, two)
+
+
+def finish_kernel(*refs, ring):
+    one_ref, two_ref, left_ref, right_ref, in_ref, out_ref = refs[2 * ring :]
     tall, width = in_ref.shape[0], out_ref.shape[1]
     half, rows = width // 2, out_ref.shape[0]
+    g1, g2 = ring_total(refs[:ring]), ring_total(refs[ring : 2 * ring])
     for at, first_ref, last_ref in ((0, one_ref, left_ref), (half, two_ref, right_ref)):
         cut = slice(at, at + half)
-        total = own_ref[:, cut].astype(F32) + first_ref[0].astype(F32) + last_ref[...].astype(F32)
+        more = first_ref[...].astype(F32) + last_ref[...].astype(F32)
+        total = g1[:, cut] + more[:rows, :]
         for j in range(in_ref.shape[1] // width):
             in_ref[:, j * width + at : j * width + at + half] = total[j * tall : (j + 1) * tall, :]
-        out_ref[:, cut] = total[rows:, :]
+        out_ref[:, cut] = g2[:, cut] + more[rows:, :]
+
+
+def finish(g1, g2, one, two, left, right, tall, hidden):
+    rows, width = g1[0].shape[1:]
+    ring, half = len(g1), width // 2
+    mine = pl.BlockSpec((None, rows, width), lambda s: (0, 0, 0))
+    first = pl.BlockSpec((None, 2 * rows, half), lambda s: (0, 0, 0))
+    whole = pl.BlockSpec((2 * rows, half), lambda s: (0, 0))
+    return pl.pallas_call(
+        functools.partial(finish_kernel, ring=ring),
+        grid=(1,),
+        out_shape=(
+            jax.ShapeDtypeStruct((tall, hidden), F32),
+            jax.ShapeDtypeStruct((rows, width), F32),
+        ),
+        in_specs=[mine] * (2 * ring) + [first] * 2 + [whole] * 2,
+        out_specs=[
+            pl.BlockSpec((tall, hidden), lambda s: (0, 0)),
+            pl.BlockSpec((rows, width), lambda s: (0, 0)),
+        ],
+        compiler_params=pltpu.CompilerParams(vmem_limit_bytes=56 << 20),
+        name="finish",
+    )(*g1, *g2, one, two, left, right)
 
 
 SEGMENTS = 8
@@ -1105,7 +1126,7 @@
 
     back, g1, g2 = lax.optimization_barrier((back, g1, g2))
     g1, g2 = over_ring(g1), over_ring(g2)
-    kept, kept_left, kept_right, grads_one, grads_two = merge(g1, g2)
+    grads_one, grads_two = merge(g1, g2)
     sums_shape = (n_batch, groups, tall, width + lanes)
     sums_shape = (
         [(sums_shape, F32)] + [(sums_shape, BF16)] * (ring - 1)
@@ -1161,7 +1182,7 @@
     )
     dkv_got = over_ring([dkv_own] + dkv_other)[1:]
     out_part = lax.all_to_all(out_part, "batch", split_axis=0, concat_axis=0, tiled=True)
-    last_left, last_right = fold(kept_left, kept_right, grads_one, grads_two)
+    last_left, last_right = fold(g1, g2, grads_one, grads_two)
     last_left = swap(last_left, "ctx", n_ctx, 2 * ring)
     last_right = swap(last_right, "ctx", n_ctx, ring)
 
@@ -1214,30 +1235,27 @@
         [returned, pick_t, middle, gate],
         [((per, width), BF16)],
     )[0][None]
-    expert_in_grad, expert_out_grad = kernel_call(
-        finish_kernel,
-        "finish",
-        [kept, grads_one, grads_two, last_left, last_right],
-        [
-            ((width // n_ctx, expert_in.shape[2]), F32),
-            ((expert_out.shape[1] // n_ctx, width), F32),
-        ],
-    )
-    packed_parts[-1], layer_out, expert_in_grad, expert_out_grad = lax.optimization_barrier(
-        (packed_parts[-1], layer_out, expert_in_grad, expert_out_grad)
+    expert_in_grad, expert_out_grad = finish(
+        g1,
+        g2,
+        grads_one,
+        grads_two,
+        last_left,
+        last_right,
+        width // n_ctx,
+        expert_in.shape[2],
+    )
+    packed_parts[1], layer_out, expert_in_grad, expert_out_grad = lax.optimization_barrier(
+        (packed_parts[1], layer_out, expert_in_grad, expert_out_grad)
     )
     packed_parts = over_batch(packed_parts)
+    packed_parts, got = lax.optimization_barrier((packed_parts, got))
     tokens_grad = kernel_call(
         functools.partial(tokens_kernel, groups=groups),
         "tokens",
         [*got, tokens[0], attn_gain, d_middle],
         [((per, width), BF16)],
     )[0][None]
-    packed_parts, layer_out, expert_in_grad, expert_out_grad, tokens_grad = (
-        lax.optimization_barrier(
-            (packed_parts, layer_out, expert_in_grad, expert_out_grad, tokens_grad)
-        )
-    )
     parts = kernel_call(
         functools.partial(quarter_kernel, batch=n_batch),
         "quarter",

time: 261 us -> 256 us (0.981)
  waiting for transfers between devices: 49.5 us -> 44.3 us
    pallas_call x1 -> x2, Pallas kernels: 2.52 us -> 7.38 us  [the longest x1 4.16 us: finish(): pl.pallas_call(functools.partial(finish_kernel, ring=ring), grid=(1,), ou...]
    ppermute x43, waiting for transfers between devices: 38.3 us -> 34 us  [swap(): return lax.ppermute(value, axis, [(i, i ^ mask) for i in range(size)])]
    pallas_call x18 -> x17, Pallas kernels: 92.9 us -> 88.8 us  [kernel_call(): pl.pallas_call(kernel, out_shape=tuple((jax.ShapeDtypeStruct(shape, kind)...]
    unnamed x87 -> x85, local copies, waits for them, and re-layouts: 8.91 us -> 8.09 us
  transfers between devices with their start and end apart: 48 -> 48, of which waited for: 14 -> 13; matrix products, arithmetic and copies ran while one was open for 1% -> 2% of each run, Pallas kernels for 40% -> 40%
where the time goes in v4:
time: 256 us; the launch traced here: 255 us
  Pallas kernels  129 us (50%)
  starting transfers between devices  67.9 us (27%)
  waiting for transfers between devices  44.3 us (17%)
  local copies, waits for them, and re-layouts  10 us (4%)
    pallas_call x17, Pallas kernels, kernel_call(): pl.pallas_call(kernel, out_shape=tuple((jax.ShapeDtypeStruct(shape, kind)...  88.8 us
    ppermute x43, starting transfers between devices, swap(): return lax.ppermute(value, axis, [(i, i ^ mask) for i in range(size)])  48.7 us
    ppermute x43, waiting for transfers between devices, swap(): return lax.ppermute(value, axis, [(i, i ^ mask) for i in range(size)])  34 us
    pallas_call x1, Pallas kernels, expert_layer(): pl.pallas_call(functools.partial(expert_kernel, experts=batch, ring=ring,...  16.8 us
    all_to_all x3, starting transfers between devices, turn_batch(): lax.all_to_all(rows, 'batch', split_axis=0, concat_axis=0, tiled=True)  12.1 us
    pallas_call x1, Pallas kernels, expert_grads(): pl.pallas_call(functools.partial(expert_grad_kernel, groups=groups, ring=...  11.2 us
    unnamed x85, local copies, waits for them, and re-layouts  8.09 us
    all_to_all x3, waiting for transfers between devices, turn_batch(): lax.all_to_all(rows, 'batch', split_axis=0, concat_axis=0, tiled=True)  7.54 us
  transfers between devices with their start and end apart: 48, of which 13 were waited for; matrix products, arithmetic and copies ran while one was open for 2% of the time, Pallas kernels for 40%

profile of v4, /device:TPU:0, one launch (start us, length us, event | category | flops | bytes accessed | tf_op | source)
XLA Modules:
  0.0 255.1 jit_solution(6617636861512102909)
XLA Ops:
  2.7 2.9 %collective-permute-start = (bf16[24,576]{1,0:T(8,128)(2,1)}, bf16[24,576]{1,0:T(8,128)(2,1)S(1)}, u32[]{:S(2)}, u32[]{:S(2)}) collective-permute-start(bf16[24,576]{1,0:T(8,128)(2,1)} %get-tuple-element.157), channel_id=1, source_target_pairs={{0,8},{4,12},{8,0},{12,4},{16,24},{20,28},{24,16},{28,20},{1,9},{5... | collective-permute-start | bytes 82952 | tf_op jit(solution)/shard_map/ppermute | solution.py:107
  15.4 3.6 %collective-permute-done.6 = bf16[96,576]{1,0:T(8,128)(2,1)S(1)} collective-permute-done((bf16[96,576]{1,0:T(8,128)(2,1)S(1)}, bf16[96,576]{1,0:T(8,128)(2,1)S(1)}, u32[]{:S(2)}, u32[]{:S(2)}) %collective-permute-start.6) | collective-permute-done | bytes 110624 | tf_op jit(solution)/shard_map/ppermute | solution.py:107
  24.1 2.6 %collective-permute-start.7 = (bf16[192,576]{1,0:T(8,128)(2,1)S(1)}, bf16[192,576]{1,0:T(8,128)(2,1)S(1)}, u32[]{:S(2)}, u32[]{:S(2)}) collective-permute-start(bf16[192,576]{1,0:T(8,128)(2,1)S(1)} %constant_dynamic-update-slice_fusion), channel_id=1, source_target_pairs={{0,2},{1,3},{2,0},{3,1},{4,6},{5,7},{6,4},{7,5},{8,10},{9,11},{10,... | collective-permute-start | bytes 663560 | tf_op jit(solution)/shard_map/ppermute | solution.py:107
  28.7 2.5 dispatch.1
  31.2 6.0 %collective-permute-done.9 = bf16[48,896]{1,0:T(8,128)(2,1)S(1)} collective-permute-done((bf16[48,896]{1,0:T(8,128)(2,1)S(1)}, bf16[48,896]{1,0:T(8,128)(2,1)S(1)}, u32[]{:S(2)}, u32[]{:S(2)}) %collective-permute-start.9) | collective-permute-done | bytes 86048 | tf_op jit(solution)/shard_map/ppermute | solution.py:107
  38.0 3.9 %all-to-all-start = ((bf16[4,128,768]{2,1,0:T(8,128)(2,1)}), bf16[4,128,768]{2,1,0:T(8,128)(2,1)S(1)}, u32[]{:S(2)}, u32[]{:S(2)}) async-start(bf16[4,128,768]{2,1,0:T(8,128)(2,1)} %bitcast.50), calls=%async_computation | async-start | bytes 1572864 | tf_op jit(solution)/shard_map/all_to_all | solution.py:1009
  42.7 4.6 %project.1 = (bf16[1024,256]{1,0:T(8,128)(2,1)}, bf16[1040,512]{1,0:T(8,128)(2,1)}, bf16[768,768]{1,0:T(8,128)(2,1)}) custom-call(bf16[272,768]{1,0:T(8,128)(2,1)} %get-tuple-element.168.refs_0_.refs_2_, bf16[272,768]{1,0:T(8,128)(2,1)} %copy-done.6, bf16[272,768]{1,0:T(8,128)(2,1)} %copy-done.5, bf16[272,768]{1,0:T(8,128)(2,1)} %copy-done.4, ...), custom_call_target="tpu_custom_call" | custom-call | tf_op jit(solution)/shard_map/project/pallas_call | solution.py:92
  52.1 15.7 %attend.1 = (f32[4,192,256]{2,1,0:T(8,128)}, f32[4,8,256]{2,1,0:T(8,128)}, bf16[256,192]{1,0:T(8,128)(2,1)}, bf16[256,192]{1,0:T(8,128)(2,1)}, bf16[256,192]{1,0:T(8,128)(2,1)}, /*index=5*/bf16[256,192]{1,0:T(8,128)(2,1)}) custom-call(bf16[1024,256]{1,0:T(8,128)(2,1)} %get-tuple-element.173.q_ref, bf16[1040,512]{1,0:T(8,128)(2,1)} %get-tuple-element.176.refs_0_, ...), custom_call_target="tpu_custom_call" | custom-call | tf_op jit(solution)/shard_map/attend/pallas_call | solution.py:92
  72.5 2.8 %gather.1.refs_4_.refs_5_.refs_8_ = bf16[768,896]{1,0:T(8,128)(2,1)} custom-call(bf16[384,896]{1,0:T(8,128)(2,1)} %bitcast.46, bf16[384,896]{1,0:T(8,128)(2,1)} %copy-done.13), custom_call_target="tpu_custom_call" | custom-call | tf_op jit(solution)/shard_map/gather/pallas_call | solution.py:92
  75.3 2.7 %collective-permute-done.16.refs_2_ = bf16[256,192]{1,0:T(8,128)(2,1)S(1)} collective-permute-done((bf16[256,192]{1,0:T(8,128)(2,1)}, bf16[256,192]{1,0:T(8,128)(2,1)S(1)}, u32[]{:S(2)}, u32[]{:S(2)}) %collective-permute-start.16) | collective-permute-done | bytes 98336 | tf_op jit(solution)/shard_map/ppermute | solution.py:107
  78.6 4.1 %middle.1 = (f32[256,768]{1,0:T(8,128)}, f32[256,1]{1,0:T(8,128)}, bf16[128,768]{1,0:T(8,128)(2,1)}, bf16[128,768]{1,0:T(8,128)(2,1)}, bf16[128,768]{1,0:T(8,128)(2,1)}, /*index=5*/bf16[128,768]{1,0:T(8,128)(2,1)}) custom-call(bf16[256,192]{1,0:T(8,128)(2,1)} %get-tuple-element.192.refs_0_, bf16[256,192]{1,0:T(8,128)(2,1)} %copy-done.16, ...), custom_call_target="tpu_custom_call" | custom-call | tf_op jit(solution)/shard_map/middle/pallas_call | solution.py:92
  87.1 5.0 %collective-permute-done.19.refs_1_ = bf16[128,768]{1,0:T(8,128)(2,1)S(1)} collective-permute-done((bf16[128,768]{1,0:T(8,128)(2,1)}, bf16[128,768]{1,0:T(8,128)(2,1)S(1)}, u32[]{:S(2)}, u32[]{:S(2)}) %collective-permute-start.19) | collective-permute-done | bytes 196640 | tf_op jit(solution)/shard_map/ppermute | solution.py:107
  92.1 8.8 %collective-permute-done.20.refs_2_ = bf16[128,768]{1,0:T(8,128)(2,1)S(1)} collective-permute-done((bf16[128,768]{1,0:T(8,128)(2,1)}, bf16[128,768]{1,0:T(8,128)(2,1)S(1)}, u32[]{:S(2)}, u32[]{:S(2)}) %collective-permute-start.20) | collective-permute-done | bytes 196640 | tf_op jit(solution)/shard_map/ppermute | solution.py:107
  101.6 16.8 %experts.1 = (bf16[512,768]{1,0:T(8,128)(2,1)}, bf16[512,768]{1,0:T(8,128)(2,1)}, bf16[512,128]{1,0:T(8,128)(2,1)}, bf16[512,768]{1,0:T(8,128)(2,1)}, bf16[512,7...) custom-call(bf16[128,768]{1,0:T(8,128)(2,1)} %get-tuple-element.198.refs_0_, ...), custom_call_target="tpu_custom_call" | custom-call | tf_op jit(solution)/shard_map/experts/pallas_call | solution.py:863
  118.4 4.8 %all-to-all-start.1 = ((bf16[4,128,768]{2,1,0:T(8,128)(2,1)}), bf16[4,128,768]{2,1,0:T(8,128)(2,1)S(1)}, u32[]{:S(2)}, u32[]{:S(2)}) async-start(bf16[4,128,768]{2,1,0:T(8,128)(2,1)} %bitcast.51), calls=%async_computation.1 | async-start | bytes 1572864 | tf_op jit(solution)/shard_map/all_to_all | solution.py:1009
  123.2 11.2 %expert_grads.1 = (f32[768,128]{1,0:T(8,128)}, bf16[4,384,768]{2,1,0:T(8,128)(2,1)}, bf16[4,384,768]{2,1,0:T(8,128)(2,1)}, bf16[4,384,768]{2,1,0:T(8,128)(2,1)}, bf16[4,384,768]{2,1,0:T(8,128)(2,1)}) custom-call(bf16[512,128]{1,0:T(8,128)(2,1)} %get-tuple-element.204.d_logits_ref, bf16[512,768]{1,0:T(8,128)(2,1)} %get-tuple-element.205.rows_ref, ...), custom_call_target="tpu_custom_call" | custom-call | tf_op jit(solution)/shard_map/expert_grads/pallas_call | solution.py:937
  134.4 7.5 %all-to-all-done.1 = bf16[4,128,768]{2,1,0:T(8,128)(2,1)S(1)} async-done(((bf16[4,128,768]{2,1,0:T(8,128)(2,1)}), bf16[4,128,768]{2,1,0:T(8,128)(2,1)S(1)}, u32[]{:S(2)}, u32[]{:S(2)}) %all-to-all-start.1) | async-done | bytes 786464 | tf_op jit(solution)/shard_map/all_to_all | solution.py:1009
  142.8 5.2 %branch.1 = (f32[256,768]{1,0:T(8,128)}, f32[1,768]{1,0:T(1,128)}, bf16[256,192]{1,0:T(8,128)(2,1)}, bf16[256,192]{1,0:T(8,128)(2,1)}, bf16[256,192]{1,0:T(8,128...) custom-call(bf16[512,768]{1,0:T(8,128)(2,1)} %bitcast.44, ...), custom_call_target="tpu_custom_call" | custom-call | tf_op jit(solution)/shard_map/branch/pallas_call | solution.py:92
  151.6 3.5 %all-to-all-start.2 = ((bf16[4,128,768]{2,1,0:T(8,128)(2,1)}), bf16[4,128,768]{2,1,0:T(8,128)(2,1)S(1)}, u32[]{:S(2)}, u32[]{:S(2)}) async-start(bf16[4,128,768]{2,1,0:T(8,128)(2,1)} %bitcast.49), calls=%async_computation.2 | async-start | bytes 1572864 | tf_op jit(solution)/shard_map/all_to_all | solution.py:1009
  155.1 4.9 %merge.1 = (bf16[2,768,384]{2,1,0:T(8,128)(2,1)}, bf16[2,768,384]{2,1,0:T(8,128)(2,1)}) custom-call(bf16[4,384,768]{2,1,0:T(8,128)(2,1)} %get-tuple-element.221.refs_0_.refs_4_, bf16[4,384,768]{2,1,0:T(8,128)(2,1)} %copy-done, bf16[4,384,768]{2,1,0:T(8,128)(2,1)} %get-tuple-element.223.refs_2_.refs_6_, ...), custom_call_target="tpu_custom_call" | custom-call | tf_op jit(solution)/shard_map/merge/pallas_call | solution.py:413
  162.2 2.5 half_out.1
  164.7 24.9 %attend_back.1 = (bf16[1024,256]{1,0:T(8,128)(2,1)}, f32[1024,512]{1,0:T(8,128)}, bf16[1024,512]{1,0:T(8,128)(2,1)}, f32[8,128]{1,0:T(8,128)}) custom-call(bf16[1024,256]{1,0:T(8,128)(2,1)} %get-tuple-element.173.q_ref, bf16[1040,512]{1,0:T(8,128)(2,1)} %get-tuple-element.176.refs_0_, bf16[1040,512]{1,0:T(8,128)(2,1)} %copy-done.3, ...), custom_call_target="tpu_custom_call" | custom-call | tf_op jit(solution)/shard_map/attend_back/pallas_call | solution.py:92
  189.7 4.2 %all-to-all-start.3 = ((bf16[4,4,24,896]{3,2,1,0:T(8,128)(2,1)}), bf16[4,4,24,896]{3,2,1,0:T(8,128)(2,1)}, u32[]{:S(2)}, u32[]{:S(2)}) async-start(bf16[4,4,24,896]{3,2,1,0:T(8,128)(2,1)} %half_out.1), calls=%async_computation.3 | async-start | bytes 1376256 | tf_op jit(solution)/shard_map/all_to_all | solution.py:1184
  193.9 3.2 %fold.1 = (bf16[768,384]{1,0:T(8,128)(2,1)}, bf16[768,384]{1,0:T(8,128)(2,1)}) custom-call(bf16[4,384,768]{2,1,0:T(8,128)(2,1)} %get-tuple-element.221.refs_0_.refs_4_, bf16[4,384,768]{2,1,0:T(8,128)(2,1)} %copy-done, bf16[4,384,768]{2,1,0:T(8,128)(2,1)} %get-tuple-element.223.refs_2_.refs_6_, bf16[4,384,768]{2,1,0:T(8,128)(2,1)} %collective-permute-done.26.refs_3_.refs_7_, ...), custom_call_target="tpu_custom_call" | custom-call | tf_op jit(solution)/shard_map/fold/pallas_call | solution.py:446
  199.1 5.8 %weight.1 = (bf16[1024,768]{1,0:T(8,128)(2,1)}, f32[4,4,24,576]{3,2,1,0:T(8,128)}, bf16[4,4,24,576]{3,2,1,0:T(8,128)(2,1)}) custom-call(bf16[1024,256]{1,0:T(8,128)(2,1)} %get-tuple-element.235.dq_ref, f32[1024,512]{1,0:T(8,128)} %get-tuple-element.236.refs_0_, bf16[1024,512]{1,0:T(8,128)(2,1)} %collective-permute-done.30.refs_1_, ...), custom_call_target="tpu_custom_call" | custom-call | tf_op jit(solution)/shard_map/weight/pallas_call | solution.py:92
  204.9 5.3 %unproject.1 = (f32[256,768]{1,0:T(8,128)}, bf16[256,768]{1,0:T(8,128)(2,1)}, bf16[256,768]{1,0:T(8,128)(2,1)}, bf16[256,768]{1,0:T(8,128)(2,1)}, f32[32,24,128]{2,1,0:T(8,128)}) custom-call(bf16[1024,768]{1,0:T(8,128)(2,1)} %get-tuple-element.246.dp_ref, bf16[768,768]{1,0:T(8,128)(2,1)} %get-tuple-element.247.w_ref, bf16[768]{0:T(1024)(128)(2,1)} %refs_5_.1, ...), custom_call_target="tpu_custom_call" | custom-call | tf_op jit(solution)/shard_map/unproject/pallas_call | solution.py:92
  210.1 2.7 %all-to-all-done.3.two_ref = bf16[4,4,24,896]{3,2,1,0:T(8,128)(2,1)} async-done(((bf16[4,4,24,896]{3,2,1,0:T(8,128)(2,1)}), bf16[4,4,24,896]{3,2,1,0:T(8,128)(2,1)}, u32[]{:S(2)}, u32[]{:S(2)}) %all-to-all-start.3) | async-done | bytes 688160 | tf_op jit(solution)/shard_map/all_to_all | solution.py:1184
  212.9 2.9 %all-to-all-start.4 = ((f32[32,24,128]{2,1,0:T(8,128)}), f32[32,24,128]{2,1,0:T(8,128)S(1)}, u32[]{:S(2)}, u32[]{:S(2)}) async-start(f32[32,24,128]{2,1,0:T(8,128)} %get-tuple-element.282), calls=%async_computation.4 | async-start | bytes 786432 | tf_op jit(solution)/shard_map/all_to_all | solution.py:1266
  219.4 2.6 %combine.1 = bf16[256,768]{1,0:T(8,128)(2,1)} custom-call(bf16[512,768]{1,0:T(8,128)(2,1)} %bitcast.43, bf16[256,512]{1,0:T(8,128)(2,1)} %get-tuple-element.214.refs_4_.pick_t_ref, f32[256,768]{1,0:T(8,128)} %get-tuple-element.215.refs_5_.middle_ref, f32[256,1]{1,0:T(8,128)} %get-tuple-element.263.gate_ref), custom_call_target="tpu_custom_call" | custom-call | tf_op jit(solution)/shard_map/combine/pallas_call | solution.py:92
  224.1 4.2 %finish.1 = (f32[96,3072]{1,0:T(8,128)}, f32[384,768]{1,0:T(8,128)}) custom-call(bf16[4,384,768]{2,1,0:T(8,128)(2,1)} %get-tuple-element.221.refs_0_.refs_4_, bf16[4,384,768]{2,1,0:T(8,128)(2,1)} %copy-done, bf16[4,384,768]{2,1,0:T(8,128)(2,1)} %get-tuple-element.223.refs_2_.refs_6_, bf16[4,384,768]{2,1,0:T(8,128)(2,1)} %collective-permute-done.26.refs_3_.refs_7_, ...), custom_call_target="tpu_custom_call" | custom-call | tf_op jit(solution)/shard_map/finish/pallas_call | solution.py:477
  234.5 3.4 %collective-permute-start.36 = (bf16[4,24,576]{2,1,0:T(8,128)(2,1)S(1)}, bf16[4,24,576]{2,1,0:T(8,128)(2,1)S(1)}, u32[]{:S(2)}, u32[]{:S(2)}) collective-permute-start(bf16[4,24,576]{2,1,0:T(8,128)(2,1)S(1)} %copy-done.37), channel_id=1, source_target_pairs={{0,3},{1,2},{2,1},{3,0},{4,7},{5,6},{6,5},{7,4},{8,11},{9,10},{10,... | collective-permute-start | bytes 331784 | tf_op jit(solution)/shard_map/ppermute | solution.py:107
  248.9 3.1 %tokens.1 = bf16[256,768]{1,0:T(8,128)(2,1)} custom-call(f32[256,768]{1,0:T(8,128)} %get-tuple-element.277.refs_0_, bf16[256,768]{1,0:T(8,128)(2,1)} %copy-done.21, bf16[256,768]{1,0:T(8,128)(2,1)} %copy-done.22, bf16[256,768]{1,0:T(8,128)(2,1)} %copy-done.23, bf16[256,768]{1,0:T(8,128)(2,1)} %bitcast.41, bf16[768]{0:T(1024)(128)(2,1)} %refs_5_.1, ...), custom_call_target="tpu_custom_call" | custom-call | tf_op jit(solution)/shard_map/tokens/pallas_call | solution.py:92
  (182 shorter events, 70.3 us)
Async XLA Ops:
  20.6 16.7 %collective-permute-start.5 = (bf16[272,768]{1,0:T(8,128)(2,1)}, bf16[272,768]{1,0:T(8,128)(2,1)S(1)}, u32[]{:S(2)}, u32[]{:S(2)}) collective-permute-start(bf16[272,768]{1,0:T(8,128)(2,1)} %get-tuple-element.168.refs_0_.refs_2_), channel_id=1, source_target_pairs={{0,24},{4,28},{8,16},{12,20},{16,8},{20,12},{24,0},{28,4},{1,25},{... | collective-permute-start | bytes 1253384 | tf_op jit(solution)/shard_map/ppermute | solution.py:107
  21.1 16.8 %collective-permute-start.4 = (bf16[272,768]{1,0:T(8,128)(2,1)}, bf16[272,768]{1,0:T(8,128)(2,1)S(1)}, u32[]{:S(2)}, u32[]{:S(2)}) collective-permute-start(bf16[272,768]{1,0:T(8,128)(2,1)} %get-tuple-element.168.refs_0_.refs_2_), channel_id=1, source_target_pairs={{0,16},{4,20},{8,24},{12,28},{16,0},{20,4},{24,8},{28,12},{1,17},{... | collective-permute-start | bytes 1253384 | tf_op jit(solution)/shard_map/ppermute | solution.py:107
  22.6 15.3 %collective-permute-start.3 = (bf16[272,768]{1,0:T(8,128)(2,1)}, bf16[272,768]{1,0:T(8,128)(2,1)S(1)}, u32[]{:S(2)}, u32[]{:S(2)}) collective-permute-start(bf16[272,768]{1,0:T(8,128)(2,1)} %get-tuple-element.168.refs_0_.refs_2_), channel_id=1, source_target_pairs={{0,8},{4,12},{8,0},{12,4},{16,24},{20,28},{24,16},{28,20},{1,9},{5... | collective-permute-start | bytes 1253384 | tf_op jit(solution)/shard_map/ppermute | solution.py:107
  24.1 13.1 %collective-permute-start.7 = (bf16[192,576]{1,0:T(8,128)(2,1)S(1)}, bf16[192,576]{1,0:T(8,128)(2,1)S(1)}, u32[]{:S(2)}, u32[]{:S(2)}) collective-permute-start(bf16[192,576]{1,0:T(8,128)(2,1)S(1)} %constant_dynamic-update-slice_fusion), channel_id=1, source_target_pairs={{0,2},{1,3},{2,0},{3,1},{4,6},{5,7},{6,4},{7,5},{8,10},{9,11},{10,... | collective-permute-start | bytes 663560 | tf_op jit(solution)/shard_map/ppermute | solution.py:107
  26.7 10.5 %collective-permute-start.9 = (bf16[48,896]{1,0:T(8,128)(2,1)S(1)}, bf16[48,896]{1,0:T(8,128)(2,1)S(1)}, u32[]{:S(2)}, u32[]{:S(2)}) collective-permute-start(bf16[48,896]{1,0:T(8,128)(2,1)S(1)} %pad_maximum_fusion.4), channel_id=1, source_target_pairs={{0,2},{1,3},{2,0},{3,1},{4,6},{5,7},{6,4},{7,5},{8,10},{9,11},{10,... | collective-permute-start | bytes 258056 | tf_op jit(solution)/shard_map/ppermute | solution.py:107
  38.0 29.8 %all-to-all-start = ((bf16[4,128,768]{2,1,0:T(8,128)(2,1)}), bf16[4,128,768]{2,1,0:T(8,128)(2,1)S(1)}, u32[]{:S(2)}, u32[]{:S(2)}) async-start(bf16[4,128,768]{2,1,0:T(8,128)(2,1)} %bitcast.50), calls=%async_computation | async-start | bytes 1572864 | tf_op jit(solution)/shard_map/all_to_all | solution.py:1009
  47.6 20.2 %collective-permute-start.14 = (bf16[96,896]{1,0:T(8,128)(2,1)S(1)}, bf16[96,896]{1,0:T(8,128)(2,1)S(1)}, u32[]{:S(2)}, u32[]{:S(2)}) collective-permute-start(bf16[96,896]{1,0:T(8,128)(2,1)S(1)} %pad_maximum_fusion.2), channel_id=1, source_target_pairs={{0,24},{4,28},{8,16},{12,20},{16,8},{20,12},{24,0},{28,4},{1,25},{... | collective-permute-start | bytes 516104 | tf_op jit(solution)/shard_map/ppermute | solution.py:107
  48.8 19.0 %collective-permute-start.13 = (bf16[96,896]{1,0:T(8,128)(2,1)S(1)}, bf16[96,896]{1,0:T(8,128)(2,1)S(1)}, u32[]{:S(2)}, u32[]{:S(2)}) collective-permute-start(bf16[96,896]{1,0:T(8,128)(2,1)S(1)} %pad_maximum_fusion.2), channel_id=1, source_target_pairs={{0,16},{4,20},{8,24},{12,28},{16,0},{20,4},{24,8},{28,12},{1,17},{... | collective-permute-start | bytes 516104 | tf_op jit(solution)/shard_map/ppermute | solution.py:107
  50.3 17.5 %collective-permute-start.12 = (bf16[96,896]{1,0:T(8,128)(2,1)S(1)}, bf16[96,896]{1,0:T(8,128)(2,1)S(1)}, u32[]{:S(2)}, u32[]{:S(2)}) collective-permute-start(bf16[96,896]{1,0:T(8,128)(2,1)S(1)} %pad_maximum_fusion.2), channel_id=1, source_target_pairs={{0,8},{4,12},{8,0},{12,4},{16,24},{20,28},{24,16},{28,20},{1,9},{5... | collective-permute-start | bytes 516104 | tf_op jit(solution)/shard_map/ppermute | solution.py:107
  69.3 8.6 %collective-permute-start.16 = (bf16[256,192]{1,0:T(8,128)(2,1)}, bf16[256,192]{1,0:T(8,128)(2,1)S(1)}, u32[]{:S(2)}, u32[]{:S(2)}) collective-permute-start(bf16[256,192]{1,0:T(8,128)(2,1)} %get-tuple-element.186), channel_id=1, source_target_pairs={{0,16},{4,20},{8,24},{12,28},{16,0},{20,4},{24,8},{28,12},{1,17},{... | collective-permute-start | bytes 294920 | tf_op jit(solution)/shard_map/ppermute | solution.py:107
  82.7 9.3 %collective-permute-start.19 = (bf16[128,768]{1,0:T(8,128)(2,1)}, bf16[128,768]{1,0:T(8,128)(2,1)S(1)}, u32[]{:S(2)}, u32[]{:S(2)}) collective-permute-start(bf16[128,768]{1,0:T(8,128)(2,1)} %get-tuple-element.199), channel_id=1, source_target_pairs={{0,1},{1,0},{2,3},{3,2},{4,5},{5,4},{6,7},{7,6},{8,9},{9,8},{10,11... | collective-permute-start | bytes 589832 | tf_op jit(solution)/shard_map/ppermute | solution.py:107
  83.8 17.1 %collective-permute-start.20 = (bf16[128,768]{1,0:T(8,128)(2,1)}, bf16[128,768]{1,0:T(8,128)(2,1)S(1)}, u32[]{:S(2)}, u32[]{:S(2)}) collective-permute-start(bf16[128,768]{1,0:T(8,128)(2,1)} %get-tuple-element.200), channel_id=1, source_target_pairs={{0,2},{1,3},{2,0},{3,1},{4,6},{5,7},{6,4},{7,5},{8,10},{9,11},{10,... | collective-permute-start | bytes 589832 | tf_op jit(solution)/shard_map/ppermute | solution.py:107
  86.1 14.7 %collective-permute-start.21 = (bf16[128,768]{1,0:T(8,128)(2,1)}, bf16[128,768]{1,0:T(8,128)(2,1)S(1)}, u32[]{:S(2)}, u32[]{:S(2)}) collective-permute-start(bf16[128,768]{1,0:T(8,128)(2,1)} %get-tuple-element.201), channel_id=1, source_target_pairs={{0,3},{1,2},{2,1},{3,0},{4,7},{5,6},{6,5},{7,4},{8,11},{9,10},{10,... | collective-permute-start | bytes 589832 | tf_op jit(solution)/shard_map/ppermute | solution.py:107
  118.4 23.5 %all-to-all-start.1 = ((bf16[4,128,768]{2,1,0:T(8,128)(2,1)}), bf16[4,128,768]{2,1,0:T(8,128)(2,1)S(1)}, u32[]{:S(2)}, u32[]{:S(2)}) async-start(bf16[4,128,768]{2,1,0:T(8,128)(2,1)} %bitcast.51), calls=%async_computation.1 | async-start | bytes 1572864 | tf_op jit(solution)/shard_map/all_to_all | solution.py:1009
  141.9 13.2 %collective-permute-start.26 = (bf16[4,384,768]{2,1,0:T(8,128)(2,1)}, bf16[4,384,768]{2,1,0:T(8,128)(2,1)}, u32[]{:S(2)}, u32[]{:S(2)}) collective-permute-start(bf16[4,384,768]{2,1,0:T(8,128)(2,1)} %get-tuple-element.224), channel_id=1, source_target_pairs={{0,4},{4,0},{8,12},{12,8},{16,20},{20,16},{24,28},{28,24},{1,5},{5... | collective-permute-start | bytes 7077896 | tf_op jit(solution)/shard_map/ppermute | solution.py:107
  148.0 12.0 %collective-permute-start.27 = (bf16[4,4,24,896]{3,2,1,0:T(8,128)(2,1)}, bf16[4,4,24,896]{3,2,1,0:T(8,128)(2,1)}, u32[]{:S(2)}, u32[]{:S(2)}) collective-permute-start(bf16[4,4,24,896]{3,2,1,0:T(8,128)(2,1)} %get-tuple-element.228), channel_id=1, source_target_pairs={{0,4},{4,0},{8,12},{12,8},{16,20},{20,16},{24,28},{28,24},{1,5},{5... | collective-permute-start | bytes 2064392 | tf_op jit(solution)/shard_map/ppermute | solution.py:107
  148.0 12.0 %collective-permute-start.22 = (bf16[256,192]{1,0:T(8,128)(2,1)}, bf16[256,192]{1,0:T(8,128)(2,1)S(1)}, u32[]{:S(2)}, u32[]{:S(2)}) collective-permute-start(bf16[256,192]{1,0:T(8,128)(2,1)} %get-tuple-element.218), channel_id=1, source_target_pairs={{0,8},{4,12},{8,0},{12,4},{16,24},{20,28},{24,16},{28,20},{1,9},{5... | collective-permute-start | bytes 294920 | tf_op jit(solution)/shard_map/ppermute | solution.py:107
  148.4 11.5 %collective-permute-start.23 = (bf16[256,192]{1,0:T(8,128)(2,1)}, bf16[256,192]{1,0:T(8,128)(2,1)S(1)}, u32[]{:S(2)}, u32[]{:S(2)}) collective-permute-start(bf16[256,192]{1,0:T(8,128)(2,1)} %get-tuple-element.219), channel_id=1, source_target_pairs={{0,16},{4,20},{8,24},{12,28},{16,0},{20,4},{24,8},{28,12},{1,17},{... | collective-permute-start | bytes 294920 | tf_op jit(solution)/shard_map/ppermute | solution.py:107
  150.2 9.8 %collective-permute-start.24 = (bf16[256,192]{1,0:T(8,128)(2,1)}, bf16[256,192]{1,0:T(8,128)(2,1)S(1)}, u32[]{:S(2)}, u32[]{:S(2)}) collective-permute-start(bf16[256,192]{1,0:T(8,128)(2,1)} %get-tuple-element.220), channel_id=1, source_target_pairs={{0,24},{4,28},{8,16},{12,20},{16,8},{20,12},{24,0},{28,4},{1,25},{... | collective-permute-start | bytes 294920 | tf_op jit(solution)/shard_map/ppermute | solution.py:107
  151.6 38.0 %all-to-all-start.2 = ((bf16[4,128,768]{2,1,0:T(8,128)(2,1)}), bf16[4,128,768]{2,1,0:T(8,128)(2,1)S(1)}, u32[]{:S(2)}, u32[]{:S(2)}) async-start(bf16[4,128,768]{2,1,0:T(8,128)(2,1)} %bitcast.49), calls=%async_computation.2 | async-start | bytes 1572864 | tf_op jit(solution)/shard_map/all_to_all | solution.py:1009
  160.0 29.6 %collective-permute-start.28 = (bf16[2,768,384]{2,1,0:T(8,128)(2,1)}, bf16[2,768,384]{2,1,0:T(8,128)(2,1)S(1)}, u32[]{:S(2)}, u32[]{:S(2)}) collective-permute-start(bf16[2,768,384]{2,1,0:T(8,128)(2,1)} %get-tuple-element.238), channel_id=1, source_target_pairs={{0,8},{4,12},{8,0},{12,4},{16,24},{20,28},{24,16},{28,20},{1,9},{5... | collective-permute-start | bytes 3538952 | tf_op jit(solution)/shard_map/ppermute | solution.py:107
  160.9 28.7 %collective-permute-start.29 = (bf16[2,768,384]{2,1,0:T(8,128)(2,1)}, bf16[2,768,384]{2,1,0:T(8,128)(2,1)S(1)}, u32[]{:S(2)}, u32[]{:S(2)}) collective-permute-start(bf16[2,768,384]{2,1,0:T(8,128)(2,1)} %get-tuple-element.239), channel_id=1, source_target_pairs={{0,16},{4,20},{8,24},{12,28},{16,0},{20,4},{24,8},{28,12},{1,17},{... | collective-permute-start | bytes 3538952 | tf_op jit(solution)/shard_map/ppermute | solution.py:107
  189.6 9.5 %collective-permute-start.30 = (bf16[1024,512]{1,0:T(8,128)(2,1)}, bf16[1024,512]{1,0:T(8,128)(2,1)}, u32[]{:S(2)}, u32[]{:S(2)}) collective-permute-start(bf16[1024,512]{1,0:T(8,128)(2,1)} %get-tuple-element.243), channel_id=1, source_target_pairs={{0,4},{4,0},{8,12},{12,8},{16,20},{20,16},{24,28},{28,24},{1,5},{5... | collective-permute-start | bytes 3145736 | tf_op jit(solution)/shard_map/ppermute | solution.py:107
  189.7 23.2 %all-to-all-start.3 = ((bf16[4,4,24,896]{3,2,1,0:T(8,128)(2,1)}), bf16[4,4,24,896]{3,2,1,0:T(8,128)(2,1)}, u32[]{:S(2)}, u32[]{:S(2)}) async-start(bf16[4,4,24,896]{3,2,1,0:T(8,128)(2,1)} %half_out.1), calls=%async_computation.3 | async-start | bytes 1376256 | tf_op jit(solution)/shard_map/all_to_all | solution.py:1184
  197.1 18.6 %collective-permute-start.32 = (bf16[768,384]{1,0:T(8,128)(2,1)}, bf16[768,384]{1,0:T(8,128)(2,1)S(1)}, u32[]{:S(2)}, u32[]{:S(2)}) collective-permute-start(bf16[768,384]{1,0:T(8,128)(2,1)} %get-tuple-element.256), channel_id=1, source_target_pairs={{0,16},{4,20},{8,24},{12,28},{16,0},{20,4},{24,8},{28,12},{1,17},{... | collective-permute-start | bytes 1769480 | tf_op jit(solution)/shard_map/ppermute | solution.py:107
  197.9 17.9 %collective-permute-start.33 = (bf16[768,384]{1,0:T(8,128)(2,1)}, bf16[768,384]{1,0:T(8,128)(2,1)S(1)}, u32[]{:S(2)}, u32[]{:S(2)}) collective-permute-start(bf16[768,384]{1,0:T(8,128)(2,1)} %get-tuple-element.257), channel_id=1, source_target_pairs={{0,8},{4,12},{8,0},{12,4},{16,24},{20,28},{24,16},{28,20},{1,9},{5... | collective-permute-start | bytes 1769480 | tf_op jit(solution)/shard_map/ppermute | solution.py:107
  204.9 10.9 %collective-permute-start.31 = (bf16[4,4,24,576]{3,2,1,0:T(8,128)(2,1)}, bf16[4,4,24,576]{3,2,1,0:T(8,128)(2,1)S(1)}, u32[]{:S(2)}, u32[]{:S(2)}) collective-permute-start(bf16[4,4,24,576]{3,2,1,0:T(8,128)(2,1)} %get-tuple-element.245), channel_id=1, source_target_pairs={{0,4},{4,0},{8,12},{12,8},{16,20},{20,16},{24,28},{28,24},{1,5},{5... | collective-permute-start | bytes 1327112 | tf_op jit(solution)/shard_map/ppermute | solution.py:107
  212.9 25.1 %all-to-all-start.4 = ((f32[32,24,128]{2,1,0:T(8,128)}), f32[32,24,128]{2,1,0:T(8,128)S(1)}, u32[]{:S(2)}, u32[]{:S(2)}) async-start(f32[32,24,128]{2,1,0:T(8,128)} %get-tuple-element.282), calls=%async_computation.4 | async-start | bytes 786432 | tf_op jit(solution)/shard_map/all_to_all | solution.py:1266
  215.8 25.5 %collective-permute-start.37 = (bf16[256,768]{1,0:T(8,128)(2,1)}, bf16[256,768]{1,0:T(8,128)(2,1)S(1)}, u32[]{:S(2)}, u32[]{:S(2)}) collective-permute-start(bf16[256,768]{1,0:T(8,128)(2,1)} %get-tuple-element.274), channel_id=1, source_target_pairs={{0,8},{4,12},{8,0},{12,4},{16,24},{20,28},{24,16},{28,20},{1,9},{5... | collective-permute-start | bytes 1179656 | tf_op jit(solution)/shard_map/ppermute | solution.py:107
  217.4 23.9 %collective-permute-start.38 = (bf16[256,768]{1,0:T(8,128)(2,1)}, bf16[256,768]{1,0:T(8,128)(2,1)S(1)}, u32[]{:S(2)}, u32[]{:S(2)}) collective-permute-start(bf16[256,768]{1,0:T(8,128)(2,1)} %get-tuple-element.275), channel_id=1, source_target_pairs={{0,16},{4,20},{8,24},{12,28},{16,0},{20,4},{24,8},{28,12},{1,17},{... | collective-permute-start | bytes 1179656 | tf_op jit(solution)/shard_map/ppermute | solution.py:107
  218.9 22.5 %collective-permute-start.39 = (bf16[256,768]{1,0:T(8,128)(2,1)}, bf16[256,768]{1,0:T(8,128)(2,1)S(1)}, u32[]{:S(2)}, u32[]{:S(2)}) collective-permute-start(bf16[256,768]{1,0:T(8,128)(2,1)} %get-tuple-element.276), channel_id=1, source_target_pairs={{0,24},{4,28},{8,16},{12,20},{16,8},{20,12},{24,0},{28,4},{1,25},{... | collective-permute-start | bytes 1179656 | tf_op jit(solution)/shard_map/ppermute | solution.py:107
  229.9 10.5 %collective-permute-start.35 = (bf16[4,24,576]{2,1,0:T(8,128)(2,1)S(1)}, bf16[4,24,576]{2,1,0:T(8,128)(2,1)S(1)}, u32[]{:S(2)}, u32[]{:S(2)}) collective-permute-start(bf16[4,24,576]{2,1,0:T(8,128)(2,1)S(1)} %copy-done.38), channel_id=1, source_target_pairs={{0,2},{1,3},{2,0},{3,1},{4,6},{5,7},{6,4},{7,5},{8,10},{9,11},{10,... | collective-permute-start | bytes 331784 | tf_op jit(solution)/shard_map/ppermute | solution.py:107
  (56 other events, 280.3 us)

commit v5 on v4

--- a/solution.py
+++ b/solution.py
@@ -1034,13 +1034,7 @@
     step = 1
     while step < n_batch:
         cuts = jnp.concatenate([cuts, swap(cuts, "batch", n_batch, step)], axis=0)
-        cuts, both = lax.optimization_barrier((cuts, both)) if step == 1 else (cuts, both)
         step = step * 2
-    step = 1
-    while step < n_batch:
-        both = jnp.concatenate([both, swap(both, "batch", n_batch, step)], axis=0)
-        step = step * 2
-
     route_row = routes.reshape(1, per)
     d_result = out_grad[0]
     pick, pick_t, dz_sent = kernel_call(
@@ -1049,6 +1043,11 @@
         [route_row, d_result],
         [((slots, per), BF16), ((per, slots), BF16), ((slots, width), BF16)],
     )
+    both, pick = lax.optimization_barrier((both, pick))
+    step = 1
+    while step < n_batch:
+        both = jnp.concatenate([both, swap(both, "batch", n_batch, step)], axis=0)
+        step = step * 2
     table = sum(
         jnp.where(group == g, bias_table[:, g * heads : (g + 1) * heads], 0) for g in range(groups)
     )

time: 256 us -> 257 us (level)
  starting transfers between devices: 67.9 us -> 74.7 us
  Pallas kernels: 129 us -> 123 us
    pallas_call x17, Pallas kernels: 88.8 us -> 82.4 us  [kernel_call(): pl.pallas_call(kernel, out_shape=tuple((jax.ShapeDtypeStruct(shape, kind)...]
    ppermute x43, starting transfers between devices: 48.7 us -> 53.6 us  [swap(): return lax.ppermute(value, axis, [(i, i ^ mask) for i in range(size)])]
    unnamed x85 -> x87, local copies, waits for them, and re-layouts: 8.09 us -> 8.72 us
  transfers between devices with their start and end apart: 48 -> 48, of which waited for: 13 -> 12; matrix products, arithmetic and copies ran while one was open for 2% -> 2% of each run, Pallas kernels for 40% -> 38%
where the time goes in v5:
time: 257 us; the launch traced here: 254 us
  Pallas kernels  123 us (48%)
  starting transfers between devices  74.7 us (29%)
  waiting for transfers between devices  43 us (17%)
  local copies, waits for them, and re-layouts  10.7 us (4%)
    pallas_call x17, Pallas kernels, kernel_call(): pl.pallas_call(kernel, out_shape=tuple((jax.ShapeDtypeStruct(shape, kind)...  82.4 us
    ppermute x43, starting transfers between devices, swap(): return lax.ppermute(value, axis, [(i, i ^ mask) for i in range(size)])  53.6 us
    ppermute x43, waiting for transfers between devices, swap(): return lax.ppermute(value, axis, [(i, i ^ mask) for i in range(size)])  33.1 us
    pallas_call x1, Pallas kernels, expert_layer(): pl.pallas_call(functools.partial(expert_kernel, experts=batch, ring=ring,...  16.9 us
    all_to_all x3, starting transfers between devices, turn_batch(): lax.all_to_all(rows, 'batch', split_axis=0, concat_axis=0, tiled=True)  13.2 us
    pallas_call x1, Pallas kernels, expert_grads(): pl.pallas_call(functools.partial(expert_grad_kernel, groups=groups, ring=...  11.2 us
    unnamed x87, local copies, waits for them, and re-layouts  8.72 us
    all_to_all x3, waiting for transfers between devices, turn_batch(): lax.all_to_all(rows, 'batch', split_axis=0, concat_axis=0, tiled=True)  7.58 us
  transfers between devices with their start and end apart: 48, of which 12 were waited for; matrix products, arithmetic and copies ran while one was open for 2% of the time, Pallas kernels for 38%

profile of v5, /device:TPU:0, one launch (start us, length us, event | category | flops | bytes accessed | tf_op | source)
XLA Modules:
  0.0 254.2 jit_solution(15970942349926652344)
XLA Ops:
  2.7 2.9 %collective-permute-start = (bf16[24,576]{1,0:T(8,128)(2,1)}, bf16[24,576]{1,0:T(8,128)(2,1)S(1)}, u32[]{:S(2)}, u32[]{:S(2)}) collective-permute-start(bf16[24,576]{1,0:T(8,128)(2,1)} %get-tuple-element.157), channel_id=1, source_target_pairs={{0,8},{4,12},{8,0},{12,4},{16,24},{20,28},{24,16},{28,20},{1,9},{5... | collective-permute-start | bytes 82952 | tf_op jit(solution)/shard_map/ppermute | solution.py:107
  8.7 2.5 dispatch.1
  13.3 2.5 collective-permute-start.5
  18.9 2.7 %collective-permute-start.9 = (bf16[48,896]{1,0:T(8,128)(2,1)S(1)}, bf16[48,896]{1,0:T(8,128)(2,1)S(1)}, u32[]{:S(2)}, u32[]{:S(2)}) collective-permute-start(bf16[48,896]{1,0:T(8,128)(2,1)S(1)} %pad_maximum_fusion.3), channel_id=1, source_target_pairs={{0,2},{1,3},{2,0},{3,1},{4,6},{5,7},{6,4},{7,5},{8,10},{9,11},{10,... | collective-permute-start | bytes 258056 | tf_op jit(solution)/shard_map/ppermute | solution.py:107
  23.3 4.0 %collective-permute-start.7 = (bf16[192,576]{1,0:T(8,128)(2,1)S(1)}, bf16[192,576]{1,0:T(8,128)(2,1)S(1)}, u32[]{:S(2)}, u32[]{:S(2)}) collective-permute-start(bf16[192,576]{1,0:T(8,128)(2,1)S(1)} %get-tuple-element.300), channel_id=1, source_target_pairs={{0,2},{1,3},{2,0},{3,1},{4,6},{5,7},{6,4},{7,5},{8,10},{9,11},{10,... | collective-permute-start | bytes 663560 | tf_op jit(solution)/shard_map/ppermute | solution.py:107
  28.1 7.7 %collective-permute-done.7 = bf16[192,576]{1,0:T(8,128)(2,1)S(1)} collective-permute-done((bf16[192,576]{1,0:T(8,128)(2,1)S(1)}, bf16[192,576]{1,0:T(8,128)(2,1)S(1)}, u32[]{:S(2)}, u32[]{:S(2)}) %collective-permute-start.7) | collective-permute-done | bytes 221216 | tf_op jit(solution)/shard_map/ppermute | solution.py:107
  36.0 4.2 %all-to-all-start = ((bf16[4,128,768]{2,1,0:T(8,128)(2,1)}), bf16[4,128,768]{2,1,0:T(8,128)(2,1)S(1)}, u32[]{:S(2)}, u32[]{:S(2)}) async-start(bf16[4,128,768]{2,1,0:T(8,128)(2,1)} %bitcast.4), calls=%async_computation | async-start | bytes 1572864 | tf_op jit(solution)/shard_map/all_to_all | solution.py:1009
  41.0 4.6 %project.1 = (bf16[1024,256]{1,0:T(8,128)(2,1)}, bf16[1040,512]{1,0:T(8,128)(2,1)}, bf16[768,768]{1,0:T(8,128)(2,1)}) custom-call(bf16[272,768]{1,0:T(8,128)(2,1)} %get-tuple-element.168.refs_0_.refs_2_, bf16[272,768]{1,0:T(8,128)(2,1)} %copy-done.6, bf16[272,768]{1,0:T(8,128)(2,1)} %copy-done.5, bf16[272,768]{1,0:T(8,128)(2,1)} %copy-done.4, ...), custom_call_target="tpu_custom_call" | custom-call | tf_op jit(solution)/shard_map/project/pallas_call | solution.py:92
  50.4 13.2 %attend.1 = (f32[4,192,256]{2,1,0:T(8,128)}, f32[4,8,256]{2,1,0:T(8,128)}, bf16[256,192]{1,0:T(8,128)(2,1)}, bf16[256,192]{1,0:T(8,128)(2,1)}, bf16[256,192]{1,0:T(8,128)(2,1)}, /*index=5*/bf16[256,192]{1,0:T(8,128)(2,1)}) custom-call(bf16[1024,256]{1,0:T(8,128)(2,1)} %get-tuple-element.173.q_ref, bf16[1040,512]{1,0:T(8,128)(2,1)} %get-tuple-element.176.refs_0_, ...), custom_call_target="tpu_custom_call" | custom-call | tf_op jit(solution)/shard_map/attend/pallas_call | solution.py:92
  68.3 2.8 %gather.1.refs_4_.refs_5_.refs_8_ = bf16[768,896]{1,0:T(8,128)(2,1)} custom-call(bf16[384,896]{1,0:T(8,128)(2,1)} %bitcast.46, bf16[384,896]{1,0:T(8,128)(2,1)} %copy-done.12), custom_call_target="tpu_custom_call" | custom-call | tf_op jit(solution)/shard_map/gather/pallas_call | solution.py:92
  71.0 2.9 %collective-permute-done.16.refs_2_ = bf16[256,192]{1,0:T(8,128)(2,1)S(1)} collective-permute-done((bf16[256,192]{1,0:T(8,128)(2,1)}, bf16[256,192]{1,0:T(8,128)(2,1)S(1)}, u32[]{:S(2)}, u32[]{:S(2)}) %collective-permute-start.16) | collective-permute-done | bytes 98336 | tf_op jit(solution)/shard_map/ppermute | solution.py:107
  75.3 4.1 %middle.1 = (f32[256,768]{1,0:T(8,128)}, f32[256,1]{1,0:T(8,128)}, bf16[128,768]{1,0:T(8,128)(2,1)}, bf16[128,768]{1,0:T(8,128)(2,1)}, bf16[128,768]{1,0:T(8,128)(2,1)}, /*index=5*/bf16[128,768]{1,0:T(8,128)(2,1)}) custom-call(bf16[256,192]{1,0:T(8,128)(2,1)} %get-tuple-element.192.refs_0_, bf16[256,192]{1,0:T(8,128)(2,1)} %copy-done.16, ...), custom_call_target="tpu_custom_call" | custom-call | tf_op jit(solution)/shard_map/middle/pallas_call | solution.py:92
  81.2 2.7 %collective-permute-start.20 = (bf16[128,768]{1,0:T(8,128)(2,1)}, bf16[128,768]{1,0:T(8,128)(2,1)S(1)}, u32[]{:S(2)}, u32[]{:S(2)}) collective-permute-start(bf16[128,768]{1,0:T(8,128)(2,1)} %get-tuple-element.200), channel_id=1, source_target_pairs={{0,2},{1,3},{2,0},{3,1},{4,6},{5,7},{6,4},{7,5},{8,10},{9,11},{10,... | collective-permute-start | bytes 589832 | tf_op jit(solution)/shard_map/ppermute | solution.py:107
  87.8 10.6 %collective-permute-done.20.refs_2_ = bf16[128,768]{1,0:T(8,128)(2,1)S(1)} collective-permute-done((bf16[128,768]{1,0:T(8,128)(2,1)}, bf16[128,768]{1,0:T(8,128)(2,1)S(1)}, u32[]{:S(2)}, u32[]{:S(2)}) %collective-permute-start.20) | collective-permute-done | bytes 196640 | tf_op jit(solution)/shard_map/ppermute | solution.py:107
  99.1 16.9 %experts.1 = (bf16[512,768]{1,0:T(8,128)(2,1)}, bf16[512,768]{1,0:T(8,128)(2,1)}, bf16[512,128]{1,0:T(8,128)(2,1)}, bf16[512,768]{1,0:T(8,128)(2,1)}, bf16[512,7...) custom-call(bf16[128,768]{1,0:T(8,128)(2,1)} %get-tuple-element.198.refs_0_, ...), custom_call_target="tpu_custom_call" | custom-call | tf_op jit(solution)/shard_map/experts/pallas_call | solution.py:863
  116.0 5.5 %all-to-all-start.1 = ((bf16[4,128,768]{2,1,0:T(8,128)(2,1)}), bf16[4,128,768]{2,1,0:T(8,128)(2,1)S(1)}, u32[]{:S(2)}, u32[]{:S(2)}) async-start(bf16[4,128,768]{2,1,0:T(8,128)(2,1)} %bitcast.50), calls=%async_computation.1 | async-start | bytes 1572864 | tf_op jit(solution)/shard_map/all_to_all | solution.py:1009
  121.6 11.2 %expert_grads.1 = (f32[768,128]{1,0:T(8,128)}, bf16[4,384,768]{2,1,0:T(8,128)(2,1)}, bf16[4,384,768]{2,1,0:T(8,128)(2,1)}, bf16[4,384,768]{2,1,0:T(8,128)(2,1)}, bf16[4,384,768]{2,1,0:T(8,128)(2,1)}) custom-call(bf16[512,128]{1,0:T(8,128)(2,1)} %get-tuple-element.204.d_logits_ref, bf16[512,768]{1,0:T(8,128)(2,1)} %get-tuple-element.205.rows_ref, ...), custom_call_target="tpu_custom_call" | custom-call | tf_op jit(solution)/shard_map/expert_grads/pallas_call | solution.py:937
  132.8 7.6 %all-to-all-done.1 = bf16[4,128,768]{2,1,0:T(8,128)(2,1)S(1)} async-done(((bf16[4,128,768]{2,1,0:T(8,128)(2,1)}), bf16[4,128,768]{2,1,0:T(8,128)(2,1)S(1)}, u32[]{:S(2)}, u32[]{:S(2)}) %all-to-all-start.1) | async-done | bytes 786464 | tf_op jit(solution)/shard_map/all_to_all | solution.py:1009
  141.2 5.2 %branch.1 = (f32[256,768]{1,0:T(8,128)}, f32[1,768]{1,0:T(1,128)}, bf16[256,192]{1,0:T(8,128)(2,1)}, bf16[256,192]{1,0:T(8,128)(2,1)}, bf16[256,192]{1,0:T(8,128...) custom-call(bf16[512,768]{1,0:T(8,128)(2,1)} %bitcast.44, ...), custom_call_target="tpu_custom_call" | custom-call | tf_op jit(solution)/shard_map/branch/pallas_call | solution.py:92
  150.3 3.5 %all-to-all-start.2 = ((bf16[4,128,768]{2,1,0:T(8,128)(2,1)}), bf16[4,128,768]{2,1,0:T(8,128)(2,1)S(1)}, u32[]{:S(2)}, u32[]{:S(2)}) async-start(bf16[4,128,768]{2,1,0:T(8,128)(2,1)} %bitcast.49), calls=%async_computation.2 | async-start | bytes 1572864 | tf_op jit(solution)/shard_map/all_to_all | solution.py:1009
  153.8 4.9 %merge.1 = (bf16[2,768,384]{2,1,0:T(8,128)(2,1)}, bf16[2,768,384]{2,1,0:T(8,128)(2,1)}) custom-call(bf16[4,384,768]{2,1,0:T(8,128)(2,1)} %get-tuple-element.221.refs_0_.refs_4_, bf16[4,384,768]{2,1,0:T(8,128)(2,1)} %copy-done, bf16[4,384,768]{2,1,0:T(8,128)(2,1)} %get-tuple-element.223.refs_2_.refs_6_, ...), custom_call_target="tpu_custom_call" | custom-call | tf_op jit(solution)/shard_map/merge/pallas_call | solution.py:413
  160.9 2.5 half_out.1
  163.4 21.0 %attend_back.1 = (bf16[1024,256]{1,0:T(8,128)(2,1)}, f32[1024,512]{1,0:T(8,128)}, bf16[1024,512]{1,0:T(8,128)(2,1)}, f32[8,128]{1,0:T(8,128)}) custom-call(bf16[1024,256]{1,0:T(8,128)(2,1)} %get-tuple-element.173.q_ref, bf16[1040,512]{1,0:T(8,128)(2,1)} %get-tuple-element.176.refs_0_, bf16[1040,512]{1,0:T(8,128)(2,1)} %copy-done.3, ...), custom_call_target="tpu_custom_call" | custom-call | tf_op jit(solution)/shard_map/attend_back/pallas_call | solution.py:92
  188.1 4.8 %all-to-all-start.3 = ((bf16[4,4,24,896]{3,2,1,0:T(8,128)(2,1)}), bf16[4,4,24,896]{3,2,1,0:T(8,128)(2,1)}, u32[]{:S(2)}, u32[]{:S(2)}) async-start(bf16[4,4,24,896]{3,2,1,0:T(8,128)(2,1)} %half_out.1), calls=%async_computation.3 | async-start | bytes 1376256 | tf_op jit(solution)/shard_map/all_to_all | solution.py:1183
  192.9 3.2 %fold.1 = (bf16[768,384]{1,0:T(8,128)(2,1)}, bf16[768,384]{1,0:T(8,128)(2,1)}) custom-call(bf16[4,384,768]{2,1,0:T(8,128)(2,1)} %get-tuple-element.221.refs_0_.refs_4_, bf16[4,384,768]{2,1,0:T(8,128)(2,1)} %copy-done, bf16[4,384,768]{2,1,0:T(8,128)(2,1)} %get-tuple-element.223.refs_2_.refs_6_, bf16[4,384,768]{2,1,0:T(8,128)(2,1)} %collective-permute-done.26.refs_3_.refs_7_, ...), custom_call_target="tpu_custom_call" | custom-call | tf_op jit(solution)/shard_map/fold/pallas_call | solution.py:446
  198.3 5.8 %weight.1 = (bf16[1024,768]{1,0:T(8,128)(2,1)}, f32[4,4,24,576]{3,2,1,0:T(8,128)}, bf16[4,4,24,576]{3,2,1,0:T(8,128)(2,1)}) custom-call(bf16[1024,256]{1,0:T(8,128)(2,1)} %get-tuple-element.235.dq_ref, f32[1024,512]{1,0:T(8,128)} %get-tuple-element.236.refs_0_, bf16[1024,512]{1,0:T(8,128)(2,1)} %collective-permute-done.30.refs_1_, ...), custom_call_target="tpu_custom_call" | custom-call | tf_op jit(solution)/shard_map/weight/pallas_call | solution.py:92
  204.1 5.3 %unproject.1 = (f32[256,768]{1,0:T(8,128)}, bf16[256,768]{1,0:T(8,128)(2,1)}, bf16[256,768]{1,0:T(8,128)(2,1)}, bf16[256,768]{1,0:T(8,128)(2,1)}, f32[32,24,128]{2,1,0:T(8,128)}) custom-call(bf16[1024,768]{1,0:T(8,128)(2,1)} %get-tuple-element.246.dp_ref, bf16[768,768]{1,0:T(8,128)(2,1)} %get-tuple-element.247.w_ref, bf16[768]{0:T(1024)(128)(2,1)} %refs_5_.1, ...), custom_call_target="tpu_custom_call" | custom-call | tf_op jit(solution)/shard_map/unproject/pallas_call | solution.py:92
  211.6 3.1 %all-to-all-start.4 = ((f32[32,24,128]{2,1,0:T(8,128)}), f32[32,24,128]{2,1,0:T(8,128)S(1)}, u32[]{:S(2)}, u32[]{:S(2)}) async-start(f32[32,24,128]{2,1,0:T(8,128)} %get-tuple-element.282), calls=%async_computation.4 | async-start | bytes 786432 | tf_op jit(solution)/shard_map/all_to_all | solution.py:1265
  218.4 2.6 %combine.1 = bf16[256,768]{1,0:T(8,128)(2,1)} custom-call(bf16[512,768]{1,0:T(8,128)(2,1)} %bitcast.43, bf16[256,512]{1,0:T(8,128)(2,1)} %get-tuple-element.214.refs_4_.pick_t_ref, f32[256,768]{1,0:T(8,128)} %get-tuple-element.215.refs_5_.middle_ref, f32[256,1]{1,0:T(8,128)} %get-tuple-element.263.gate_ref), custom_call_target="tpu_custom_call" | custom-call | tf_op jit(solution)/shard_map/combine/pallas_call | solution.py:92
  223.1 4.2 %finish.1 = (f32[96,3072]{1,0:T(8,128)}, f32[384,768]{1,0:T(8,128)}) custom-call(bf16[4,384,768]{2,1,0:T(8,128)(2,1)} %get-tuple-element.221.refs_0_.refs_4_, bf16[4,384,768]{2,1,0:T(8,128)(2,1)} %copy-done, bf16[4,384,768]{2,1,0:T(8,128)(2,1)} %get-tuple-element.223.refs_2_.refs_6_, bf16[4,384,768]{2,1,0:T(8,128)(2,1)} %collective-permute-done.26.refs_3_.refs_7_, ...), custom_call_target="tpu_custom_call" | custom-call | tf_op jit(solution)/shard_map/finish/pallas_call | solution.py:477
  233.5 3.4 %collective-permute-start.36 = (bf16[4,24,576]{2,1,0:T(8,128)(2,1)S(1)}, bf16[4,24,576]{2,1,0:T(8,128)(2,1)S(1)}, u32[]{:S(2)}, u32[]{:S(2)}) collective-permute-start(bf16[4,24,576]{2,1,0:T(8,128)(2,1)S(1)} %copy-done.38), channel_id=1, source_target_pairs={{0,3},{1,2},{2,1},{3,0},{4,7},{5,6},{6,5},{7,4},{8,11},{9,10},{10,... | collective-permute-start | bytes 331784 | tf_op jit(solution)/shard_map/ppermute | solution.py:107
  247.9 3.1 %tokens.1 = bf16[256,768]{1,0:T(8,128)(2,1)} custom-call(f32[256,768]{1,0:T(8,128)} %get-tuple-element.277.refs_0_, bf16[256,768]{1,0:T(8,128)(2,1)} %copy-done.21, bf16[256,768]{1,0:T(8,128)(2,1)} %copy-done.22, bf16[256,768]{1,0:T(8,128)(2,1)} %copy-done.23, bf16[256,768]{1,0:T(8,128)(2,1)} %bitcast.41, bf16[768]{0:T(1024)(128)(2,1)} %refs_5_.1, ...), custom_call_target="tpu_custom_call" | custom-call | tf_op jit(solution)/shard_map/tokens/pallas_call | solution.py:92
  (184 shorter events, 71.9 us)
Async XLA Ops:
  2.7 10.5 %collective-permute-start = (bf16[24,576]{1,0:T(8,128)(2,1)}, bf16[24,576]{1,0:T(8,128)(2,1)S(1)}, u32[]{:S(2)}, u32[]{:S(2)}) collective-permute-start(bf16[24,576]{1,0:T(8,128)(2,1)} %get-tuple-element.157), channel_id=1, source_target_pairs={{0,8},{4,12},{8,0},{12,4},{16,24},{20,28},{24,16},{28,20},{1,9},{5... | collective-permute-start | bytes 82952 | tf_op jit(solution)/shard_map/ppermute | solution.py:107
  13.3 22.6 %collective-permute-start.5 = (bf16[272,768]{1,0:T(8,128)(2,1)}, bf16[272,768]{1,0:T(8,128)(2,1)S(1)}, u32[]{:S(2)}, u32[]{:S(2)}) collective-permute-start(bf16[272,768]{1,0:T(8,128)(2,1)} %get-tuple-element.168.refs_0_.refs_2_), channel_id=1, source_target_pairs={{0,24},{4,28},{8,16},{12,20},{16,8},{20,12},{24,0},{28,4},{1,25},{... | collective-permute-start | bytes 1253384 | tf_op jit(solution)/shard_map/ppermute | solution.py:107
  15.8 20.1 %collective-permute-start.4 = (bf16[272,768]{1,0:T(8,128)(2,1)}, bf16[272,768]{1,0:T(8,128)(2,1)S(1)}, u32[]{:S(2)}, u32[]{:S(2)}) collective-permute-start(bf16[272,768]{1,0:T(8,128)(2,1)} %get-tuple-element.168.refs_0_.refs_2_), channel_id=1, source_target_pairs={{0,16},{4,20},{8,24},{12,28},{16,0},{20,4},{24,8},{28,12},{1,17},{... | collective-permute-start | bytes 1253384 | tf_op jit(solution)/shard_map/ppermute | solution.py:107
  16.3 19.6 %collective-permute-start.3 = (bf16[272,768]{1,0:T(8,128)(2,1)}, bf16[272,768]{1,0:T(8,128)(2,1)S(1)}, u32[]{:S(2)}, u32[]{:S(2)}) collective-permute-start(bf16[272,768]{1,0:T(8,128)(2,1)} %get-tuple-element.168.refs_0_.refs_2_), channel_id=1, source_target_pairs={{0,8},{4,12},{8,0},{12,4},{16,24},{20,28},{24,16},{28,20},{1,9},{5... | collective-permute-start | bytes 1253384 | tf_op jit(solution)/shard_map/ppermute | solution.py:107
  18.9 9.2 %collective-permute-start.9 = (bf16[48,896]{1,0:T(8,128)(2,1)S(1)}, bf16[48,896]{1,0:T(8,128)(2,1)S(1)}, u32[]{:S(2)}, u32[]{:S(2)}) collective-permute-start(bf16[48,896]{1,0:T(8,128)(2,1)S(1)} %pad_maximum_fusion.3), channel_id=1, source_target_pairs={{0,2},{1,3},{2,0},{3,1},{4,6},{5,7},{6,4},{7,5},{8,10},{9,11},{10,... | collective-permute-start | bytes 258056 | tf_op jit(solution)/shard_map/ppermute | solution.py:107
  23.3 12.5 %collective-permute-start.7 = (bf16[192,576]{1,0:T(8,128)(2,1)S(1)}, bf16[192,576]{1,0:T(8,128)(2,1)S(1)}, u32[]{:S(2)}, u32[]{:S(2)}) collective-permute-start(bf16[192,576]{1,0:T(8,128)(2,1)S(1)} %get-tuple-element.300), channel_id=1, source_target_pairs={{0,2},{1,3},{2,0},{3,1},{4,6},{5,7},{6,4},{7,5},{8,10},{9,11},{10,... | collective-permute-start | bytes 663560 | tf_op jit(solution)/shard_map/ppermute | solution.py:107
  36.0 27.6 %all-to-all-start = ((bf16[4,128,768]{2,1,0:T(8,128)(2,1)}), bf16[4,128,768]{2,1,0:T(8,128)(2,1)S(1)}, u32[]{:S(2)}, u32[]{:S(2)}) async-start(bf16[4,128,768]{2,1,0:T(8,128)(2,1)} %bitcast.4), calls=%async_computation | async-start | bytes 1572864 | tf_op jit(solution)/shard_map/all_to_all | solution.py:1009
  45.9 17.7 %collective-permute-start.14 = (bf16[96,896]{1,0:T(8,128)(2,1)S(1)}, bf16[96,896]{1,0:T(8,128)(2,1)S(1)}, u32[]{:S(2)}, u32[]{:S(2)}) collective-permute-start(bf16[96,896]{1,0:T(8,128)(2,1)S(1)} %pad_maximum_fusion.1), channel_id=1, source_target_pairs={{0,24},{4,28},{8,16},{12,20},{16,8},{20,12},{24,0},{28,4},{1,25},{... | collective-permute-start | bytes 516104 | tf_op jit(solution)/shard_map/ppermute | solution.py:107
  48.3 15.2 %collective-permute-start.13 = (bf16[96,896]{1,0:T(8,128)(2,1)S(1)}, bf16[96,896]{1,0:T(8,128)(2,1)S(1)}, u32[]{:S(2)}, u32[]{:S(2)}) collective-permute-start(bf16[96,896]{1,0:T(8,128)(2,1)S(1)} %pad_maximum_fusion.1), channel_id=1, source_target_pairs={{0,16},{4,20},{8,24},{12,28},{16,0},{20,4},{24,8},{28,12},{1,17},{... | collective-permute-start | bytes 516104 | tf_op jit(solution)/shard_map/ppermute | solution.py:107
  48.9 14.7 %collective-permute-start.12 = (bf16[96,896]{1,0:T(8,128)(2,1)S(1)}, bf16[96,896]{1,0:T(8,128)(2,1)S(1)}, u32[]{:S(2)}, u32[]{:S(2)}) collective-permute-start(bf16[96,896]{1,0:T(8,128)(2,1)S(1)} %pad_maximum_fusion.1), channel_id=1, source_target_pairs={{0,8},{4,12},{8,0},{12,4},{16,24},{20,28},{24,16},{28,20},{1,9},{5... | collective-permute-start | bytes 516104 | tf_op jit(solution)/shard_map/ppermute | solution.py:107
  65.4 8.6 %collective-permute-start.16 = (bf16[256,192]{1,0:T(8,128)(2,1)}, bf16[256,192]{1,0:T(8,128)(2,1)S(1)}, u32[]{:S(2)}, u32[]{:S(2)}) collective-permute-start(bf16[256,192]{1,0:T(8,128)(2,1)} %get-tuple-element.186), channel_id=1, source_target_pairs={{0,16},{4,20},{8,24},{12,28},{16,0},{20,4},{24,8},{28,12},{1,17},{... | collective-permute-start | bytes 294920 | tf_op jit(solution)/shard_map/ppermute | solution.py:107
  81.2 17.1 %collective-permute-start.20 = (bf16[128,768]{1,0:T(8,128)(2,1)}, bf16[128,768]{1,0:T(8,128)(2,1)S(1)}, u32[]{:S(2)}, u32[]{:S(2)}) collective-permute-start(bf16[128,768]{1,0:T(8,128)(2,1)} %get-tuple-element.200), channel_id=1, source_target_pairs={{0,2},{1,3},{2,0},{3,1},{4,6},{5,7},{6,4},{7,5},{8,10},{9,11},{10,... | collective-permute-start | bytes 589832 | tf_op jit(solution)/shard_map/ppermute | solution.py:107
  83.9 14.4 %collective-permute-start.21 = (bf16[128,768]{1,0:T(8,128)(2,1)}, bf16[128,768]{1,0:T(8,128)(2,1)S(1)}, u32[]{:S(2)}, u32[]{:S(2)}) collective-permute-start(bf16[128,768]{1,0:T(8,128)(2,1)} %get-tuple-element.201), channel_id=1, source_target_pairs={{0,3},{1,2},{2,1},{3,0},{4,7},{5,6},{6,5},{7,4},{8,11},{9,10},{10,... | collective-permute-start | bytes 589832 | tf_op jit(solution)/shard_map/ppermute | solution.py:107
  116.0 24.3 %all-to-all-start.1 = ((bf16[4,128,768]{2,1,0:T(8,128)(2,1)}), bf16[4,128,768]{2,1,0:T(8,128)(2,1)S(1)}, u32[]{:S(2)}, u32[]{:S(2)}) async-start(bf16[4,128,768]{2,1,0:T(8,128)(2,1)} %bitcast.50), calls=%async_computation.1 | async-start | bytes 1572864 | tf_op jit(solution)/shard_map/all_to_all | solution.py:1009
  140.4 13.4 %collective-permute-start.26 = (bf16[4,384,768]{2,1,0:T(8,128)(2,1)}, bf16[4,384,768]{2,1,0:T(8,128)(2,1)}, u32[]{:S(2)}, u32[]{:S(2)}) collective-permute-start(bf16[4,384,768]{2,1,0:T(8,128)(2,1)} %get-tuple-element.224), channel_id=1, source_target_pairs={{0,4},{4,0},{8,12},{12,8},{16,20},{20,16},{24,28},{28,24},{1,5},{5... | collective-permute-start | bytes 7077896 | tf_op jit(solution)/shard_map/ppermute | solution.py:107
  146.4 12.2 %collective-permute-start.27 = (bf16[4,4,24,896]{3,2,1,0:T(8,128)(2,1)}, bf16[4,4,24,896]{3,2,1,0:T(8,128)(2,1)}, u32[]{:S(2)}, u32[]{:S(2)}) collective-permute-start(bf16[4,4,24,896]{3,2,1,0:T(8,128)(2,1)} %get-tuple-element.228), channel_id=1, source_target_pairs={{0,4},{4,0},{8,12},{12,8},{16,20},{20,16},{24,28},{28,24},{1,5},{5... | collective-permute-start | bytes 2064392 | tf_op jit(solution)/shard_map/ppermute | solution.py:107
  146.5 12.2 %collective-permute-start.22 = (bf16[256,192]{1,0:T(8,128)(2,1)}, bf16[256,192]{1,0:T(8,128)(2,1)S(1)}, u32[]{:S(2)}, u32[]{:S(2)}) collective-permute-start(bf16[256,192]{1,0:T(8,128)(2,1)} %get-tuple-element.218), channel_id=1, source_target_pairs={{0,8},{4,12},{8,0},{12,4},{16,24},{20,28},{24,16},{28,20},{1,9},{5... | collective-permute-start | bytes 294920 | tf_op jit(solution)/shard_map/ppermute | solution.py:107
  148.7 9.9 %collective-permute-start.23 = (bf16[256,192]{1,0:T(8,128)(2,1)}, bf16[256,192]{1,0:T(8,128)(2,1)S(1)}, u32[]{:S(2)}, u32[]{:S(2)}) collective-permute-start(bf16[256,192]{1,0:T(8,128)(2,1)} %get-tuple-element.219), channel_id=1, source_target_pairs={{0,16},{4,20},{8,24},{12,28},{16,0},{20,4},{24,8},{28,12},{1,17},{... | collective-permute-start | bytes 294920 | tf_op jit(solution)/shard_map/ppermute | solution.py:107
  148.9 9.8 %collective-permute-start.24 = (bf16[256,192]{1,0:T(8,128)(2,1)}, bf16[256,192]{1,0:T(8,128)(2,1)S(1)}, u32[]{:S(2)}, u32[]{:S(2)}) collective-permute-start(bf16[256,192]{1,0:T(8,128)(2,1)} %get-tuple-element.220), channel_id=1, source_target_pairs={{0,24},{4,28},{8,16},{12,20},{16,8},{20,12},{24,0},{28,4},{1,25},{... | collective-permute-start | bytes 294920 | tf_op jit(solution)/shard_map/ppermute | solution.py:107
  150.3 34.1 %all-to-all-start.2 = ((bf16[4,128,768]{2,1,0:T(8,128)(2,1)}), bf16[4,128,768]{2,1,0:T(8,128)(2,1)S(1)}, u32[]{:S(2)}, u32[]{:S(2)}) async-start(bf16[4,128,768]{2,1,0:T(8,128)(2,1)} %bitcast.49), calls=%async_computation.2 | async-start | bytes 1572864 | tf_op jit(solution)/shard_map/all_to_all | solution.py:1009
  158.7 28.0 %collective-permute-start.28 = (bf16[2,768,384]{2,1,0:T(8,128)(2,1)}, bf16[2,768,384]{2,1,0:T(8,128)(2,1)S(1)}, u32[]{:S(2)}, u32[]{:S(2)}) collective-permute-start(bf16[2,768,384]{2,1,0:T(8,128)(2,1)} %get-tuple-element.238), channel_id=1, source_target_pairs={{0,8},{4,12},{8,0},{12,4},{16,24},{20,28},{24,16},{28,20},{1,9},{5... | collective-permute-start | bytes 3538952 | tf_op jit(solution)/shard_map/ppermute | solution.py:107
  160.7 27.4 %collective-permute-start.29 = (bf16[2,768,384]{2,1,0:T(8,128)(2,1)}, bf16[2,768,384]{2,1,0:T(8,128)(2,1)S(1)}, u32[]{:S(2)}, u32[]{:S(2)}) collective-permute-start(bf16[2,768,384]{2,1,0:T(8,128)(2,1)} %get-tuple-element.239), channel_id=1, source_target_pairs={{0,16},{4,20},{8,24},{12,28},{16,0},{20,4},{24,8},{28,12},{1,17},{... | collective-permute-start | bytes 3538952 | tf_op jit(solution)/shard_map/ppermute | solution.py:107
  188.1 10.2 %collective-permute-start.30 = (bf16[1024,512]{1,0:T(8,128)(2,1)}, bf16[1024,512]{1,0:T(8,128)(2,1)}, u32[]{:S(2)}, u32[]{:S(2)}) collective-permute-start(bf16[1024,512]{1,0:T(8,128)(2,1)} %get-tuple-element.243), channel_id=1, source_target_pairs={{0,4},{4,0},{8,12},{12,8},{16,20},{20,16},{24,28},{28,24},{1,5},{5... | collective-permute-start | bytes 3145736 | tf_op jit(solution)/shard_map/ppermute | solution.py:107
  188.1 23.5 %all-to-all-start.3 = ((bf16[4,4,24,896]{3,2,1,0:T(8,128)(2,1)}), bf16[4,4,24,896]{3,2,1,0:T(8,128)(2,1)}, u32[]{:S(2)}, u32[]{:S(2)}) async-start(bf16[4,4,24,896]{3,2,1,0:T(8,128)(2,1)} %half_out.1), calls=%async_computation.3 | async-start | bytes 1376256 | tf_op jit(solution)/shard_map/all_to_all | solution.py:1183
  196.1 18.7 %collective-permute-start.32 = (bf16[768,384]{1,0:T(8,128)(2,1)}, bf16[768,384]{1,0:T(8,128)(2,1)S(1)}, u32[]{:S(2)}, u32[]{:S(2)}) collective-permute-start(bf16[768,384]{1,0:T(8,128)(2,1)} %get-tuple-element.256), channel_id=1, source_target_pairs={{0,16},{4,20},{8,24},{12,28},{16,0},{20,4},{24,8},{28,12},{1,17},{... | collective-permute-start | bytes 1769480 | tf_op jit(solution)/shard_map/ppermute | solution.py:107
  196.6 18.2 %collective-permute-start.33 = (bf16[768,384]{1,0:T(8,128)(2,1)}, bf16[768,384]{1,0:T(8,128)(2,1)S(1)}, u32[]{:S(2)}, u32[]{:S(2)}) collective-permute-start(bf16[768,384]{1,0:T(8,128)(2,1)} %get-tuple-element.257), channel_id=1, source_target_pairs={{0,8},{4,12},{8,0},{12,4},{16,24},{20,28},{24,16},{28,20},{1,9},{5... | collective-permute-start | bytes 1769480 | tf_op jit(solution)/shard_map/ppermute | solution.py:107
  204.1 10.7 %collective-permute-start.31 = (bf16[4,4,24,576]{3,2,1,0:T(8,128)(2,1)}, bf16[4,4,24,576]{3,2,1,0:T(8,128)(2,1)S(1)}, u32[]{:S(2)}, u32[]{:S(2)}) collective-permute-start(bf16[4,4,24,576]{3,2,1,0:T(8,128)(2,1)} %get-tuple-element.245), channel_id=1, source_target_pairs={{0,4},{4,0},{8,12},{12,8},{16,20},{20,16},{24,28},{28,24},{1,5},{5... | collective-permute-start | bytes 1327112 | tf_op jit(solution)/shard_map/ppermute | solution.py:107
  211.6 25.3 %all-to-all-start.4 = ((f32[32,24,128]{2,1,0:T(8,128)}), f32[32,24,128]{2,1,0:T(8,128)S(1)}, u32[]{:S(2)}, u32[]{:S(2)}) async-start(f32[32,24,128]{2,1,0:T(8,128)} %get-tuple-element.282), calls=%async_computation.4 | async-start | bytes 786432 | tf_op jit(solution)/shard_map/all_to_all | solution.py:1265
  214.8 25.5 %collective-permute-start.37 = (bf16[256,768]{1,0:T(8,128)(2,1)}, bf16[256,768]{1,0:T(8,128)(2,1)S(1)}, u32[]{:S(2)}, u32[]{:S(2)}) collective-permute-start(bf16[256,768]{1,0:T(8,128)(2,1)} %get-tuple-element.274), channel_id=1, source_target_pairs={{0,8},{4,12},{8,0},{12,4},{16,24},{20,28},{24,16},{28,20},{1,9},{5... | collective-permute-start | bytes 1179656 | tf_op jit(solution)/shard_map/ppermute | solution.py:107
  216.4 23.9 %collective-permute-start.38 = (bf16[256,768]{1,0:T(8,128)(2,1)}, bf16[256,768]{1,0:T(8,128)(2,1)S(1)}, u32[]{:S(2)}, u32[]{:S(2)}) collective-permute-start(bf16[256,768]{1,0:T(8,128)(2,1)} %get-tuple-element.275), channel_id=1, source_target_pairs={{0,16},{4,20},{8,24},{12,28},{16,0},{20,4},{24,8},{28,12},{1,17},{... | collective-permute-start | bytes 1179656 | tf_op jit(solution)/shard_map/ppermute | solution.py:107
  217.9 22.4 %collective-permute-start.39 = (bf16[256,768]{1,0:T(8,128)(2,1)}, bf16[256,768]{1,0:T(8,128)(2,1)S(1)}, u32[]{:S(2)}, u32[]{:S(2)}) collective-permute-start(bf16[256,768]{1,0:T(8,128)(2,1)} %get-tuple-element.276), channel_id=1, source_target_pairs={{0,24},{4,28},{8,16},{12,20},{16,8},{20,12},{24,0},{28,4},{1,25},{... | collective-permute-start | bytes 1179656 | tf_op jit(solution)/shard_map/ppermute | solution.py:107
  228.9 10.5 %collective-permute-start.35 = (bf16[4,24,576]{2,1,0:T(8,128)(2,1)S(1)}, bf16[4,24,576]{2,1,0:T(8,128)(2,1)S(1)}, u32[]{:S(2)}, u32[]{:S(2)}) collective-permute-start(bf16[4,24,576]{2,1,0:T(8,128)(2,1)S(1)} %copy-done.39), channel_id=1, source_target_pairs={{0,2},{1,3},{2,0},{3,1},{4,6},{5,7},{6,4},{7,5},{8,10},{9,11},{10,... | collective-permute-start | bytes 331784 | tf_op jit(solution)/shard_map/ppermute | solution.py:107
  (57 other events, 322.2 us)
